TPU v7x, 32 devices: a whole 2x2x4 slice. The times are simulated.
32 devices in a mesh: member: 4 (over y, x), slab: 8 (over z, core).
Axes of the slice: x: 2, y: 2, z: 4, core: 2. Of those that a mesh axis runs over, the one named last changes fastest.
Arguments:
- fluid_head_start: float32 [192, 128, 128], P('member', 'slab'), may hold values from -6 to 6
- conductivity_matrix: float32 [192, 128, 128], P('member', 'slab'), may hold values from 0.1 to 1
- well_rates: float32 [128, 128], P('slab'), may hold values from -3 to 3
- cell_layer: int32 [128, 128], P('slab'), may hold values from 0 to 7
- pixel_coords: int32 [2, 4096], replicated, may hold values from 0 to 63
- obs_index: int32 [1024], replicated, may hold values from 0 to 4095
- obs_value: float32 [1024], replicated, may hold values from -0.6 to 0.6
- obs_sigma: float32 [1024], replicated, may hold values from 0.05 to 0.5
Outputs:
- analysed: float32 [192, 128, 128], P('member', 'slab')
- subsidence: float32 [4096, 192], P(('member', 'slab'))
All inputs are finite; a program needn't handle non-finite values.
Results may differ from a plain program's by a relative error of at most 0.00028.
Values sent between devices are 32-bit elements; how exact they have to be, the bound alone decides.
No kernel may reach another device: no remote copies, remote signals or barrier semaphores. Data moves between devices by JAX's collectives and lax.ppermute only.
A program may use at most 64 MiB of HBM per device.

v0:
```python
import math

import jax
import jax.numpy as jnp
from jax import lax
from jax.sharding import PartitionSpec as P

STEPS = 4


time_step = 0.15
pixel_span = 64.0
top_depth = 2.0


def padded(value, sides, width):
    for axis, dim in sides:
        size, length = (lax.axis_size(axis), value.shape[dim])
        up = [(i, (i + 1) % size) for i in range(size - 1)]
        down = [(j, i) for i, j in up]
        last = lax.slice_in_dim(value, length - width, length, axis=dim)
        initial = lax.slice_in_dim(value, 0, width, axis=dim)
        before = lax.ppermute(last, axis, up)
        after = lax.ppermute(initial, axis, down)
        value = jnp.concatenate([before, value, after], axis=dim)
    return value


def advance_in_time(fluid_head_grid, perm_field, source, open_faces):
    mobility = perm_field * (1.0 + 0.5 * jnp.tanh(fluid_head_grid))
    sample_vectors, height, across_cells = fluid_head_grid.shape
    across = 0.5 * (mobility[:, 1:] + mobility[:, :-1]) * open_faces[None, :, None]
    flux_rows = across * (fluid_head_grid[:, 1:] - fluid_head_grid[:, :-1])
    zero_row = jnp.zeros((sample_vectors, 1, across_cells), fluid_head_grid.dtype)
    inflow = jnp.concatenate([flux_rows, zero_row], 1) - jnp.concatenate([zero_row, flux_rows], 1)
    along = 0.5 * (mobility[:, :, 1:] + mobility[:, :, :-1])
    flux_cols = along * (fluid_head_grid[:, :, 1:] - fluid_head_grid[:, :, :-1])
    zero_col = jnp.zeros((sample_vectors, height, 1), fluid_head_grid.dtype)
    inflow = inflow + (
        jnp.concatenate([flux_cols, zero_col], 2) - jnp.concatenate([zero_col, flux_cols], 2)
    )
    return fluid_head_grid + time_step * (inflow + source[None])


def kernel_rows(pixel_x, pixel_y, cell_x, cell_y, depth, volume):
    delta_x = cell_x[None, :] - pixel_x[:, None]
    delta_y = cell_y[None, :] - pixel_y[:, None]
    radius = delta_x * delta_x + delta_y * delta_y + depth[None, :] * depth[None, :]
    return volume * depth[None, :] / (radius * jnp.sqrt(radius))


def gram_terms(predicted, obs_value, obs_sigma, owned):
    centre = jnp.mean(predicted, axis=1)
    anomaly = predicted - centre[:, None]
    inverse_var = 1.0 / (obs_sigma * obs_sigma)
    weighted = anomaly * inverse_var[:, None]
    gram = lax.dot_general(
        anomaly, weighted, (((0,), (0,)), ((), ())), precision=lax.Precision.HIGHEST
    )
    rhs = jnp.dot(owned * (obs_value - centre), weighted, precision=lax.Precision.HIGHEST)
    return (gram, rhs)


def finish(gram, rhs, sample_vector_pile):
    sample_vectors = sample_vector_pile.shape[0]
    ident = jnp.eye(sample_vectors, dtype=gram.dtype)
    gram = gram + (sample_vectors - 1.0) * ident
    factor = jnp.linalg.cholesky(gram)
    inverse = jax.scipy.linalg.solve_triangular(factor, ident, lower=True)
    weights = jnp.dot(
        inverse.T,
        jnp.dot(inverse, rhs, precision=lax.Precision.HIGHEST),
        precision=lax.Precision.HIGHEST,
    )
    transform = jnp.sqrt(sample_vectors - 1.0) * inverse.T
    mix = weights[:, None] + transform
    centre = jnp.mean(sample_vector_pile, axis=0)
    spread = sample_vector_pile - centre[None]
    return centre[None] + lax.dot_general(
        mix, spread, (((0,), (0,)), ((), ())), precision=lax.Precision.HIGHEST
    )


def face_mask(first_global, height, total_rows):
    index = first_global + jnp.arange(height - 1, dtype=jnp.int32)
    return ((index >= 0) & (index + 1 <= total_rows - 1)).astype(jnp.float32)


def shards(
    fluid_head_start,
    conductivity_matrix,
    well_rates,
    cell_layer,
    pixel_coords,
    obs_index,
    obs_value,
    obs_sigma,
):
    local_members, slab_rows, across_cells = fluid_head_start.shape
    member_count = lax.axis_size("member")
    slab_count = lax.axis_size("slab")
    slab_index = lax.axis_index("slab")
    member_index = lax.axis_index("member")
    total_rows = slab_rows * slab_count
    rim_width = STEPS
    static = jnp.concatenate([conductivity_matrix, well_rates[None]], 0)
    static_ext = padded(static, (("slab", 1),), rim_width)
    permeability_extended = static_ext[:-1]
    source_extended = static_ext[-1]
    fluid_head_grid = padded(fluid_head_start, (("slab", 1),), STEPS)
    open_faces = face_mask(slab_index * slab_rows - STEPS, slab_rows + 2 * STEPS, total_rows)
    for repeat in range(STEPS):
        fluid_head_grid = advance_in_time(
            fluid_head_grid, permeability_extended, source_extended, open_faces
        )
    predicted_ensemble = fluid_head_grid[:, STEPS : STEPS + slab_rows]
    collected_states = lax.all_to_all(
        predicted_ensemble, "member", split_axis=1, concat_axis=0, tiled=True
    )
    sample_vectors = collected_states.shape[0]
    sub_rows = collected_states.shape[1]
    sample_vector_pile = collected_states.reshape(sample_vectors, sub_rows * across_cells)
    row_global = (
        slab_index * slab_rows + member_index * sub_rows + jnp.arange(sub_rows, dtype=jnp.int32)
    )
    row_pos = (row_global.astype(jnp.float32) + 0.5) * (pixel_span / total_rows)
    col_pos = (jnp.arange(across_cells).astype(jnp.float32) + 0.5) * (pixel_span / across_cells)
    cell_x = jnp.broadcast_to(row_pos[:, None], (sub_rows, across_cells)).reshape(-1)
    cell_y = jnp.broadcast_to(col_pos[None, :], (sub_rows, across_cells)).reshape(-1)
    layers = lax.dynamic_slice_in_dim(cell_layer, member_index * sub_rows, sub_rows, 0).astype(
        jnp.float32
    )
    depth = (top_depth + layers).reshape(-1)
    volume = pixel_span * pixel_span / (total_rows * across_cells)
    pixel_f = pixel_coords.astype(jnp.float32)
    pixel_total = pixel_coords.shape[1]
    own_rows = pixel_total // (member_count * slab_count)
    own_first = lax.axis_index(("member", "slab")) * own_rows
    block = math.gcd(pixel_total, 512)

    def pixel_block(offset):
        coords = lax.dynamic_slice_in_dim(pixel_f, offset, block, 1)
        kern = kernel_rows(coords[0], coords[1], cell_x, cell_y, depth, volume)
        return lax.dot_general(
            kern, sample_vector_pile, (((1,), (1,)), ((), ())), precision=lax.Precision.HIGHEST
        )

    offsets = 0 + block * jnp.arange(pixel_total // block, dtype=jnp.int32)
    whole = lax.psum(
        lax.map(pixel_block, offsets).reshape(pixel_total, sample_vectors), ("member", "slab")
    )
    own_part = lax.dynamic_slice_in_dim(whole, own_first, own_rows, 0)
    predicted = jnp.take(whole, obs_index, axis=0)
    gram, rhs = gram_terms(predicted, obs_value, obs_sigma, jnp.ones_like(obs_value))
    analysed = finish(gram, rhs, sample_vector_pile).reshape(sample_vectors, sub_rows, across_cells)
    returned = lax.all_to_all(analysed, "member", split_axis=0, concat_axis=1, tiled=True)
    return (returned, own_part)


def solution(mesh):
    return jax.shard_map(
        shards,
        mesh=mesh,
        in_specs=(
            P("member", "slab", None),
            P("member", "slab", None),
            P("slab", None),
            P("slab", None),
            P(),
            P(),
            P(),
            P(),
        ),
        out_specs=(P("member", "slab", None), P(("member", "slab"), None)),
        check_vma=False,
    )
```

profile of v0, /device:TPU:0, one launch (start us, length us, event | category | flops | bytes accessed | tf_op | source)
XLA Modules:
  0.0 308.3 jit_solution(1163523892559287635)
XLA Ops:
  7.2 1.1 copy.19
  8.3 0.7 pad_maximum_fusion.7
  9.0 1.3 collective-permute-start.3
  10.3 3.0 collective-permute-start.2
  13.4 1.1 fusion.84
  14.5 4.6 %collective-permute-start = (f32[48,4,128]{2,0,1:T(8,128)S(1)}, f32[48,4,128]{2,0,1:T(8,128)S(1)}, u32[]{:S(2)}, u32[]{:S(2)}) collective-permute-start(f32[48,4,128]{2,0,1:T(8,128)S(1)} %copy.34), channel_id=1, source_target_pairs={{0,1},{1,2},{2,3},{3,4},{4,5},{5,6},{6,7},{8,9},{9,10},{10,11},{11... | collective-permute-start | bytes 294920 | tf_op jit(solution)/shard_map/ppermute | solution.py:23
  19.1 1.3 collective-permute-start.1
  20.4 0.8 convert_element_type.28
  21.2 1.1 constant_dynamic-update-slice_fusion.1
  25.7 0.9 slice_add_fusion.8
  26.6 3.7 %all-to-all-start = ((f32[48,16,128]{2,0,1:T(8,128)}), f32[48,16,128]{2,0,1:T(8,128)S(1)}, u32[]{:S(2)}, u32[]{:S(2)}) async-start(f32[48,16,128]{2,0,1:T(8,128)} %slice_add_fusion.8), calls=%async_computation | async-start | bytes 786432 | tf_op jit(solution)/shard_map/all_to_all | solution.py:117
  30.4 0.7 fusion.83
  31.1 5.4 %all-to-all-done = f32[48,16,128]{2,0,1:T(8,128)S(1)} async-done(((f32[48,16,128]{2,0,1:T(8,128)}), f32[48,16,128]{2,0,1:T(8,128)S(1)}, u32[]{:S(2)}, u32[]{:S(2)}) %all-to-all-start) | async-done | bytes 393248 | tf_op jit(solution)/shard_map/all_to_all | solution.py:117
  36.6 42.0 %while.14 = (s32[]{:T(128)}, f32[8,512,192]{1,2,0:T(8,128)}, f32[4,128]{1,0:T(4,128)S(1)}, s32[8]{0:T(128)S(1)}, f32[2,4096]{1,0:T(2,128)S(1)}, /*index=5*/f32[1...) while((s32[]{:T(128)}, f32[8,512,192]{1,2,0:T(8,128)}, ...), condition=%wide.region_2.3_spmd.clone, body=%wide.region_1.2_spmd.clone.sunk | while | flops 606077440 | bytes 815835 | solution.py:150
  36.6 0.6 dynamic_slice.23
  39.3 2.5 fusion.98
  41.9 0.6 dynamic_slice.23
  44.5 2.6 fusion.98
  47.1 0.6 dynamic_slice.23
  49.8 2.6 fusion.98
  52.3 0.6 dynamic_slice.23
  55.0 2.6 fusion.98
  57.6 0.6 dynamic_slice.23
  60.3 2.6 fusion.98
  62.9 0.6 dynamic_slice.23
  65.5 2.6 fusion.98
  68.1 0.6 dynamic_slice.23
  70.8 2.6 fusion.98
  76.0 2.6 fusion.98
  78.6 4.9 %copy.21 = f32[8,512,192]{2,1,0:T(8,128)} copy(f32[8,512,192]{1,2,0:T(8,128)} %get-tuple-element.81) | data formatting | bytes 6291456 | tf_op jit(solution)/shard_map/while | solution.py:150
  83.6 0.6 copy-done.1
  84.5 143.6 %all-reduce.21.cloned.1.call-done = f32[4096,192]{1,0:T(8,128)} async-done(((f32[4096,192]{1,0:T(8,128)}), f32[4096,192]{1,0:T(8,128)}) %all-reduce.21.cloned.1.call-update) | async-done | bytes 3145744 | tf_op jit(solution)/shard_map/psum | solution.py:149
  228.0 5.8 %gather_fusion = f32[1024,192]{1,0:T(8,128)S(1)} fusion(f32[4096,192]{1,0:T(8,128)} %all-reduce.21.cloned.1.call-done, s32[1024]{0:T(1024)S(1)} %fusion.75), kind=kCustom, calls=%fused_computation | custom fusion | bytes 1576960 | tf_op jit(solution)/shard_map/jit(_take)/gather | solution.py:153
  234.3 2.5 fusion.21
  237.0 11.7 %cholesky.50 = f32[128,128]{1,0:T(8,128)S(1)} custom-call(f32[128,128]{1,0:T(8,128)S(1)} %cholesky.121), custom_call_target="Cholesky" | custom-call | tf_op jit(solution)/shard_map/jit(cholesky)/cholesky | solution.py:68
  248.7 9.8 %custom-call.15 = f32[1,128,128]{1,2,0:T(8,128)S(1)} custom-call(f32[1,128,128]{2,1,0:T(8,128)S(1)} %get-tuple-element.164), custom_call_target="InvertDiagBlocksLowerTriangular" | custom-call | tf_op jit(solution)/shard_map/jit(cholesky)/cholesky | solution.py:68
  258.9 5.8 %cholesky.108 = f32[64,64]{1,0:T(8,128)S(1)} custom-call(f32[64,64]{1,0:T(8,128)S(1)} %convolution_subtract_fusion.1), custom_call_target="Cholesky" | custom-call | tf_op jit(solution)/shard_map/jit(cholesky)/cholesky | solution.py:68
  264.8 0.6 compare_reduce_fusion.1
  265.5 0.6 compare_reduce_fusion
  267.5 19.9 %custom-call.16 = f32[2,128,128]{1,2,0:T(8,128)S(1)} custom-call(f32[2,128,128]{2,1,0:T(8,128)S(1)} %pad_maximum_fusion.2), custom_call_target="InvertDiagBlocksLowerTriangular" | custom-call | tf_op jit(solution)/shard_map/jit(_solve_triangular)/triangular_solve | solution.py:69
  288.4 0.9 fusion.23
  289.7 0.8 convolution_add_fusion
  290.5 0.9 reshape.109
  291.4 3.5 %all-to-all-start.1 = ((f32[192,4,128]{2,1,0:T(4,128)}), f32[192,4,128]{2,1,0:T(4,128)S(1)}, u32[]{:S(2)}, u32[]{:S(2)}) async-start(f32[192,4,128]{2,1,0:T(4,128)} %reshape.109), calls=%async_computation.1 | async-start | bytes 786432 | tf_op jit(solution)/shard_map/all_to_all | solution.py:156
  294.8 0.9 constant_dynamic-slice_fusion.1
  295.8 0.7 copy.25
  296.5 4.2 %all-to-all-done.1 = f32[192,4,128]{2,1,0:T(4,128)S(1)} async-done(((f32[192,4,128]{2,1,0:T(4,128)}), f32[192,4,128]{2,1,0:T(4,128)S(1)}, u32[]{:S(2)}, u32[]{:S(2)}) %all-to-all-start.1) | async-done | bytes 393248 | tf_op jit(solution)/shard_map/all_to_all | solution.py:156
  300.7 0.8 copy.24
  (91 shorter events, 8.1 us)
Async XLA Ops:
  7.2 15.2 %copy-start = (f32[16,128]{1,0:T(8,128)S(1)}, f32[16,128]{1,0:T(8,128)}, u32[]{:S(2)}) copy-start(f32[16,128]{1,0:T(8,128)} %param.12) | copy-start | bytes 24580
  9.0 13.3 %collective-permute-start.3 = (f32[49,4,128]{2,0,1:T(8,128)S(1)}, f32[49,4,128]{2,0,1:T(8,128)S(1)}, u32[]{:S(2)}, u32[]{:S(2)}) collective-permute-start(f32[49,4,128]{2,0,1:T(8,128)S(1)} %get-tuple-element.160), channel_id=1, source_target_pairs={{1,0},{2,1},{3,2},{4,3},{5,4},{6,5},{7,6},{9,8},{10,9},{11,10},{12... | collective-permute-start | bytes 301064 | tf_op jit(solution)/shard_map/ppermute | solution.py:24
  10.3 12.0 %collective-permute-start.2 = (f32[49,4,128]{2,0,1:T(8,128)S(1)}, f32[49,4,128]{2,0,1:T(8,128)S(1)}, u32[]{:S(2)}, u32[]{:S(2)}) collective-permute-start(f32[49,4,128]{2,0,1:T(8,128)S(1)} %get-tuple-element.159), channel_id=1, source_target_pairs={{0,1},{1,2},{2,3},{3,4},{4,5},{5,6},{6,7},{8,9},{9,10},{10,11},{11... | collective-permute-start | bytes 301064 | tf_op jit(solution)/shard_map/ppermute | solution.py:23
  14.5 6.7 %collective-permute-start = (f32[48,4,128]{2,0,1:T(8,128)S(1)}, f32[48,4,128]{2,0,1:T(8,128)S(1)}, u32[]{:S(2)}, u32[]{:S(2)}) collective-permute-start(f32[48,4,128]{2,0,1:T(8,128)S(1)} %copy.34), channel_id=1, source_target_pairs={{0,1},{1,2},{2,3},{3,4},{4,5},{5,6},{6,7},{8,9},{9,10},{10,11},{11... | collective-permute-start | bytes 294920 | tf_op jit(solution)/shard_map/ppermute | solution.py:23
  19.1 3.3 %collective-permute-start.1 = (f32[48,4,128]{2,0,1:T(8,128)S(1)}, f32[48,4,128]{2,0,1:T(8,128)S(1)}, u32[]{:S(2)}, u32[]{:S(2)}) collective-permute-start(f32[48,4,128]{2,0,1:T(8,128)S(1)} %copy.35), channel_id=1, source_target_pairs={{1,0},{2,1},{3,2},{4,3},{5,4},{6,5},{7,6},{9,8},{10,9},{11,10},{12... | collective-permute-start | bytes 294920 | tf_op jit(solution)/shard_map/ppermute | solution.py:24
  26.6 9.8 %all-to-all-start = ((f32[48,16,128]{2,0,1:T(8,128)}), f32[48,16,128]{2,0,1:T(8,128)S(1)}, u32[]{:S(2)}, u32[]{:S(2)}) async-start(f32[48,16,128]{2,0,1:T(8,128)} %slice_add_fusion.8), calls=%async_computation | async-start | bytes 786432 | tf_op jit(solution)/shard_map/all_to_all | solution.py:117
  30.3 197.7 %all-reduce.21.cloned.1.call-start = ((), (), s32[]{:S(2)}) async-start(), calls=%async_computation.2 | async-start | bytes 8388608 | tf_op jit(solution)/shard_map/psum | solution.py:149
  83.5 0.7 copy-start.1
  83.5 0.7 copy-start.2
  84.4 149.8 %copy-start.3 = (f32[1024]{0:T(1024)S(1)}, f32[1024]{0:T(1024)}, u32[]{:S(2)}) copy-start(f32[1024]{0:T(1024)} %param.16) | copy-start | bytes 12292
  291.4 9.3 %all-to-all-start.1 = ((f32[192,4,128]{2,1,0:T(4,128)}), f32[192,4,128]{2,1,0:T(4,128)S(1)}, u32[]{:S(2)}, u32[]{:S(2)}) async-start(f32[192,4,128]{2,1,0:T(4,128)} %reshape.109), calls=%async_computation.1 | async-start | bytes 786432 | tf_op jit(solution)/shard_map/all_to_all | solution.py:156
Sparse Core Ops, SparseCore 0:
  83.6 144.3 all-reduce.20
where the time goes:
time: 309 us; the launch traced here: 308 us
  waiting for transfers between devices  153 us (50%)
  other arithmetic  55.8 us (18%)
  matrix products  26.4 us (9%)
  local copies, waits for them, and re-layouts  24.2 us (8%)
  starting transfers between devices  17.4 us (6%)
  between operations  15.8 us (5%)
  loops' own time  15.6 us (5%)
    psum x1, waiting for transfers between devices, shards(): lax.psum(lax.map(pixel_block, offsets).reshape(pixel_total, sample_vector...  144 us
    another operation x7, other arithmetic, finish(): factor = jnp.linalg.cholesky(gram)  28.7 us
    dot_general x8, matrix products, pixel_block(): lax.dot_general(kern, sample_vector_pile, (((1,), (1,)), ((), ())), preci...  20.5 us
    another operation x6, other arithmetic, finish(): inverse = jax.scipy.linalg.solve_triangular(factor, ident, lower=True)  20 us
    another operation x1, loops' own time, shards(): lax.map(pixel_block, offsets).reshape(pixel_total, sample_vectors)  15.6 us
    ppermute x2, starting transfers between devices, padded(): before = lax.ppermute(last, axis, up)  7.61 us
  transfers between devices with their start and end apart: 7, of which 3 were waited for; matrix products, arithmetic and copies ran while one was open for 2% of the time, Pallas kernels for 0%

commit v1 on v0

v1 whole, which is shorter than its diff:
```python
import functools
import math

import jax
import jax.numpy as jnp
from jax import lax
from jax.experimental import pallas as pl
from jax.experimental.pallas import tpu as pltpu
from jax.sharding import PartitionSpec as P

STEPS = 4

time_step = 0.15
pixel_span = 64.0
top_depth = 2.0

F32 = jnp.float32
BF16 = jnp.bfloat16
VMEM_BYTES = 56 * 1024 * 1024


def params(**more):
    return pltpu.CompilerParams(vmem_limit_bytes=VMEM_BYTES, **more)


def cost(flops, bytes_accessed):
    return pl.CostEstimate(flops=int(flops), bytes_accessed=int(bytes_accessed), transcendentals=0)


def split(value):
    high = value.astype(BF16)
    return high, (value - high.astype(F32)).astype(BF16)


def dot(a, b):
    return lax.dot_general(a, b, (((1,), (0,)), ((), ())), preferred_element_type=F32)


def accumulate(step, total_ref, part):
    @pl.when(step == 0)
    def _():
        total_ref[...] = part

    @pl.when(step > 0)
    def _():
        total_ref[...] = total_ref[...] + part


def pack_kernel(slab_ref, head_ref, perm_ref, wells_ref, near_ref, far_ref):
    members, rows, cells = head_ref.shape
    even = lax.rem(slab_ref[0], 2) == 0
    for k in range(STEPS):
        for source, first in ((head_ref, 0), (perm_ref, members)):
            top = source[:, k, :]
            bottom = source[:, rows - STEPS + k, :]
            near_ref[k, first : first + members, :] = jnp.where(even, bottom, top)
            far_ref[k, first : first + members, :] = jnp.where(even, top, bottom)
        top = jnp.broadcast_to(wells_ref[k : k + 1, :], (8, cells))
        bottom = jnp.broadcast_to(wells_ref[rows - STEPS + k : rows - STEPS + k + 1, :], (8, cells))
        near_ref[k, 2 * members :, :] = jnp.where(even, bottom, top)
        far_ref[k, 2 * members :, :] = jnp.where(even, top, bottom)


def pack(slab, head, perm, wells):
    members, _, cells = head.shape
    out = jax.ShapeDtypeStruct((STEPS, 2 * members + 8, cells), F32)
    return pl.pallas_call(
        pack_kernel,
        out_shape=(out, out),
        in_specs=[pl.BlockSpec(memory_space=pltpu.SMEM)] + [pl.BlockSpec(memory_space=pltpu.VMEM)] * 3,
        out_specs=(pl.BlockSpec(memory_space=pltpu.VMEM),) * 2,
        compiler_params=params(),
        name="pack_rims",
    )(slab, head, perm, wells)


def kernel_body(total_rows, rows_here, slab_ref, px, py, layer_ref, high_ref, low_ref, dy2_ref):
    cells = dy2_ref.shape[0]
    pixels = dy2_ref.shape[1]
    row = pl.program_id(0)

    @pl.when(row == 0)
    def _():
        position = lax.broadcasted_iota(jnp.int32, (cells, 128), 0).astype(F32)
        cell_y = (position + 0.5) * (pixel_span / cells)
        for lane in range(0, pixels, 128):
            delta = cell_y - jnp.broadcast_to(py(lane), (cells, 128))
            dy2_ref[:, lane : lane + 128] = delta * delta

    global_row = slab_ref[0] * rows_here + row
    cell_x = (global_row.astype(F32) + 0.5) * (pixel_span / total_rows)
    layer = layer_ref[pl.ds(row, 1), :].astype(F32) + top_depth
    depth = jnp.swapaxes(jnp.broadcast_to(layer, (cells, cells)), 0, 1)
    depth2 = depth * depth
    scaled = depth * (pixel_span * pixel_span / (total_rows * cells))
    for lane in range(0, pixels, 128):
        delta = cell_x - px(lane)
        dx2 = jnp.broadcast_to(delta * delta, (32, 128))
        for sub in range(0, cells, 32):
            r2 = dy2_ref[sub : sub + 32, lane : lane + 128] + dx2 + depth2[sub : sub + 32, :128]
            inverse = lax.rsqrt(r2)
            value = scaled[sub : sub + 32, :128] * inverse * (inverse * inverse)
            high, low = split(value)
            high_ref[sub : sub + 32, lane : lane + 128] = high
            low_ref[sub : sub + 32, lane : lane + 128] = low


def observed_kernel(total_rows, rows_here, slab_ref, table_ref, index_ref, layer_ref, high_ref, low_ref, dy2_ref, at_ref):
    pixels = dy2_ref.shape[1]
    tall = table_ref.shape[0] // 2

    @pl.when(pl.program_id(0) == 0)
    def _():
        for lane in range(0, pixels, 128):
            index = index_ref[0:1, lane : lane + 128]
            low = index & 127
            high = index >> 7
            pick = (lax.broadcasted_iota(jnp.int32, (128, 128), 0) == low).astype(BF16)
            found = dot(table_ref[...].astype(BF16), pick)
            own = lax.broadcasted_iota(jnp.int32, (tall, 128), 0) == high
            at_ref[0:1, lane : lane + 128] = jnp.sum(jnp.where(own, found[:tall], 0.0), 0, keepdims=True)
            at_ref[1:2, lane : lane + 128] = jnp.sum(jnp.where(own, found[tall:], 0.0), 0, keepdims=True)

    px = lambda lane: at_ref[0:1, lane : lane + 128]
    py = lambda lane: at_ref[1:2, lane : lane + 128]
    kernel_body(total_rows, rows_here, slab_ref, px, py, layer_ref, high_ref, low_ref, dy2_ref)


def pixel_kernel(total_rows, rows_here, slab_ref, at_in_ref, layer_ref, high_ref, low_ref, dy2_ref):
    px = lambda lane: at_in_ref[0:1, lane : lane + 128]
    py = lambda lane: at_in_ref[1:2, lane : lane + 128]
    kernel_body(total_rows, rows_here, slab_ref, px, py, layer_ref, high_ref, low_ref, dy2_ref)


def forward_kernel(total_rows, slab, layer, at=None, table=None, index=None):
    rows, cells = layer.shape
    whole = lambda a: pl.BlockSpec(a.shape, lambda i: (0,) * a.ndim)
    smem = pl.BlockSpec(memory_space=pltpu.SMEM)
    if at is None:
        pixels = index.shape[1]
        body = functools.partial(observed_kernel, total_rows, rows)
        operands = (slab, table, index, layer)
        scratch = [pltpu.VMEM((cells, pixels), F32), pltpu.VMEM((8, pixels), F32)]
    else:
        pixels = at.shape[1]
        body = functools.partial(pixel_kernel, total_rows, rows)
        operands = (slab, at, layer)
        scratch = [pltpu.VMEM((cells, pixels), F32)]
    out = jax.ShapeDtypeStruct((rows * cells, pixels), BF16)
    return pl.pallas_call(
        body,
        grid=(rows,),
        out_shape=(out, out),
        in_specs=[smem] + [whole(a) for a in operands[1:]],
        out_specs=(pl.BlockSpec((cells, pixels), lambda i: (i, 0)),) * 2,
        scratch_shapes=scratch,
        compiler_params=params(dimension_semantics=("arbitrary",)),
        cost_estimate=cost(rows * cells * pixels * 16, rows * cells * pixels * 4),
        name="kernel_of_observed" if at is None else "kernel_of_pixels",
    )(*operands)


def forecast_steps(rows, slab, slabs, head_ref, perm_ref, wells_ref, near_ref, far_ref, p_ref, k_ref):
    members, _, cells = head_ref.shape
    even = lax.rem(slab, 2) == 0
    reach = rows + 2 * STEPS
    for k in range(STEPS):
        near = near_ref[k]
        far = far_ref[k]
        before = jnp.where(even, far, near)
        after = jnp.where(even, near, far)
        p_ref[k] = before[:members]
        k_ref[k] = before[members : 2 * members]
        p_ref[STEPS + rows + k] = after[:members]
        k_ref[STEPS + rows + k] = after[members : 2 * members]
    for k in range(rows):
        p_ref[STEPS + k] = head_ref[:, k, :]
        k_ref[STEPS + k] = perm_ref[:, k, :]
    last_lane = lax.broadcasted_iota(jnp.int32, (members, cells), 1) == cells - 1
    no_before = slab == 0
    no_after = slab == slabs - 1

    def wells_of(i):
        if i < STEPS:
            return jnp.where(even, far_ref[i, 2 * members : 2 * members + 1, :], near_ref[i, 2 * members : 2 * members + 1, :])
        if i >= STEPS + rows:
            j = i - STEPS - rows
            return jnp.where(even, near_ref[j, 2 * members : 2 * members + 1, :], far_ref[j, 2 * members : 2 * members + 1, :])
        return wells_ref[i - STEPS : i - STEPS + 1, :]

    def row_flux(mobility, head, mobility_next, head_next, i):
        flux = 0.5 * (mobility_next + mobility) * (head_next - head)
        if i == STEPS - 1:
            flux = jnp.where(no_before, 0.0, flux)
        if i == STEPS + rows - 1:
            flux = jnp.where(no_after, 0.0, flux)
        return flux

    def mobility_of(i, head):
        return k_ref[i] * (1.0 + 0.5 * jnp.tanh(head))

    for step in range(STEPS):
        first = step + 1
        head_before = p_ref[first - 1]
        head = p_ref[first]
        mobility_before = mobility_of(first - 1, head_before)
        mobility = mobility_of(first, head)
        flux_before = row_flux(mobility_before, head_before, mobility, head, first - 1)
        for i in range(first, reach - first):
            head_next = p_ref[i + 1]
            mobility_next = mobility_of(i + 1, head_next)
            flux_after = row_flux(mobility, head, mobility_next, head_next, i)
            along = 0.5 * (pltpu.roll(mobility, cells - 1, 1) + mobility) * (pltpu.roll(head, cells - 1, 1) - head)
            along = jnp.where(last_lane, 0.0, along)
            inflow = (flux_after - flux_before) + (along - pltpu.roll(along, 1, 1))
            p_ref[i] = head + time_step * (inflow + wells_of(i))
            head, mobility, flux_before = head_next, mobility_next, flux_after


def forecast_kernel(slabs, slab_ref, head_ref, perm_ref, wells_ref, near_ref, far_ref, high_ref, low_ref, cast_ref, own_ref, other_ref, p_ref, k_ref, lhs_ref, wide_ref, thin_ref):
    members, rows, cells = head_ref.shape
    padded = cast_ref.shape[0]
    depth = high_ref.shape[0]
    step = pl.program_id(0)

    @pl.when(step == 0)
    def _():
        forecast_steps(rows, slab_ref[0], slabs, head_ref, perm_ref, wells_ref, near_ref, far_ref, p_ref, k_ref)
        per = depth // cells
        if padded != members:
            cast_ref[...] = jnp.zeros_like(cast_ref)
            lhs_ref[...] = jnp.zeros_like(lhs_ref)
        for i in range(rows):
            value = p_ref[STEPS + i]
            high, low = split(value)
            lane = (i % per) * cells
            cast_ref[0:members, i * cells : (i + 1) * cells] = value
            lhs_ref[i // per, 0:members, lane : lane + cells] = high
            lhs_ref[i // per, padded : padded + members, lane : lane + cells] = low

    both = lhs_ref[step]
    accumulate(step, wide_ref, dot(both, high_ref[...]))
    accumulate(step, thin_ref, dot(both[:padded], low_ref[...]))

    @pl.when(step == pl.num_programs(0) - 1)
    def _():
        half = own_ref.shape[1]
        seen = wide_ref[0:padded, :] + wide_ref[padded:, :] + thin_ref[...]
        own_ref[...] = seen[:, :half]
        other_ref[...] = seen[:, half:]


def forecast(slabs, padded, slab, head, perm, wells, near, far, high, low):
    members, rows, cells = head.shape
    total, observed = high.shape
    depth = min(total, 512)
    whole = lambda a: pl.BlockSpec(a.shape, lambda i: (0,) * a.ndim)
    const = lambda shape: pl.BlockSpec(shape, lambda i: (0,) * len(shape))
    half = (padded, observed // 2)
    return pl.pallas_call(
        functools.partial(forecast_kernel, slabs),
        grid=(total // depth,),
        out_shape=(
            jax.ShapeDtypeStruct((padded, total), F32),
            jax.ShapeDtypeStruct(half, F32),
            jax.ShapeDtypeStruct(half, F32),
        ),
        in_specs=[pl.BlockSpec(memory_space=pltpu.SMEM)]
        + [whole(a) for a in (head, perm, wells, near, far)]
        + [pl.BlockSpec((depth, observed), lambda i: (i, 0))] * 2,
        out_specs=(const((padded, total)), const(half), const(half)),
        scratch_shapes=[
            pltpu.VMEM((rows + 2 * STEPS, members, cells), F32),
            pltpu.VMEM((rows + 2 * STEPS, members, cells), F32),
            pltpu.VMEM((total // depth, 2 * padded, depth), BF16),
            pltpu.VMEM((2 * padded, observed), F32),
            pltpu.VMEM((padded, observed), F32),
        ],
        compiler_params=params(dimension_semantics=("arbitrary",)),
        cost_estimate=cost(6 * padded * total * observed, 4 * total * observed),
        name="forecast",
    )(slab, head, perm, wells, near, far, high, low)


def subsidence_kernel(groups, member_ref, *refs):
    pieces = refs[:groups]
    high_ref, low_ref, own_ref, other_ref, lhs_ref, wide_ref, thin_ref = refs[groups:]
    padded = pieces[0].shape[0]
    every = groups * padded
    depth = high_ref.shape[0]
    step = pl.program_id(0)

    for offset in range(groups):
        at = member_ref[0] ^ offset
        high, low = split(pieces[offset][...])
        lhs_ref[at] = high
        lhs_ref[groups + at] = low
    both = lhs_ref[...].reshape(2 * every, depth)
    accumulate(step, wide_ref, dot(both, high_ref[...]))
    accumulate(step, thin_ref, dot(both[:every], low_ref[...]))

    @pl.when(step == pl.num_programs(0) - 1)
    def _():
        half = own_ref.shape[1]
        seen = wide_ref[0:every, :] + wide_ref[every:, :] + thin_ref[...]
        own_ref[...] = seen[:, :half]
        other_ref[...] = seen[:, half:]


def subsidence_partial(member, pieces, high, low):
    groups = len(pieces)
    padded, total = pieces[0].shape
    pixels = high.shape[1]
    depth = min(total, 512)
    every = groups * padded
    half = (every, pixels // 2)
    out = jax.ShapeDtypeStruct(half, F32)
    return pl.pallas_call(
        functools.partial(subsidence_kernel, groups),
        grid=(total // depth,),
        out_shape=(out, out),
        in_specs=[pl.BlockSpec(memory_space=pltpu.SMEM)]
        + [pl.BlockSpec((padded, depth), lambda i: (0, i))] * groups
        + [pl.BlockSpec((depth, pixels), lambda i: (i, 0))] * 2,
        out_specs=(pl.BlockSpec(half, lambda i: (0, 0)),) * 2,
        scratch_shapes=[
            pltpu.VMEM((2 * groups, padded, depth), BF16),
            pltpu.VMEM((2 * every, pixels), F32),
            pltpu.VMEM((every, pixels), F32),
        ],
        compiler_params=params(dimension_semantics=("arbitrary",)),
        cost_estimate=cost(6 * every * total * pixels, 4 * total * pixels + 4 * every * total),
        name="subsidence",
    )(member, *pieces, high, low)


def gram_kernel(groups, members, member_ref, *refs):
    pieces = refs[:groups]
    value_ref, sigma_ref, out_ref, seen_ref = refs[groups:]
    padded, half = pieces[0].shape
    every = groups * padded
    for offset in range(groups):
        seen_ref[member_ref[0] ^ offset] = pieces[offset][...]
    seen = seen_ref[...].reshape(every, half)
    centre = jnp.sum(seen, 0, keepdims=True) * (1.0 / (groups * members))
    anomaly = seen - centre
    if padded != members:
        here = lax.rem(lax.broadcasted_iota(jnp.int32, (every, half), 0), padded) < members
        anomaly = jnp.where(here, anomaly, 0.0)
    sigma = sigma_ref[...]
    weighted = anomaly * (1.0 / (sigma * sigma))
    innovation = jnp.broadcast_to(value_ref[...] - centre, (8, half))
    extra = jnp.where(lax.broadcasted_iota(jnp.int32, (8, half), 0) == 0, innovation, 0.0)
    contract = (((1,), (1,)), ((), ()))
    out_ref[...] = jnp.zeros_like(out_ref)
    out_ref[:, 0:every] = lax.dot_general(
        weighted, anomaly, contract, precision=lax.Precision.HIGHEST, preferred_element_type=F32
    )
    out_ref[:, every : every + 8] = lax.dot_general(
        weighted, extra, contract, precision=lax.Precision.HIGHEST, preferred_element_type=F32
    )


def gram_partial(members, member, pieces, value, sigma):
    groups = len(pieces)
    padded, half = pieces[0].shape
    every = groups * padded
    width = -(-(every + 8) // 128) * 128
    vmem = pl.BlockSpec(memory_space=pltpu.VMEM)
    return pl.pallas_call(
        functools.partial(gram_kernel, groups, members),
        out_shape=jax.ShapeDtypeStruct((every, width), F32),
        in_specs=[pl.BlockSpec(memory_space=pltpu.SMEM)] + [vmem] * (groups + 2),
        out_specs=vmem,
        scratch_shapes=[pltpu.VMEM((groups, padded, half), F32)],
        compiler_params=params(),
        cost_estimate=cost(12 * every * every * half, 4 * every * half),
        name="gram",
    )(member, *pieces, value, sigma)


def update_kernel(groups, members, member_ref, mix_ref, *refs):
    pieces = refs[:groups]
    out_ref, cast_ref = refs[groups:]
    padded, total = pieces[0].shape
    rows, cells = out_ref.shape[1:]
    every = groups * padded
    for offset in range(groups):
        at = member_ref[0] ^ offset
        high, low = split(pieces[offset][...])
        cast_ref[at] = high
        cast_ref[groups + at] = low
    mix_high, mix_low = split(mix_ref[...])
    mix_both = jnp.concatenate([mix_high, mix_low], 0)
    depth = 4 * cells if rows % 4 == 0 else cells
    for lane in range(0, total, depth):
        high = cast_ref[0:groups, :, lane : lane + depth].reshape(every, depth)
        low = cast_ref[groups:, :, lane : lane + depth].reshape(every, depth)
        both = dot(mix_both, high)
        value = both[:padded] + both[padded:] + dot(mix_high, low)
        for part in range(depth // cells):
            out_ref[:, lane // cells + part, :] = value[:members, part * cells : (part + 1) * cells]


def update(members, rows, cells, member, mix, pieces):
    groups = len(pieces)
    padded, total = pieces[0].shape
    vmem = pl.BlockSpec(memory_space=pltpu.VMEM)
    return pl.pallas_call(
        functools.partial(update_kernel, groups, members),
        out_shape=jax.ShapeDtypeStruct((members, rows, cells), F32),
        in_specs=[pl.BlockSpec(memory_space=pltpu.SMEM)] + [vmem] * (groups + 1),
        out_specs=vmem,
        scratch_shapes=[pltpu.VMEM((2 * groups, padded, total), BF16)],
        compiler_params=params(),
        cost_estimate=cost(6 * padded * groups * padded * total, 4 * groups * padded * total),
        name="update",
    )(member, mix, *pieces)


def weights_of(members, padded, member, gram_sum):
    every = gram_sum.shape[0]
    count = every // padded * members
    ident = jnp.eye(every, dtype=F32)
    gram = gram_sum[:, :every] + (count - 1.0) * ident
    rhs = gram_sum[:, every]
    factor = jnp.linalg.cholesky(gram)
    inverse = jax.scipy.linalg.solve_triangular(factor, ident, lower=True)
    high = lax.Precision.HIGHEST
    weights = jnp.dot(inverse.T, jnp.dot(inverse, rhs, precision=high), precision=high)
    own = lax.dynamic_slice_in_dim(inverse, member * padded, padded, 0)
    mix = weights[None, :] + math.sqrt(count - 1.0) * own
    here = (jnp.arange(every) % padded < members).astype(F32)
    mix = mix * here[None, :]
    return (mix + (1.0 - jnp.sum(mix, 1, keepdims=True)) / count) * here[None, :]


def shards(head, perm, wells, layer, coords, obs_index, obs_value, obs_sigma):
    members, rows, cells = head.shape
    groups = lax.axis_size("member")
    slabs = lax.axis_size("slab")
    slab = lax.axis_index("slab")
    member = lax.axis_index("member")
    core = slab % 2
    total_rows = rows * slabs
    padded = -(-members // 16) * 16
    slab_s = slab.astype(jnp.int32).reshape(1)
    member_s = member.astype(jnp.int32).reshape(1)
    pair = [(i, i ^ 1) for i in range(slabs)]
    across = [(i, i + 1) for i in range(1, slabs - 1, 2)] + [(i + 1, i) for i in range(1, slabs - 1, 2)]

    def swap(value, axis, offset):
        size = lax.axis_size(axis)
        return lax.ppermute(value, axis, [(i, i ^ offset) for i in range(size)])

    near, far = pack(slab_s, head, perm, wells)
    far = lax.ppermute(far, "slab", across)
    near = lax.ppermute(near, "slab", pair)

    observed = obs_index.shape[0]
    half = observed // 2

    def own_first(row):
        return jnp.where(core == 0, row, jnp.roll(row, half)).reshape(1, observed)

    pixel_total = coords.shape[1]
    table = coords.astype(F32).reshape(2 * pixel_total // 128, 128)
    high, low = forward_kernel(total_rows, slab_s, layer, table=table, index=own_first(obs_index))

    cast, own, other = forecast(slabs, padded, slab_s, head, perm, wells, near, far, high, low)
    seen = own + swap(other, "slab", 1)
    pieces = [cast] + [swap(cast, "member", offset) for offset in range(1, groups)]
    offset = 2
    while offset < slabs:
        seen = seen + swap(seen, "slab", offset)
        offset *= 2
    views = [seen] + [swap(seen, "member", offset) for offset in range(1, groups)]
    value = own_first(obs_value)[:, :half]
    sigma = own_first(obs_sigma)[:, :half]
    gram = gram_partial(members, member_s, views, value, sigma)
    gram = gram + swap(gram, "slab", 1)

    chips = slabs // 2
    own_rows = pixel_total // (groups * slabs)
    at = coords.astype(F32).reshape(2, groups, chips, 2, own_rows)
    at = lax.dynamic_index_in_dim(at, member, 1, keepdims=False)
    at = jnp.swapaxes(at, 1, 2)
    at = jnp.where(core == 0, at, at[:, ::-1]).reshape(2, pixel_total // groups)
    pixel_high, pixel_low = forward_kernel(total_rows, slab_s, layer, at=at)
    sunk, sunk_other = subsidence_partial(member_s, pieces, pixel_high, pixel_low)
    sunk_recv = swap(sunk_other, "slab", 1)
    chip = slab // 2

    def block(which):
        first = which * own_rows
        return lax.dynamic_slice_in_dim(sunk, first, own_rows, 1) + lax.dynamic_slice_in_dim(
            sunk_recv, first, own_rows, 1
        )

    sunk_own = block(chip)
    for offset in range(1, chips):
        sunk_own = sunk_own + swap(block(chip ^ offset), "slab", 2 * offset)
    if padded != members:
        sunk_own = sunk_own.reshape(groups, padded, own_rows)[:, :members].reshape(groups * members, own_rows)
    subsidence = sunk_own.T

    mix = weights_of(members, padded, member, gram)
    analysed = update(members, rows, cells, member_s, mix, pieces)
    return (analysed, subsidence)


def solution(mesh):
    return jax.shard_map(
        shards,
        mesh=mesh,
        in_specs=(
            P("member", "slab", None),
            P("member", "slab", None),
            P("slab", None),
            P("slab", None),
            P(),
            P(),
            P(),
            P(),
        ),
        out_specs=(P("member", "slab", None), P(("member", "slab"), None)),
        check_vma=False,
    )
```

time: 309 us -> 148 us (0.48)
  waiting for transfers between devices: 153 us -> 12 us
  Pallas kernels: 0 us -> 47.5 us
  matrix products: 26.4 us -> 1.7 us
  local copies, waits for them, and re-layouts: 24.2 us -> 7.6 us
  loops' own time: 15.6 us -> 0 us
  between operations: 15.8 us -> 2.34 us
  starting transfers between devices: 17.4 us -> 23.3 us
    psum x1 -> x0, waiting for transfers between devices: 144 us -> none  [shards(): lax.psum(lax.map(pixel_block, offsets).reshape(pixel_total, sample_vector...]
    pallas_call x0 -> x7, Pallas kernels: none -> 47.5 us  [the longest x2 19.3 us: forward_kernel(): pl.pallas_call(body, grid=(rows,), out_shape=(out, out), in_specs=[smem]...]
    dot_general x13 -> x2, matrix products: 25.1 us -> 0.48 us  [the longest x1 0.26 us: weights_of(): jnp.dot(inverse.T, jnp.dot(inverse, rhs, precision=high), precision=high)]
    another operation x1 -> x0, loops' own time: 15.6 us -> none  [shards(): lax.map(pixel_block, offsets).reshape(pixel_total, sample_vectors)]
    ppermute x4 -> x16, starting transfers between devices: 10.2 us -> 23.3 us  [the longest x14 22.1 us: swap(): return lax.ppermute(value, axis, [(i, i ^ offset) for i in range(size)])]
    ppermute x4 -> x16, waiting for transfers between devices: 0.01 us -> 12 us  [the longest x14 12 us: swap(): return lax.ppermute(value, axis, [(i, i ^ offset) for i in range(size)])]
    all_to_all x2 -> x0, waiting for transfers between devices: 9.53 us -> none  [the longest x1 5.35 us: shards(): lax.all_to_all(predicted_ensemble, 'member', split_axis=1, concat_axis=0,...]
    all_to_all x2 -> x0, starting transfers between devices: 7.18 us -> none  [the longest x1 3.72 us: shards(): lax.all_to_all(predicted_ensemble, 'member', split_axis=1, concat_axis=0,...]
  transfers between devices with their start and end apart: 7 -> 16, of which waited for: 3 -> 4; matrix products, arithmetic and copies ran while one was open for 2% -> 40% of each run, Pallas kernels for 0% -> 22%
where the time goes in v1:
time: 148 us
  other arithmetic  53.3 us (36%)
  Pallas kernels  47.5 us (32%)
  starting transfers between devices  23.3 us (16%)
  waiting for transfers between devices  12 us (8%)
  local copies, waits for them, and re-layouts  7.6 us (5%)
  between operations  2.34 us (2%)
  matrix products  1.7 us (1%)
    another operation x7, other arithmetic, weights_of(): factor = jnp.linalg.cholesky(gram)  28.8 us
    ppermute x14, starting transfers between devices, swap(): return lax.ppermute(value, axis, [(i, i ^ offset) for i in range(size)])  22.1 us
    another operation x6, other arithmetic, weights_of(): inverse = jax.scipy.linalg.solve_triangular(factor, ident, lower=True)  19.8 us
    pallas_call x2, Pallas kernels, forward_kernel(): pl.pallas_call(body, grid=(rows,), out_shape=(out, out), in_specs=[smem]...  19.3 us
    pallas_call x1, Pallas kernels, forecast(): pl.pallas_call(functools.partial(forecast_kernel, slabs), grid=(total //...  12.3 us
    ppermute x14, waiting for transfers between devices, swap(): return lax.ppermute(value, axis, [(i, i ^ offset) for i in range(size)])  12 us
    pallas_call x1, Pallas kernels, subsidence_partial(): pl.pallas_call(functools.partial(subsidence_kernel, groups), grid=(total...  8.16 us
  transfers between devices with their start and end apart: 16, of which 4 were waited for; matrix products, arithmetic and copies ran while one was open for 40% of the time, Pallas kernels for 22%

profile of v1, /device:TPU:0, one launch (start us, length us, event | category | flops | bytes accessed | tf_op | source)
XLA Modules:
  0.0 147.8 jit_solution(2948028180209235361)
XLA Ops:
  0.6 2.2 %pack_rims.1 = (f32[4,104,128]{2,1,0:T(8,128)}, f32[4,104,128]{2,1,0:T(8,128)}) custom-call(s32[1]{0:T(128)} %bitcast.1.slab_ref, f32[48,16,128]{2,1,0:T(8,128)} %head_ref.3, f32[48,16,128]{2,1,0:T(8,128)} %perm_ref.3, f32[16,128]{1,0:T(8,128)} %wells_ref.3), custom_call_target="tpu_custom_call" | custom-call | tf_op jit(solution)/shard_map/pack_rims/pallas_call | solution.py:67
  2.8 0.5 collective-permute-start
  3.3 0.7 collective-permute-start.1
  4.0 0.8 convert_element_type.14
  4.8 0.6 reshape.71.table_ref
  5.5 0.8 fusion.20
  6.3 0.8 fusion.18
  7.0 1.3 add_select_fusion
  8.3 9.8 %kernel_of_observed.1 = (bf16[2048,1024]{1,0:T(8,128)(2,1)}, bf16[2048,1024]{1,0:T(8,128)(2,1)}) custom-call(s32[1]{0:T(128)} %bitcast.1.slab_ref, f32[64,128]{1,0:T(8,128)} %reshape.71.table_ref, s32[1,1024]{1,0:T(1,128)} %bitcast.53, s32[16,128]{1,0:T(8,128)} %layer_ref.3), custom_call_target="tpu_custom_call" | custom-call | flops 33554432 | bytes 8388608 | tf_op jit(solution)/shard_map/kernel_of_observed/pallas_call | solution.py:150
  18.1 0.8 fusion.19
  18.9 0.7 copy-done.4
  19.6 12.3 %forecast.1 = (f32[48,2048]{1,0:T(8,128)}, f32[48,512]{1,0:T(8,128)}, f32[48,512]{1,0:T(8,128)}) custom-call(s32[1]{0:T(128)} %bitcast.1.slab_ref, f32[48,16,128]{2,1,0:T(8,128)} %head_ref.3, f32[48,16,128]{2,1,0:T(8,128)} %perm_ref.3, f32[16,128]{1,0:T(8,128)} %wells_ref.3, f32[4,104,128]{2,1,0:T(8,128)} %copy-done.4, f32[4,104,128]{2,1,0:T(8,128)} %copy-done.5, ...), custom_call_target="tpu_custom_call" | custom-call | flops 603979776 | bytes 8388608 | tf_op jit(solution)/shard_map/forecast/pallas_call | solution.py:260
  32.0 3.2 %collective-permute-start.2 = (f32[48,512]{1,0:T(8,128)}, f32[48,512]{1,0:T(8,128)S(1)}, u32[]{:S(2)}, u32[]{:S(2)}) collective-permute-start(f32[48,512]{1,0:T(8,128)} %get-tuple-element.18), channel_id=1, source_target_pairs={{0,1},{1,0},{2,3},{3,2},{4,5},{5,4},{6,7},{7,6},{8,9},{9,8},{10,11... | collective-permute-start | bytes 294920 | tf_op jit(solution)/shard_map/ppermute | solution.py:454
  35.2 1.6 %collective-permute-start.10 = (f32[48,2048]{1,0:T(8,128)}, f32[48,2048]{1,0:T(8,128)S(1)}, u32[]{:S(2)}, u32[]{:S(2)}) collective-permute-start(f32[48,2048]{1,0:T(8,128)} %get-tuple-element.19.refs_0_), channel_id=1, source_target_pairs={{0,16},{8,24},{16,0},{24,8},{1,17},{9,25},{17,1},{25,9},{2,18},{10... | collective-permute-start | bytes 1179656 | tf_op jit(solution)/shard_map/ppermute | solution.py:454
  36.8 1.4 collective-permute-start.11
  38.2 0.5 collective-permute-start.9
  38.8 0.9 add.118
  39.7 1.6 %collective-permute-start.3 = (f32[48,512]{1,0:T(8,128)S(1)}, f32[48,512]{1,0:T(8,128)S(1)}, u32[]{:S(2)}, u32[]{:S(2)}) collective-permute-start(f32[48,512]{1,0:T(8,128)S(1)} %add.118), channel_id=1, source_target_pairs={{0,2},{1,3},{2,0},{3,1},{4,6},{5,7},{6,4},{7,5},{8,10},{9,11},{10,... | collective-permute-start | bytes 294920 | tf_op jit(solution)/shard_map/ppermute | solution.py:454
  41.4 0.6 reshape.76.at_in_ref
  42.0 0.6 slice.112.refs_4_
  42.6 0.6 slice.113.refs_5_
  43.1 9.5 %kernel_of_pixels.1 = (bf16[2048,1024]{1,0:T(8,128)(2,1)}, bf16[2048,1024]{1,0:T(8,128)(2,1)}) custom-call(s32[1]{0:T(128)} %bitcast.1.slab_ref, f32[2,1024]{1,0:T(2,128)} %reshape.76.at_in_ref, s32[16,128]{1,0:T(8,128)} %layer_ref.3), custom_call_target="tpu_custom_call" | custom-call | flops 33554432 | bytes 8388608 | tf_op jit(solution)/shard_map/kernel_of_pixels/pallas_call | solution.py:150
  52.7 2.2 %collective-permute-start.4 = (f32[48,512]{1,0:T(8,128)S(1)}, f32[48,512]{1,0:T(8,128)S(1)}, u32[]{:S(2)}, u32[]{:S(2)}) collective-permute-start(f32[48,512]{1,0:T(8,128)S(1)} %add.119), channel_id=1, source_target_pairs={{0,4},{1,5},{2,6},{3,7},{4,0},{5,1},{6,2},{7,3},{8,12},{9,13},{10,... | collective-permute-start | bytes 294920 | tf_op jit(solution)/shard_map/ppermute | solution.py:454
  54.9 4.3 %collective-permute-done.4 = f32[48,512]{1,0:T(8,128)S(1)} collective-permute-done((f32[48,512]{1,0:T(8,128)S(1)}, f32[48,512]{1,0:T(8,128)S(1)}, u32[]{:S(2)}, u32[]{:S(2)}) %collective-permute-start.4) | collective-permute-done | bytes 98336 | tf_op jit(solution)/shard_map/ppermute | solution.py:454
  59.3 1.6 %collective-permute-start.5 = (f32[48,512]{1,0:T(8,128)S(1)}, f32[48,512]{1,0:T(8,128)S(1)}, u32[]{:S(2)}, u32[]{:S(2)}) collective-permute-start(f32[48,512]{1,0:T(8,128)S(1)} %add.120.refs_0_), channel_id=1, source_target_pairs={{0,8},{8,0},{16,24},{24,16},{1,9},{9,1},{17,25},{25,17},{2,10},{10... | collective-permute-start | bytes 294920 | tf_op jit(solution)/shard_map/ppermute | solution.py:454
  60.8 1.6 %collective-permute-start.6 = (f32[48,512]{1,0:T(8,128)S(1)}, f32[48,512]{1,0:T(8,128)S(1)}, u32[]{:S(2)}, u32[]{:S(2)}) collective-permute-start(f32[48,512]{1,0:T(8,128)S(1)} %add.120.refs_0_), channel_id=1, source_target_pairs={{0,16},{8,24},{16,0},{24,8},{1,17},{9,25},{17,1},{25,9},{2,18},{10... | collective-permute-start | bytes 294920 | tf_op jit(solution)/shard_map/ppermute | solution.py:454
  62.4 1.5 %collective-permute-done.5.refs_1_ = f32[48,512]{1,0:T(8,128)S(1)} collective-permute-done((f32[48,512]{1,0:T(8,128)S(1)}, f32[48,512]{1,0:T(8,128)S(1)}, u32[]{:S(2)}, u32[]{:S(2)}) %collective-permute-start.5) | collective-permute-done | bytes 98336 | tf_op jit(solution)/shard_map/ppermute | solution.py:454
  63.9 3.3 %collective-permute-start.7 = (f32[48,512]{1,0:T(8,128)S(1)}, f32[48,512]{1,0:T(8,128)S(1)}, u32[]{:S(2)}, u32[]{:S(2)}) collective-permute-start(f32[48,512]{1,0:T(8,128)S(1)} %add.120.refs_0_), channel_id=1, source_target_pairs={{0,24},{8,16},{16,8},{24,0},{1,25},{9,17},{17,9},{25,1},{2,26},{10... | collective-permute-start | bytes 294920 | tf_op jit(solution)/shard_map/ppermute | solution.py:454
  67.3 2.6 %collective-permute-done.7.refs_3_ = f32[48,512]{1,0:T(8,128)S(1)} collective-permute-done((f32[48,512]{1,0:T(8,128)S(1)}, f32[48,512]{1,0:T(8,128)S(1)}, u32[]{:S(2)}, u32[]{:S(2)}) %collective-permute-start.7) | collective-permute-done | bytes 98336 | tf_op jit(solution)/shard_map/ppermute | solution.py:454
  69.9 0.6 copy-done.12
  70.5 2.6 %gram.1 = f32[192,256]{1,0:T(8,128)} custom-call(s32[1]{0:T(128)} %bitcast.member_ref, f32[48,512]{1,0:T(8,128)} %copy-done.7, f32[48,512]{1,0:T(8,128)} %copy-done.10, f32[48,512]{1,0:T(8,128)} %copy-done.11, f32[48,512]{1,0:T(8,128)} %copy-done.12, f32[1,512]{1,0:T(1,128)} %slice.112.refs_4_, f32[1,512]{1,0:T(1,128)} %slice.113.refs_5_), custom_call_target="tpu_custom_call" | custom-call | flops 226492416 | bytes 393216 | tf_op jit(solution)/shard_map/gram/pallas_call | solution.py:370
  73.2 0.7 copy-done
  74.2 8.2 %subsidence.1 = (f32[192,512]{1,0:T(8,128)}, f32[192,512]{1,0:T(8,128)}) custom-call(s32[1]{0:T(128)} %bitcast.member_ref, f32[48,2048]{1,0:T(8,128)} %get-tuple-element.19.refs_0_, f32[48,2048]{1,0:T(8,128)} %copy-done.2, f32[48,2048]{1,0:T(8,128)} %copy-done, f32[48,2048]{1,0:T(8,128)} %copy-done.1, bf16[2048,1024]{1,0:T(8,128)(2,1)} %get-tuple-element.20.refs_4_, ...), custom_call_target="tpu_custom_call" | custom-call | flops 2415919104 | bytes 9961472 | tf_op jit(solution)/shard_map/subsidence/pallas_call | solution.py:318
  82.3 0.5 collective-permute-start.12
  83.1 11.7 %cholesky.50 = f32[128,128]{1,0:T(8,128)S(1)} custom-call(f32[128,128]{1,0:T(8,128)S(1)} %cholesky.121), custom_call_target="Cholesky" | custom-call | tf_op jit(solution)/shard_map/jit(cholesky)/cholesky | solution.py:427
  94.9 9.8 %custom-call.15 = f32[1,128,128]{1,2,0:T(8,128)S(1)} custom-call(f32[1,128,128]{2,1,0:T(8,128)S(1)} %get-tuple-element.48), custom_call_target="InvertDiagBlocksLowerTriangular" | custom-call | tf_op jit(solution)/shard_map/jit(cholesky)/cholesky | solution.py:427
  105.1 5.8 %cholesky.108 = f32[64,64]{1,0:T(8,128)S(1)} custom-call(f32[64,64]{1,0:T(8,128)S(1)} %convolution_subtract_fusion.1), custom_call_target="Cholesky" | custom-call | tf_op jit(solution)/shard_map/jit(cholesky)/cholesky | solution.py:427
  111.0 0.7 compare_reduce_fusion
  111.7 0.6 compare_reduce_fusion.1
  113.8 19.7 %custom-call.16 = f32[2,128,128]{1,2,0:T(8,128)S(1)} custom-call(f32[2,128,128]{2,1,0:T(8,128)S(1)} %pad_maximum_fusion.3), custom_call_target="InvertDiagBlocksLowerTriangular" | custom-call | tf_op jit(solution)/shard_map/jit(_solve_triangular)/triangular_solve | solution.py:428
  133.5 0.3 fusion.3
  133.9 0.3 convolution_subtract_fusion
  135.5 3.7 %collective-permute-start.14 = (f32[192,128]{1,0:T(8,128)S(1)}, f32[192,128]{1,0:T(8,128)S(1)}, u32[]{:S(2)}, u32[]{:S(2)}) collective-permute-start(f32[192,128]{1,0:T(8,128)S(1)} %get-tuple-element.46), channel_id=1, source_target_pairs={{0,4},{1,5},{2,6},{3,7},{4,0},{5,1},{6,2},{7,3},{8,12},{9,13},{10,... | collective-permute-start | bytes 294920 | tf_op jit(solution)/shard_map/ppermute | solution.py:454
  139.2 0.7 collective-permute-start.15
  139.9 0.7 add_multiply_fusion.mix_ref
  140.5 3.0 %update.1 = f32[48,16,128]{2,1,0:T(8,128)} custom-call(s32[1]{0:T(128)} %bitcast.member_ref, f32[48,192]{1,0:T(8,128)} %add_multiply_fusion.mix_ref, f32[48,2048]{1,0:T(8,128)} %get-tuple-element.19.refs_0_, f32[48,2048]{1,0:T(8,128)} %copy-done.2, f32[48,2048]{1,0:T(8,128)} %copy-done, f32[48,2048]{1,0:T(8,128)} %copy-done.1), custom_call_target="tpu_custom_call" | custom-call | flops 113246208 | bytes 1572864 | tf_op jit(solution)/shard_map/update/pallas_call | solution.py:409
  143.5 3.6 %collective-permute-done.14 = f32[192,128]{1,0:T(8,128)S(1)} collective-permute-done((f32[192,128]{1,0:T(8,128)S(1)}, f32[192,128]{1,0:T(8,128)S(1)}, u32[]{:S(2)}, u32[]{:S(2)}) %collective-permute-start.14) | collective-permute-done | bytes 98336 | tf_op jit(solution)/shard_map/ppermute | solution.py:454
  147.1 0.7 add_bitcast_fusion
  (71 shorter events, 2.7 us)
Async XLA Ops:
  2.8 16.0 %collective-permute-start = (f32[4,104,128]{2,1,0:T(8,128)}, f32[4,104,128]{2,1,0:T(8,128)S(1)}, u32[]{:S(2)}, u32[]{:S(2)}) collective-permute-start(f32[4,104,128]{2,1,0:T(8,128)} %get-tuple-element.13), channel_id=1, source_target_pairs={{0,1},{1,0},{2,3},{3,2},{4,5},{5,4},{6,7},{7,6},{8,9},{9,8},{10,11... | collective-permute-start | bytes 638984 | tf_op jit(solution)/shard_map/ppermute | solution.py:458
  3.3 15.5 %collective-permute-start.1 = (f32[4,104,128]{2,1,0:T(8,128)}, f32[4,104,128]{2,1,0:T(8,128)S(1)}, u32[]{:S(2)}, u32[]{:S(2)}) collective-permute-start(f32[4,104,128]{2,1,0:T(8,128)} %get-tuple-element.14), channel_id=1, source_target_pairs={{1,2},{3,4},{5,6},{2,1},{4,3},{6,5},{9,10},{11,12},{13,14},{10,9},... | collective-permute-start | bytes 638984 | tf_op jit(solution)/shard_map/ppermute | solution.py:457
  18.9 0.7 copy-start.4
  18.9 0.8 copy-start.5
  19.6 15.5 %copy-start.8 = (f32[1024]{0:T(1024)S(1)}, f32[1024]{0:T(1024)}, u32[]{:S(2)}) copy-start(f32[1024]{0:T(1024)} %param.14) | copy-start | bytes 12292
  19.6 15.5 %copy-start.9 = (f32[1024]{0:T(1024)S(1)}, f32[1024]{0:T(1024)}, u32[]{:S(2)}) copy-start(f32[1024]{0:T(1024)} %param.15) | copy-start | bytes 12292
  32.0 6.8 %collective-permute-start.2 = (f32[48,512]{1,0:T(8,128)}, f32[48,512]{1,0:T(8,128)S(1)}, u32[]{:S(2)}, u32[]{:S(2)}) collective-permute-start(f32[48,512]{1,0:T(8,128)} %get-tuple-element.18), channel_id=1, source_target_pairs={{0,1},{1,0},{2,3},{3,2},{4,5},{5,4},{6,7},{7,6},{8,9},{9,8},{10,11... | collective-permute-start | bytes 294920 | tf_op jit(solution)/shard_map/ppermute | solution.py:454
  35.2 37.9 %collective-permute-start.10 = (f32[48,2048]{1,0:T(8,128)}, f32[48,2048]{1,0:T(8,128)S(1)}, u32[]{:S(2)}, u32[]{:S(2)}) collective-permute-start(f32[48,2048]{1,0:T(8,128)} %get-tuple-element.19.refs_0_), channel_id=1, source_target_pairs={{0,16},{8,24},{16,0},{24,8},{1,17},{9,25},{17,1},{25,9},{2,18},{10... | collective-permute-start | bytes 1179656 | tf_op jit(solution)/shard_map/ppermute | solution.py:454
  36.8 36.4 %collective-permute-start.11 = (f32[48,2048]{1,0:T(8,128)}, f32[48,2048]{1,0:T(8,128)S(1)}, u32[]{:S(2)}, u32[]{:S(2)}) collective-permute-start(f32[48,2048]{1,0:T(8,128)} %get-tuple-element.19.refs_0_), channel_id=1, source_target_pairs={{0,24},{8,16},{16,8},{24,0},{1,25},{9,17},{17,9},{25,1},{2,26},{10... | collective-permute-start | bytes 1179656 | tf_op jit(solution)/shard_map/ppermute | solution.py:454
  38.2 35.0 %collective-permute-start.9 = (f32[48,2048]{1,0:T(8,128)}, f32[48,2048]{1,0:T(8,128)S(1)}, u32[]{:S(2)}, u32[]{:S(2)}) collective-permute-start(f32[48,2048]{1,0:T(8,128)} %get-tuple-element.19.refs_0_), channel_id=1, source_target_pairs={{0,8},{8,0},{16,24},{24,16},{1,9},{9,1},{17,25},{25,17},{2,10},{10... | collective-permute-start | bytes 1179656 | tf_op jit(solution)/shard_map/ppermute | solution.py:454
  39.7 13.0 %collective-permute-start.3 = (f32[48,512]{1,0:T(8,128)S(1)}, f32[48,512]{1,0:T(8,128)S(1)}, u32[]{:S(2)}, u32[]{:S(2)}) collective-permute-start(f32[48,512]{1,0:T(8,128)S(1)} %add.118), channel_id=1, source_target_pairs={{0,2},{1,3},{2,0},{3,1},{4,6},{5,7},{6,4},{7,5},{8,10},{9,11},{10,... | collective-permute-start | bytes 294920 | tf_op jit(solution)/shard_map/ppermute | solution.py:454
  52.7 6.6 %collective-permute-start.4 = (f32[48,512]{1,0:T(8,128)S(1)}, f32[48,512]{1,0:T(8,128)S(1)}, u32[]{:S(2)}, u32[]{:S(2)}) collective-permute-start(f32[48,512]{1,0:T(8,128)S(1)} %add.119), channel_id=1, source_target_pairs={{0,4},{1,5},{2,6},{3,7},{4,0},{5,1},{6,2},{7,3},{8,12},{9,13},{10,... | collective-permute-start | bytes 294920 | tf_op jit(solution)/shard_map/ppermute | solution.py:454
  59.3 10.6 %copy-start.7 = (f32[48,512]{1,0:T(8,128)}, f32[48,512]{1,0:T(8,128)S(1)}, u32[]{:S(2)}) copy-start(f32[48,512]{1,0:T(8,128)S(1)} %add.120.refs_0_) | copy-start | bytes 294916
  59.3 4.7 %collective-permute-start.5 = (f32[48,512]{1,0:T(8,128)S(1)}, f32[48,512]{1,0:T(8,128)S(1)}, u32[]{:S(2)}, u32[]{:S(2)}) collective-permute-start(f32[48,512]{1,0:T(8,128)S(1)} %add.120.refs_0_), channel_id=1, source_target_pairs={{0,8},{8,0},{16,24},{24,16},{1,9},{9,1},{17,25},{25,17},{2,10},{10... | collective-permute-start | bytes 294920 | tf_op jit(solution)/shard_map/ppermute | solution.py:454
  60.8 6.4 %collective-permute-start.6 = (f32[48,512]{1,0:T(8,128)S(1)}, f32[48,512]{1,0:T(8,128)S(1)}, u32[]{:S(2)}, u32[]{:S(2)}) collective-permute-start(f32[48,512]{1,0:T(8,128)S(1)} %add.120.refs_0_), channel_id=1, source_target_pairs={{0,16},{8,24},{16,0},{24,8},{1,17},{9,25},{17,1},{25,9},{2,18},{10... | collective-permute-start | bytes 294920 | tf_op jit(solution)/shard_map/ppermute | solution.py:454
  63.9 5.9 %copy-start.10 = (f32[48,512]{1,0:T(8,128)}, f32[48,512]{1,0:T(8,128)S(1)}, u32[]{:S(2)}) copy-start(f32[48,512]{1,0:T(8,128)S(1)} %collective-permute-done.5.refs_1_) | copy-start | bytes 294916
  63.9 5.9 %collective-permute-start.7 = (f32[48,512]{1,0:T(8,128)S(1)}, f32[48,512]{1,0:T(8,128)S(1)}, u32[]{:S(2)}, u32[]{:S(2)}) collective-permute-start(f32[48,512]{1,0:T(8,128)S(1)} %add.120.refs_0_), channel_id=1, source_target_pairs={{0,24},{8,16},{16,8},{24,0},{1,25},{9,17},{17,9},{25,1},{2,26},{10... | collective-permute-start | bytes 294920 | tf_op jit(solution)/shard_map/ppermute | solution.py:454
  67.3 2.6 %copy-start.11 = (f32[48,512]{1,0:T(8,128)}, f32[48,512]{1,0:T(8,128)S(1)}, u32[]{:S(2)}) copy-start(f32[48,512]{1,0:T(8,128)S(1)} %collective-permute-done.6.refs_2_) | copy-start | bytes 294916
  69.9 0.6 copy-start.12
  73.1 9.7 %collective-permute-start.8 = (f32[192,256]{1,0:T(8,128)}, f32[192,256]{1,0:T(8,128)S(1)}, u32[]{:S(2)}, u32[]{:S(2)}) collective-permute-start(f32[192,256]{1,0:T(8,128)} %gram.1), channel_id=1, source_target_pairs={{0,1},{1,0},{2,3},{3,2},{4,5},{5,4},{6,7},{7,6},{8,9},{9,8},{10,11... | collective-permute-start | bytes 589832 | tf_op jit(solution)/shard_map/ppermute | solution.py:454
  73.1 0.8 copy-start
  73.2 0.9 copy-start.1
  73.2 1.0 copy-start.2
  74.2 8.7 %copy-start.6 = (f32[192,256]{1,0:T(8,128)S(1)}, f32[192,256]{1,0:T(8,128)}, u32[]{:S(2)}) copy-start(f32[192,256]{1,0:T(8,128)} %gram.1) | copy-start | bytes 589828
  82.3 53.0 %copy-start.3 = (f32[192,512]{1,0:T(8,128)S(1)}, f32[192,512]{1,0:T(8,128)}, u32[]{:S(2)}) copy-start(f32[192,512]{1,0:T(8,128)} %get-tuple-element.22) | copy-start | bytes 1179652
  82.3 52.9 %collective-permute-start.12 = (f32[192,512]{1,0:T(8,128)}, f32[192,512]{1,0:T(8,128)S(1)}, u32[]{:S(2)}, u32[]{:S(2)}) collective-permute-start(f32[192,512]{1,0:T(8,128)} %get-tuple-element.23), channel_id=1, source_target_pairs={{0,1},{1,0},{2,3},{3,2},{4,5},{5,4},{6,7},{7,6},{8,9},{9,8},{10,11... | collective-permute-start | bytes 1179656 | tf_op jit(solution)/shard_map/ppermute | solution.py:454
  135.4 8.1 %collective-permute-start.13 = (f32[192,128]{1,0:T(8,128)S(1)}, f32[192,128]{1,0:T(8,128)S(1)}, u32[]{:S(2)}, u32[]{:S(2)}) collective-permute-start(f32[192,128]{1,0:T(8,128)S(1)} %get-tuple-element.44), channel_id=1, source_target_pairs={{0,2},{1,3},{2,0},{3,1},{4,6},{5,7},{6,4},{7,5},{8,10},{9,11},{10,... | collective-permute-start | bytes 294920 | tf_op jit(solution)/shard_map/ppermute | solution.py:454
  135.5 11.6 %collective-permute-start.14 = (f32[192,128]{1,0:T(8,128)S(1)}, f32[192,128]{1,0:T(8,128)S(1)}, u32[]{:S(2)}, u32[]{:S(2)}) collective-permute-start(f32[192,128]{1,0:T(8,128)S(1)} %get-tuple-element.46), channel_id=1, source_target_pairs={{0,4},{1,5},{2,6},{3,7},{4,0},{5,1},{6,2},{7,3},{8,12},{9,13},{10,... | collective-permute-start | bytes 294920 | tf_op jit(solution)/shard_map/ppermute | solution.py:454
  139.2 7.9 %collective-permute-start.15 = (f32[192,128]{1,0:T(8,128)S(1)}, f32[192,128]{1,0:T(8,128)S(1)}, u32[]{:S(2)}, u32[]{:S(2)}) collective-permute-start(f32[192,128]{1,0:T(8,128)S(1)} %get-tuple-element.45), channel_id=1, source_target_pairs={{0,6},{1,7},{2,4},{3,5},{4,2},{5,3},{6,0},{7,1},{8,14},{9,15},{10,... | collective-permute-start | bytes 294920 | tf_op jit(solution)/shard_map/ppermute | solution.py:454

commit v2 on v1

--- a/solution.py
+++ b/solution.py
@@ -16,11 +16,11 @@
 
 F32 = jnp.float32
 BF16 = jnp.bfloat16
-VMEM_BYTES = 56 * 1024 * 1024
-
-
-def params(**more):
-    return pltpu.CompilerParams(vmem_limit_bytes=VMEM_BYTES, **more)
+MIB = 1024 * 1024
+
+
+def params(mib=16, **more):
+    return pltpu.CompilerParams(vmem_limit_bytes=mib * MIB, **more)
 
 
 def cost(flops, bytes_accessed):
@@ -379,18 +379,105 @@
     )(member, *pieces, value, sigma)
 
 
-def update_kernel(groups, members, member_ref, mix_ref, *refs):
+def eliminate_panel(rows, scaled, first, count):
+    groups = count // 8
+    tiles = rows.shape[1] // 128
+    sub_row = lax.broadcasted_iota(jnp.int32, (8, 128), 0)
+    lane = lax.broadcasted_iota(jnp.int32, (8, 128), 1)
+    x = [[rows[8 * g : 8 * g + 8, 128 * t : 128 * t + 128] for t in range(tiles)] for g in range(groups)]
+    full = lambda v: jnp.broadcast_to(v, (8, 128))
+    scale = [None] * groups
+    for s in range(groups):
+        column = first + 8 * s
+        tile, at = column // 128, column % 128
+        c = [[full(x[g][tile][:, at + j : at + j + 1]) for g in range(s, groups)] for j in range(8)]
+        scale[s] = jnp.zeros((8, 128), F32)
+        for j in range(8):
+            pivot = full(c[j][0][j : j + 1, :])
+            inverse = pltpu.reciprocal(pivot, approx=False)
+            below = sub_row > j
+            m = [v * inverse for v in c[j]]
+            m[0] = jnp.where(below, m[0], 0.0)
+            root = lax.rsqrt(pivot)
+            root = root * (1.5 - 0.5 * pivot * root * root)
+            scale[s] = jnp.where(sub_row == j, root, scale[s])
+            for l in range(j + 1, 8):
+                entry = full(c[l][0][j : j + 1, :])
+                c[l] = [v - k * entry for v, k in zip(c[l], m)]
+            here = lane == at + j
+            for t in range(tiles):
+                row = full(x[s][t][j : j + 1, :])
+                if t == tile:
+                    row = jnp.where(here, 1.0, row)
+                for g in range(s, groups):
+                    old = x[g][t]
+                    if t == tile:
+                        old = jnp.where(here & below if g == s else here, 0.0, old)
+                    x[g][t] = old - m[g - s] * row
+    for g in range(groups):
+        for t in range(tiles):
+            value = x[g][t]
+            column = lane + 128 * t
+            row = first + 8 * g + sub_row
+            inside = column < first + count
+            value = jnp.where(inside & (column == row), 1.0, jnp.where(inside & (column > row), 0.0, value))
+            scaled[first + 8 * g : first + 8 * g + 8, 128 * t : 128 * t + 128] = value * scale[g]
+
+
+def invert(count, work_ref):
+    every, width = work_ref.shape
+    panel = 32
+    for first in range(0, every, panel):
+        eliminate_panel(work_ref[first : first + panel, :], work_ref, first, panel)
+        below = first + panel
+        if below < every:
+            done = work_ref[first:below, :]
+            product = lax.dot_general(
+                done[:, below:every] if below % 128 == 0 else done[:, below // 128 * 128 : every],
+                done,
+                (((0,), (0,)), ((), ())),
+                precision=lax.Precision.HIGHEST,
+                preferred_element_type=F32,
+            )
+            column = lax.broadcasted_iota(jnp.int32, (every - below, width), 1)
+            own = (column >= first) & (column < below)
+            old = jnp.where(own, 0.0, work_ref[below:every, :])
+            work_ref[below:every, :] = old - product[below - below // 128 * 128 :]
+
+
+def finish_kernel(groups, members, member_ref, gram_ref, more_ref, *refs):
     pieces = refs[:groups]
-    out_ref, cast_ref = refs[groups:]
+    out_ref, cast_ref, work_ref = refs[groups:]
     padded, total = pieces[0].shape
     rows, cells = out_ref.shape[1:]
-    every = groups * padded
+    every, width = work_ref.shape
+    count = groups * members
+    member = member_ref[0]
     for offset in range(groups):
-        at = member_ref[0] ^ offset
+        at = member ^ offset
         high, low = split(pieces[offset][...])
         cast_ref[at] = high
         cast_ref[groups + at] = low
-    mix_high, mix_low = split(mix_ref[...])
+    row = lax.broadcasted_iota(jnp.int32, (every, width), 0)
+    column = lax.broadcasted_iota(jnp.int32, (every, width), 1)
+    work_ref[...] = gram_ref[...] + more_ref[...] + jnp.where(row == column, count - 1.0, 0.0)
+    invert(count, work_ref)
+
+    solved = jnp.broadcast_to(work_ref[:, every : every + 1], (every, width))
+    inverse = jnp.where(column <= row, work_ref[...], 0.0)
+    weights = jnp.sum(inverse * solved, 0, keepdims=True)
+    first = pl.multiple_of(member * padded, padded)
+    column = lax.broadcasted_iota(jnp.int32, (padded, width), 1)
+    row = lax.broadcasted_iota(jnp.int32, (padded, width), 0) + first
+    own = jnp.where(column <= row, work_ref[pl.ds(first, padded), :], 0.0)
+    here = column < every
+    if padded != members:
+        here = here & (lax.rem(column, padded) < members)
+    mix = jnp.where(here, weights + math.sqrt(count - 1.0) * own, 0.0)
+    mix = mix + (1.0 - jnp.sum(mix, 1, keepdims=True)) * (1.0 / count)
+    mix = jnp.where(here, mix, 0.0)[:, :every]
+
+    mix_high, mix_low = split(mix)
     mix_both = jnp.concatenate([mix_high, mix_low], 0)
     depth = 4 * cells if rows % 4 == 0 else cells
     for lane in range(0, total, depth):
@@ -402,37 +489,20 @@
             out_ref[:, lane // cells + part, :] = value[:members, part * cells : (part + 1) * cells]
 
 
-def update(members, rows, cells, member, mix, pieces):
+def finish(members, rows, cells, member, gram, more, pieces):
     groups = len(pieces)
     padded, total = pieces[0].shape
     vmem = pl.BlockSpec(memory_space=pltpu.VMEM)
     return pl.pallas_call(
-        functools.partial(update_kernel, groups, members),
+        functools.partial(finish_kernel, groups, members),
         out_shape=jax.ShapeDtypeStruct((members, rows, cells), F32),
-        in_specs=[pl.BlockSpec(memory_space=pltpu.SMEM)] + [vmem] * (groups + 1),
+        in_specs=[pl.BlockSpec(memory_space=pltpu.SMEM)] + [vmem] * (groups + 2),
         out_specs=vmem,
-        scratch_shapes=[pltpu.VMEM((2 * groups, padded, total), BF16)],
+        scratch_shapes=[pltpu.VMEM((2 * groups, padded, total), BF16), pltpu.VMEM(gram.shape, F32)],
         compiler_params=params(),
         cost_estimate=cost(6 * padded * groups * padded * total, 4 * groups * padded * total),
-        name="update",
-    )(member, mix, *pieces)
-
-
-def weights_of(members, padded, member, gram_sum):
-    every = gram_sum.shape[0]
-    count = every // padded * members
-    ident = jnp.eye(every, dtype=F32)
-    gram = gram_sum[:, :every] + (count - 1.0) * ident
-    rhs = gram_sum[:, every]
-    factor = jnp.linalg.cholesky(gram)
-    inverse = jax.scipy.linalg.solve_triangular(factor, ident, lower=True)
-    high = lax.Precision.HIGHEST
-    weights = jnp.dot(inverse.T, jnp.dot(inverse, rhs, precision=high), precision=high)
-    own = lax.dynamic_slice_in_dim(inverse, member * padded, padded, 0)
-    mix = weights[None, :] + math.sqrt(count - 1.0) * own
-    here = (jnp.arange(every) % padded < members).astype(F32)
-    mix = mix * here[None, :]
-    return (mix + (1.0 - jnp.sum(mix, 1, keepdims=True)) / count) * here[None, :]
+        name="finish",
+    )(member, gram, more, *pieces)
 
 
 def shards(head, perm, wells, layer, coords, obs_index, obs_value, obs_sigma):
@@ -478,7 +548,7 @@
     value = own_first(obs_value)[:, :half]
     sigma = own_first(obs_sigma)[:, :half]
     gram = gram_partial(members, member_s, views, value, sigma)
-    gram = gram + swap(gram, "slab", 1)
+    gram_more = swap(gram, "slab", 1)
 
     chips = slabs // 2
     own_rows = pixel_total // (groups * slabs)
@@ -504,8 +574,7 @@
         sunk_own = sunk_own.reshape(groups, padded, own_rows)[:, :members].reshape(groups * members, own_rows)
     subsidence = sunk_own.T
 
-    mix = weights_of(members, padded, member, gram)
-    analysed = update(members, rows, cells, member_s, mix, pieces)
+    analysed = finish(members, rows, cells, member_s, gram, gram_more, pieces)
     return (analysed, subsidence)
 
 

time: 148 us -> 76.6 us (0.52)
  other arithmetic: 53.3 us -> 2.3 us
  Pallas kernels: 47.5 us -> 32.3 us
  matrix products: 1.7 us -> 0 us
  between operations: 2.34 us -> 0.85 us
    another operation x13 -> x0, other arithmetic: 48.6 us -> none  [the longest x7 28.8 us: weights_of(): factor = jnp.linalg.cholesky(gram)]
    pallas_call x2, Pallas kernels: 19.3 us -> 8.95 us  [forward_kernel(): pl.pallas_call(body, grid=(rows,), out_shape=(out, out), in_specs=[smem]...]
    pallas_call x1, Pallas kernels: 2.96 us -> 8.26 us  [finish(): pl.pallas_call(functools.partial(finish_kernel, groups, members), out_sha...]
    pallas_call x1, Pallas kernels: 12.3 us -> 8.6 us  [forecast(): pl.pallas_call(functools.partial(forecast_kernel, slabs), grid=(total //...]
    unnamed x26 -> x20, local copies, waits for them, and re-layouts: 2.41 us -> 6.07 us
    pallas_call x1, Pallas kernels: 8.16 us -> 5.26 us  [subsidence_partial(): pl.pallas_call(functools.partial(subsidence_kernel, groups), grid=(total...]
    pallas_call x1, Pallas kernels: 2.21 us -> 0.35 us  [pack(): pl.pallas_call(pack_kernel, out_shape=(out, out), in_specs=[pl.BlockSpec(...]
    pallas_call x1, Pallas kernels: 2.62 us -> 0.88 us  [gram_partial(): pl.pallas_call(functools.partial(gram_kernel, groups, members), out_shape...]
  transfers between devices with their start and end apart: 16 -> 16, of which waited for: 4 -> 6; matrix products, arithmetic and copies ran while one was open for 40% -> 3% of each run, Pallas kernels for 22% -> 31%
where the time goes in v2:
time: 76.6 us; the launch traced here: 76 us
  Pallas kernels  32.3 us (42%)
  starting transfers between devices  22.4 us (29%)
  waiting for transfers between devices  11.2 us (15%)
  local copies, waits for them, and re-layouts  6.95 us (9%)
  other arithmetic  2.3 us (3%)
  between operations  0.85 us (1%)
    ppermute x14, starting transfers between devices, swap(): return lax.ppermute(value, axis, [(i, i ^ offset) for i in range(size)])  21.2 us
    ppermute x14, waiting for transfers between devices, swap(): return lax.ppermute(value, axis, [(i, i ^ offset) for i in range(size)])  11.2 us
    pallas_call x2, Pallas kernels, forward_kernel(): pl.pallas_call(body, grid=(rows,), out_shape=(out, out), in_specs=[smem]...  8.95 us
    pallas_call x1, Pallas kernels, forecast(): pl.pallas_call(functools.partial(forecast_kernel, slabs), grid=(total //...  8.6 us
    pallas_call x1, Pallas kernels, finish(): pl.pallas_call(functools.partial(finish_kernel, groups, members), out_sha...  8.26 us
    unnamed x20, local copies, waits for them, and re-layouts  6.07 us
    pallas_call x1, Pallas kernels, subsidence_partial(): pl.pallas_call(functools.partial(subsidence_kernel, groups), grid=(total...  5.26 us
  transfers between devices with their start and end apart: 16, of which 6 were waited for; matrix products, arithmetic and copies ran while one was open for 3% of the time, Pallas kernels for 31%

profile of v2, /device:TPU:0, one launch (start us, length us, event | category | flops | bytes accessed | tf_op | source)
XLA Modules:
  0.0 76.0 jit_solution(1119609943992869606)
XLA Ops:
  0.6 0.0 copy-start
  0.6 1.0 %copy-done = f32[48,16,128]{2,1,0:T(8,128)S(1)} copy-done((f32[48,16,128]{2,1,0:T(8,128)S(1)}, f32[48,16,128]{2,1,0:T(8,128)}, u32[]{:S(2)}) %copy-start) | copy-done | bytes 393240
  1.6 1.0 %copy-done.2 = f32[48,16,128]{2,1,0:T(8,128)S(1)} copy-done((f32[48,16,128]{2,1,0:T(8,128)S(1)}, f32[48,16,128]{2,1,0:T(8,128)}, u32[]{:S(2)}) %copy-start.2) | copy-done | bytes 393240
  2.6 0.7 copy-done.4
  3.3 0.4 pack_rims.1
  3.7 0.6 collective-permute-start
  4.2 0.7 collective-permute-start.1
  4.9 0.8 %convert_element_type.4 = f32[2,4096]{1,0:T(2,128)S(1)} convert(s32[2,4096]{1,0:T(2,128)} %param.12) | non-fusion elementwise | flops 8192 | bytes 65536 | tf_op jit(solution)/shard_map/convert_element_type | solution.py:537
  5.8 0.8 %fusion.2 = (s32[512]{0:T(512)S(1)}, s32[512]{0:T(512)S(1)}) fusion(s32[1024]{0:T(1024)} %param.13), kind=kLoop, calls=%fused_computation.12 | loop fusion | bytes 8192 | tf_op jit(solution)/shard_map/jit(_roll_static)/slice | solution.py:534
  6.6 0.7 add_select_fusion
  7.3 0.7 copy-done.6
  8.0 4.6 %kernel_of_observed.1 = (bf16[2048,1024]{1,0:T(8,128)(2,1)S(1)}, bf16[2048,1024]{1,0:T(8,128)(2,1)S(1)}) custom-call(s32[1]{0:T(128)} %bitcast.1.slab_ref, f32[64,128]{1,0:T(8,128)S(1)} %reshape.30.table_ref, s32[1,1024]{1,0:T(1,128)S(1)} %bitcast.12, s32[16,128]{1,0:T(8,128)S(1)} %copy-done.6), custom_call_target="tpu_custom_call" | custom-call | flops 33554432 | bytes 8388608 | tf_op jit(solution)/shard_map/kernel_of_observed/pallas_call | solution.py:150
  12.5 0.0 collective-permute-done.near_ref
  12.6 0.0 collective-permute-done.1.far_ref
  12.6 0.0 copy-start.1
  12.6 1.0 %copy-done.1 = f32[48,16,128]{2,1,0:T(8,128)S(1)} copy-done((f32[48,16,128]{2,1,0:T(8,128)S(1)}, f32[48,16,128]{2,1,0:T(8,128)}, u32[]{:S(2)}) %copy-start.1) | copy-done | bytes 393240
  13.6 1.0 %copy-done.3 = f32[48,16,128]{2,1,0:T(8,128)S(1)} copy-done((f32[48,16,128]{2,1,0:T(8,128)S(1)}, f32[48,16,128]{2,1,0:T(8,128)}, u32[]{:S(2)}) %copy-start.3) | copy-done | bytes 393240
  14.6 0.7 copy-done.5
  15.3 8.6 %forecast.1 = (f32[48,2048]{1,0:T(8,128)S(1)}, f32[48,512]{1,0:T(8,128)S(1)}, f32[48,512]{1,0:T(8,128)S(1)}) custom-call(s32[1]{0:T(128)} %bitcast.1.slab_ref, f32[48,16,128]{2,1,0:T(8,128)S(1)} %copy-done.1, f32[48,16,128]{2,1,0:T(8,128)S(1)} %copy-done.3, f32[16,128]{1,0:T(8,128)S(1)} %copy-done.5, f32[4,104,128]{2,1,0:T(8,128)S(1)} %collective-permute-done.near_ref, ...), custom_call_target="tpu_custom_call" | custom-call | flops 603979776 | bytes 8388608 | tf_op jit(solution)/shard_map/forecast/pallas_call | solution.py:260
  23.9 2.6 %collective-permute-start.10 = (f32[48,2048]{1,0:T(8,128)S(1)}, f32[48,2048]{1,0:T(8,128)S(1)}, u32[]{:S(2)}, u32[]{:S(2)}) collective-permute-start(f32[48,2048]{1,0:T(8,128)S(1)} %get-tuple-element.19.refs_0_), channel_id=1, source_target_pairs={{0,16},{8,24},{16,0},{24,8},{1,17},{9,25},{17,1},{25,9},{2,18},{10... | collective-permute-start | bytes 1179656 | tf_op jit(solution)/shard_map/ppermute | solution.py:524
  26.5 1.4 %collective-permute-start.11 = (f32[48,2048]{1,0:T(8,128)S(1)}, f32[48,2048]{1,0:T(8,128)S(1)}, u32[]{:S(2)}, u32[]{:S(2)}) collective-permute-start(f32[48,2048]{1,0:T(8,128)S(1)} %get-tuple-element.19.refs_0_), channel_id=1, source_target_pairs={{0,24},{8,16},{16,8},{24,0},{1,25},{9,17},{17,9},{25,1},{2,26},{10... | collective-permute-start | bytes 1179656 | tf_op jit(solution)/shard_map/ppermute | solution.py:524
  27.9 0.1 collective-permute-start.9
  28.0 1.8 %collective-permute-start.2 = (f32[48,512]{1,0:T(8,128)S(1)}, f32[48,512]{1,0:T(8,128)S(1)}, u32[]{:S(2)}, u32[]{:S(2)}) collective-permute-start(f32[48,512]{1,0:T(8,128)S(1)} %get-tuple-element.18), channel_id=1, source_target_pairs={{0,1},{1,0},{2,3},{3,2},{4,5},{5,4},{6,7},{7,6},{8,9},{9,8},{10,11... | collective-permute-start | bytes 294920 | tf_op jit(solution)/shard_map/ppermute | solution.py:524
  29.8 0.9 %collective-permute-done.2 = f32[48,512]{1,0:T(8,128)S(1)} collective-permute-done((f32[48,512]{1,0:T(8,128)S(1)}, f32[48,512]{1,0:T(8,128)S(1)}, u32[]{:S(2)}, u32[]{:S(2)}) %collective-permute-start.2) | collective-permute-done | bytes 98336 | tf_op jit(solution)/shard_map/ppermute | solution.py:524
  30.8 1.9 %collective-permute-start.3 = (f32[48,512]{1,0:T(8,128)S(1)}, f32[48,512]{1,0:T(8,128)S(1)}, u32[]{:S(2)}, u32[]{:S(2)}) collective-permute-start(f32[48,512]{1,0:T(8,128)S(1)} %add.56), channel_id=1, source_target_pairs={{0,2},{1,3},{2,0},{3,1},{4,6},{5,7},{6,4},{7,5},{8,10},{9,11},{10,... | collective-permute-start | bytes 294920 | tf_op jit(solution)/shard_map/ppermute | solution.py:524
  32.8 4.4 %kernel_of_pixels.1 = (bf16[2048,1024]{1,0:T(8,128)(2,1)S(1)}, bf16[2048,1024]{1,0:T(8,128)(2,1)S(1)}) custom-call(s32[1]{0:T(128)} %bitcast.1.slab_ref, f32[2,1024]{1,0:T(2,128)S(1)} %reshape.35.at_in_ref, s32[16,128]{1,0:T(8,128)S(1)} %copy-done.7), custom_call_target="tpu_custom_call" | custom-call | flops 33554432 | bytes 8388608 | tf_op jit(solution)/shard_map/kernel_of_pixels/pallas_call | solution.py:150
  37.2 3.1 %collective-permute-start.4 = (f32[48,512]{1,0:T(8,128)S(1)}, f32[48,512]{1,0:T(8,128)S(1)}, u32[]{:S(2)}, u32[]{:S(2)}) collective-permute-start(f32[48,512]{1,0:T(8,128)S(1)} %add.57), channel_id=1, source_target_pairs={{0,4},{1,5},{2,6},{3,7},{4,0},{5,1},{6,2},{7,3},{8,12},{9,13},{10,... | collective-permute-start | bytes 294920 | tf_op jit(solution)/shard_map/ppermute | solution.py:524
  40.3 3.0 %collective-permute-done.10.refs_2_ = f32[48,2048]{1,0:T(8,128)S(1)} collective-permute-done((f32[48,2048]{1,0:T(8,128)S(1)}, f32[48,2048]{1,0:T(8,128)S(1)}, u32[]{:S(2)}, u32[]{:S(2)}) %collective-permute-start.10) | collective-permute-done | bytes 393248 | tf_op jit(solution)/shard_map/ppermute | solution.py:524
  43.3 0.0 collective-permute-done.11.refs_3_
  43.3 1.7 %collective-permute-done.9.refs_1_ = f32[48,2048]{1,0:T(8,128)S(1)} collective-permute-done((f32[48,2048]{1,0:T(8,128)S(1)}, f32[48,2048]{1,0:T(8,128)S(1)}, u32[]{:S(2)}, u32[]{:S(2)}) %collective-permute-start.9) | collective-permute-done | bytes 393248 | tf_op jit(solution)/shard_map/ppermute | solution.py:524
  45.1 5.3 %subsidence.1 = (f32[192,512]{1,0:T(8,128)S(1)}, f32[192,512]{1,0:T(8,128)S(1)}) custom-call(s32[1]{0:T(128)} %bitcast.member_ref, f32[48,2048]{1,0:T(8,128)S(1)} %get-tuple-element.19.refs_0_, f32[48,2048]{1,0:T(8,128)S(1)} %collective-permute-done.9.refs_1_, f32[48,2048]{1,0:T(8,128)S(1)} %collective-permute-done.10.refs_2_, ...), custom_call_target="tpu_custom_call" | custom-call | flops 2415919104 | bytes 9961472 | tf_op jit(solution)/shard_map/subsidence/pallas_call | solution.py:318
  50.3 1.3 %collective-permute-start.12 = (f32[192,512]{1,0:T(8,128)S(1)}, f32[192,512]{1,0:T(8,128)S(1)}, u32[]{:S(2)}, u32[]{:S(2)}) collective-permute-start(f32[192,512]{1,0:T(8,128)S(1)} %get-tuple-element.23), channel_id=1, source_target_pairs={{0,1},{1,0},{2,3},{3,2},{4,5},{5,4},{6,7},{7,6},{8,9},{9,8},{10,11... | collective-permute-start | bytes 1179656 | tf_op jit(solution)/shard_map/ppermute | solution.py:524
  51.6 2.0 %collective-permute-start.5 = (f32[48,512]{1,0:T(8,128)S(1)}, f32[48,512]{1,0:T(8,128)S(1)}, u32[]{:S(2)}, u32[]{:S(2)}) collective-permute-start(f32[48,512]{1,0:T(8,128)S(1)} %add.58.refs_0_), channel_id=1, source_target_pairs={{0,8},{8,0},{16,24},{24,16},{1,9},{9,1},{17,25},{25,17},{2,10},{10... | collective-permute-start | bytes 294920 | tf_op jit(solution)/shard_map/ppermute | solution.py:524
  53.6 1.5 %collective-permute-start.6 = (f32[48,512]{1,0:T(8,128)S(1)}, f32[48,512]{1,0:T(8,128)S(1)}, u32[]{:S(2)}, u32[]{:S(2)}) collective-permute-start(f32[48,512]{1,0:T(8,128)S(1)} %add.58.refs_0_), channel_id=1, source_target_pairs={{0,16},{8,24},{16,0},{24,8},{1,17},{9,25},{17,1},{25,9},{2,18},{10... | collective-permute-start | bytes 294920 | tf_op jit(solution)/shard_map/ppermute | solution.py:524
  55.1 0.0 collective-permute-start.7
  55.2 1.5 %collective-permute-done.5.refs_1_ = f32[48,512]{1,0:T(8,128)S(1)} collective-permute-done((f32[48,512]{1,0:T(8,128)S(1)}, f32[48,512]{1,0:T(8,128)S(1)}, u32[]{:S(2)}, u32[]{:S(2)}) %collective-permute-start.5) | collective-permute-done | bytes 98336 | tf_op jit(solution)/shard_map/ppermute | solution.py:524
  56.7 2.6 %collective-permute-done.6.refs_2_ = f32[48,512]{1,0:T(8,128)S(1)} collective-permute-done((f32[48,512]{1,0:T(8,128)S(1)}, f32[48,512]{1,0:T(8,128)S(1)}, u32[]{:S(2)}, u32[]{:S(2)}) %collective-permute-start.6) | collective-permute-done | bytes 98336 | tf_op jit(solution)/shard_map/ppermute | solution.py:524
  59.3 1.3 %collective-permute-done.7.refs_3_ = f32[48,512]{1,0:T(8,128)S(1)} collective-permute-done((f32[48,512]{1,0:T(8,128)S(1)}, f32[48,512]{1,0:T(8,128)S(1)}, u32[]{:S(2)}, u32[]{:S(2)}) %collective-permute-start.7) | collective-permute-done | bytes 98336 | tf_op jit(solution)/shard_map/ppermute | solution.py:524
  60.7 0.9 %gram.1.gram_ref = f32[192,256]{1,0:T(8,128)S(1)} custom-call(s32[1]{0:T(128)} %bitcast.member_ref, f32[48,512]{1,0:T(8,128)S(1)} %add.58.refs_0_, f32[48,512]{1,0:T(8,128)S(1)} %collective-permute-done.5.refs_1_, f32[48,512]{1,0:T(8,128)S(1)} %collective-permute-done.6.refs_2_, f32[48,512]{1,0:T(8,128)S(1)} %collective-permute-done.7.refs_3_, ...), custom_call_target="tpu_custom_call" | custom-call | flops 226492416 | bytes 393216 | tf_op jit(solution)/shard_map/gram/pallas_call | solution.py:370
  61.5 0.1 collective-permute-start.8
  61.6 0.1 dynamic-slice_add_fusion.2
  61.7 2.9 %collective-permute-start.13 = (f32[192,128]{1,0:T(8,128)S(1)}, f32[192,128]{1,0:T(8,128)S(1)}, u32[]{:S(2)}, u32[]{:S(2)}) collective-permute-start(f32[192,128]{1,0:T(8,128)S(1)} %get-tuple-element.24), channel_id=1, source_target_pairs={{0,2},{1,3},{2,0},{3,1},{4,6},{5,7},{6,4},{7,5},{8,10},{9,11},{10,... | collective-permute-start | bytes 294920 | tf_op jit(solution)/shard_map/ppermute | solution.py:524
  64.6 1.1 %collective-permute-start.14 = (f32[192,128]{1,0:T(8,128)S(1)}, f32[192,128]{1,0:T(8,128)S(1)}, u32[]{:S(2)}, u32[]{:S(2)}) collective-permute-start(f32[192,128]{1,0:T(8,128)S(1)} %get-tuple-element.26), channel_id=1, source_target_pairs={{0,4},{1,5},{2,6},{3,7},{4,0},{5,1},{6,2},{7,3},{8,12},{9,13},{10,... | collective-permute-start | bytes 294920 | tf_op jit(solution)/shard_map/ppermute | solution.py:524
  65.7 1.4 %collective-permute-start.15 = (f32[192,128]{1,0:T(8,128)S(1)}, f32[192,128]{1,0:T(8,128)S(1)}, u32[]{:S(2)}, u32[]{:S(2)}) collective-permute-start(f32[192,128]{1,0:T(8,128)S(1)} %get-tuple-element.25), channel_id=1, source_target_pairs={{0,6},{1,7},{2,4},{3,5},{4,2},{5,3},{6,0},{7,1},{8,14},{9,15},{10,... | collective-permute-start | bytes 294920 | tf_op jit(solution)/shard_map/ppermute | solution.py:524
  67.1 8.3 %finish.1 = f32[48,16,128]{2,1,0:T(8,128)} custom-call(s32[1]{0:T(128)} %bitcast.member_ref, f32[192,256]{1,0:T(8,128)S(1)} %gram.1.gram_ref, f32[192,256]{1,0:T(8,128)S(1)} %collective-permute-done.8.more_ref, f32[48,2048]{1,0:T(8,128)S(1)} %get-tuple-element.19.refs_0_, f32[48,2048]{1,0:T(8,128)S(1)} %collective-permute-done.9.refs_1_, ...), custom_call_target="tpu_custom_call" | custom-call | flops 113246208 | bytes 1572864 | tf_op jit(solution)/shard_map/finish/pallas_call | solution.py:496
  75.3 0.0 collective-permute-done.13
  75.3 0.0 collective-permute-done.14
  75.4 0.7 add_bitcast_fusion
  (30 shorter events, 0.2 us)
Async XLA Ops:
  0.6 1.0 %copy-start = (f32[48,16,128]{2,1,0:T(8,128)S(1)}, f32[48,16,128]{2,1,0:T(8,128)}, u32[]{:S(2)}) copy-start(f32[48,16,128]{2,1,0:T(8,128)} %head_ref.3) | copy-start | bytes 1179652
  1.6 1.0 %copy-start.2 = (f32[48,16,128]{2,1,0:T(8,128)S(1)}, f32[48,16,128]{2,1,0:T(8,128)}, u32[]{:S(2)}) copy-start(f32[48,16,128]{2,1,0:T(8,128)} %perm_ref.3) | copy-start | bytes 1179652
  2.6 0.7 copy-start.4
  3.7 8.9 %collective-permute-start = (f32[4,104,128]{2,1,0:T(8,128)S(1)}, f32[4,104,128]{2,1,0:T(8,128)S(1)}, u32[]{:S(2)}, u32[]{:S(2)}) collective-permute-start(f32[4,104,128]{2,1,0:T(8,128)S(1)} %get-tuple-element.13), channel_id=1, source_target_pairs={{0,1},{1,0},{2,3},{3,2},{4,5},{5,4},{6,7},{7,6},{8,9},{9,8},{10,11... | collective-permute-start | bytes 638984 | tf_op jit(solution)/shard_map/ppermute | solution.py:528
  4.2 8.3 %collective-permute-start.1 = (f32[4,104,128]{2,1,0:T(8,128)S(1)}, f32[4,104,128]{2,1,0:T(8,128)S(1)}, u32[]{:S(2)}, u32[]{:S(2)}) collective-permute-start(f32[4,104,128]{2,1,0:T(8,128)S(1)} %get-tuple-element.14), channel_id=1, source_target_pairs={{1,2},{3,4},{5,6},{2,1},{4,3},{6,5},{9,10},{11,12},{13,14},{10,9},... | collective-permute-start | bytes 638984 | tf_op jit(solution)/shard_map/ppermute | solution.py:527
  7.3 0.7 copy-start.6
  12.6 1.0 %copy-start.1 = (f32[48,16,128]{2,1,0:T(8,128)S(1)}, f32[48,16,128]{2,1,0:T(8,128)}, u32[]{:S(2)}) copy-start(f32[48,16,128]{2,1,0:T(8,128)} %head_ref.3) | copy-start | bytes 1179652
  13.6 1.0 %copy-start.3 = (f32[48,16,128]{2,1,0:T(8,128)S(1)}, f32[48,16,128]{2,1,0:T(8,128)}, u32[]{:S(2)}) copy-start(f32[48,16,128]{2,1,0:T(8,128)} %perm_ref.3) | copy-start | bytes 1179652
  14.6 0.7 copy-start.5
  15.3 17.5 %copy-start.9 = (f32[1024]{0:T(1024)S(1)}, f32[1024]{0:T(1024)}, u32[]{:S(2)}) copy-start(f32[1024]{0:T(1024)} %param.15) | copy-start | bytes 12292
  15.3 17.5 %copy-start.7 = (s32[16,128]{1,0:T(8,128)S(1)}, s32[16,128]{1,0:T(8,128)}, u32[]{:S(2)}) copy-start(s32[16,128]{1,0:T(8,128)} %layer_ref.3) | copy-start | bytes 24580
  23.9 19.4 %collective-permute-start.10 = (f32[48,2048]{1,0:T(8,128)S(1)}, f32[48,2048]{1,0:T(8,128)S(1)}, u32[]{:S(2)}, u32[]{:S(2)}) collective-permute-start(f32[48,2048]{1,0:T(8,128)S(1)} %get-tuple-element.19.refs_0_), channel_id=1, source_target_pairs={{0,16},{8,24},{16,0},{24,8},{1,17},{9,25},{17,1},{25,9},{2,18},{10... | collective-permute-start | bytes 1179656 | tf_op jit(solution)/shard_map/ppermute | solution.py:524
  26.5 16.9 %collective-permute-start.11 = (f32[48,2048]{1,0:T(8,128)S(1)}, f32[48,2048]{1,0:T(8,128)S(1)}, u32[]{:S(2)}, u32[]{:S(2)}) collective-permute-start(f32[48,2048]{1,0:T(8,128)S(1)} %get-tuple-element.19.refs_0_), channel_id=1, source_target_pairs={{0,24},{8,16},{16,8},{24,0},{1,25},{9,17},{17,9},{25,1},{2,26},{10... | collective-permute-start | bytes 1179656 | tf_op jit(solution)/shard_map/ppermute | solution.py:524
  27.9 17.2 %collective-permute-start.9 = (f32[48,2048]{1,0:T(8,128)S(1)}, f32[48,2048]{1,0:T(8,128)S(1)}, u32[]{:S(2)}, u32[]{:S(2)}) collective-permute-start(f32[48,2048]{1,0:T(8,128)S(1)} %get-tuple-element.19.refs_0_), channel_id=1, source_target_pairs={{0,8},{8,0},{16,24},{24,16},{1,9},{9,1},{17,25},{25,17},{2,10},{10... | collective-permute-start | bytes 1179656 | tf_op jit(solution)/shard_map/ppermute | solution.py:524
  28.0 2.8 %collective-permute-start.2 = (f32[48,512]{1,0:T(8,128)S(1)}, f32[48,512]{1,0:T(8,128)S(1)}, u32[]{:S(2)}, u32[]{:S(2)}) collective-permute-start(f32[48,512]{1,0:T(8,128)S(1)} %get-tuple-element.18), channel_id=1, source_target_pairs={{0,1},{1,0},{2,3},{3,2},{4,5},{5,4},{6,7},{7,6},{8,9},{9,8},{10,11... | collective-permute-start | bytes 294920 | tf_op jit(solution)/shard_map/ppermute | solution.py:524
  30.8 6.4 %collective-permute-start.3 = (f32[48,512]{1,0:T(8,128)S(1)}, f32[48,512]{1,0:T(8,128)S(1)}, u32[]{:S(2)}, u32[]{:S(2)}) collective-permute-start(f32[48,512]{1,0:T(8,128)S(1)} %add.56), channel_id=1, source_target_pairs={{0,2},{1,3},{2,0},{3,1},{4,6},{5,7},{6,4},{7,5},{8,10},{9,11},{10,... | collective-permute-start | bytes 294920 | tf_op jit(solution)/shard_map/ppermute | solution.py:524
  37.2 14.4 %collective-permute-start.4 = (f32[48,512]{1,0:T(8,128)S(1)}, f32[48,512]{1,0:T(8,128)S(1)}, u32[]{:S(2)}, u32[]{:S(2)}) collective-permute-start(f32[48,512]{1,0:T(8,128)S(1)} %add.57), channel_id=1, source_target_pairs={{0,4},{1,5},{2,6},{3,7},{4,0},{5,1},{6,2},{7,3},{8,12},{9,13},{10,... | collective-permute-start | bytes 294920 | tf_op jit(solution)/shard_map/ppermute | solution.py:524
  45.1 6.5 %copy-start.8 = (f32[1024]{0:T(1024)S(1)}, f32[1024]{0:T(1024)}, u32[]{:S(2)}) copy-start(f32[1024]{0:T(1024)} %param.14) | copy-start | bytes 12292
  50.3 11.3 %collective-permute-start.12 = (f32[192,512]{1,0:T(8,128)S(1)}, f32[192,512]{1,0:T(8,128)S(1)}, u32[]{:S(2)}, u32[]{:S(2)}) collective-permute-start(f32[192,512]{1,0:T(8,128)S(1)} %get-tuple-element.23), channel_id=1, source_target_pairs={{0,1},{1,0},{2,3},{3,2},{4,5},{5,4},{6,7},{7,6},{8,9},{9,8},{10,11... | collective-permute-start | bytes 1179656 | tf_op jit(solution)/shard_map/ppermute | solution.py:524
  51.6 5.1 %collective-permute-start.5 = (f32[48,512]{1,0:T(8,128)S(1)}, f32[48,512]{1,0:T(8,128)S(1)}, u32[]{:S(2)}, u32[]{:S(2)}) collective-permute-start(f32[48,512]{1,0:T(8,128)S(1)} %add.58.refs_0_), channel_id=1, source_target_pairs={{0,8},{8,0},{16,24},{24,16},{1,9},{9,1},{17,25},{25,17},{2,10},{10... | collective-permute-start | bytes 294920 | tf_op jit(solution)/shard_map/ppermute | solution.py:524
  53.6 5.7 %collective-permute-start.6 = (f32[48,512]{1,0:T(8,128)S(1)}, f32[48,512]{1,0:T(8,128)S(1)}, u32[]{:S(2)}, u32[]{:S(2)}) collective-permute-start(f32[48,512]{1,0:T(8,128)S(1)} %add.58.refs_0_), channel_id=1, source_target_pairs={{0,16},{8,24},{16,0},{24,8},{1,17},{9,25},{17,1},{25,9},{2,18},{10... | collective-permute-start | bytes 294920 | tf_op jit(solution)/shard_map/ppermute | solution.py:524
  55.1 5.5 %collective-permute-start.7 = (f32[48,512]{1,0:T(8,128)S(1)}, f32[48,512]{1,0:T(8,128)S(1)}, u32[]{:S(2)}, u32[]{:S(2)}) collective-permute-start(f32[48,512]{1,0:T(8,128)S(1)} %add.58.refs_0_), channel_id=1, source_target_pairs={{0,24},{8,16},{16,8},{24,0},{1,25},{9,17},{17,9},{25,1},{2,26},{10... | collective-permute-start | bytes 294920 | tf_op jit(solution)/shard_map/ppermute | solution.py:524
  61.5 5.5 %collective-permute-start.8 = (f32[192,256]{1,0:T(8,128)S(1)}, f32[192,256]{1,0:T(8,128)S(1)}, u32[]{:S(2)}, u32[]{:S(2)}) collective-permute-start(f32[192,256]{1,0:T(8,128)S(1)} %gram.1.gram_ref), channel_id=1, source_target_pairs={{0,1},{1,0},{2,3},{3,2},{4,5},{5,4},{6,7},{7,6},{8,9},{9,8},{10,11... | collective-permute-start | bytes 589832 | tf_op jit(solution)/shard_map/ppermute | solution.py:524
  61.7 13.6 %collective-permute-start.13 = (f32[192,128]{1,0:T(8,128)S(1)}, f32[192,128]{1,0:T(8,128)S(1)}, u32[]{:S(2)}, u32[]{:S(2)}) collective-permute-start(f32[192,128]{1,0:T(8,128)S(1)} %get-tuple-element.24), channel_id=1, source_target_pairs={{0,2},{1,3},{2,0},{3,1},{4,6},{5,7},{6,4},{7,5},{8,10},{9,11},{10,... | collective-permute-start | bytes 294920 | tf_op jit(solution)/shard_map/ppermute | solution.py:524
  64.6 10.8 %collective-permute-start.14 = (f32[192,128]{1,0:T(8,128)S(1)}, f32[192,128]{1,0:T(8,128)S(1)}, u32[]{:S(2)}, u32[]{:S(2)}) collective-permute-start(f32[192,128]{1,0:T(8,128)S(1)} %get-tuple-element.26), channel_id=1, source_target_pairs={{0,4},{1,5},{2,6},{3,7},{4,0},{5,1},{6,2},{7,3},{8,12},{9,13},{10,... | collective-permute-start | bytes 294920 | tf_op jit(solution)/shard_map/ppermute | solution.py:524
  65.7 9.7 %collective-permute-start.15 = (f32[192,128]{1,0:T(8,128)S(1)}, f32[192,128]{1,0:T(8,128)S(1)}, u32[]{:S(2)}, u32[]{:S(2)}) collective-permute-start(f32[192,128]{1,0:T(8,128)S(1)} %get-tuple-element.25), channel_id=1, source_target_pairs={{0,6},{1,7},{2,4},{3,5},{4,2},{5,3},{6,0},{7,1},{8,14},{9,15},{10,... | collective-permute-start | bytes 294920 | tf_op jit(solution)/shard_map/ppermute | solution.py:524

commit v3 on v2

v3 whole, which is shorter than its diff:
```python
import functools
import math

import jax
import jax.numpy as jnp
from jax import lax
from jax.experimental import pallas as pl
from jax.experimental.pallas import tpu as pltpu
from jax.sharding import PartitionSpec as P


STEPS = 4

time_step = 0.15
pixel_span = 64.0
top_depth = 2.0

F32 = jnp.float32
BF16 = jnp.bfloat16
MIB = 1024 * 1024


def params(mib=16, **more):
    return pltpu.CompilerParams(vmem_limit_bytes=mib * MIB, **more)


def cost(flops, bytes_accessed):
    return pl.CostEstimate(flops=int(flops), bytes_accessed=int(bytes_accessed), transcendentals=0)


def split(value):
    high = value.astype(BF16)
    return high, (value - high.astype(F32)).astype(BF16)


def dot(a, b):
    return lax.dot_general(a, b, (((1,), (0,)), ((), ())), preferred_element_type=F32)


VMEM = pl.BlockSpec(memory_space=pltpu.VMEM)
SMEM = pl.BlockSpec(memory_space=pltpu.SMEM)
HBM = pl.BlockSpec(memory_space=pltpu.HBM)


def pack_kernel(slab_ref, head_ref, perm_ref, wells_ref, *refs):
    small = (len(refs) - 3) // 2
    smalls = refs[:small]
    near_ref, far_ref = refs[small : small + 2]
    copies = refs[small + 2 : -1]
    sems = refs[-1]
    members, rows, _ = head_ref.shape
    even = lax.rem(slab_ref[0], 2) == 0
    moves = []

    def move(source, target):
        moves.append(pltpu.make_async_copy(source, target, sems.at[len(moves)]))
        moves[-1].start()

    for k in range(STEPS):
        near = jnp.where(even, rows - STEPS + k, k)
        far = jnp.where(even, k, rows - STEPS + k)
        for target, at in ((near_ref, near), (far_ref, far)):
            move(head_ref.at[:, at, :], target.at[k, 0:members, :])
            move(perm_ref.at[:, at, :], target.at[k, members : 2 * members, :])
            move(wells_ref.at[pl.ds(at, 1), :], target.at[k, 2 * members : 2 * members + 1, :])
    for source, target in zip(smalls, copies):
        move(source, target)
    for one in moves:
        one.wait()


def pack(slab, head, perm, wells, smalls):
    members, _, cells = head.shape
    out = jax.ShapeDtypeStruct((STEPS, 2 * members + 8, cells), F32)
    return pl.pallas_call(
        pack_kernel,
        out_shape=(out, out) + tuple(jax.ShapeDtypeStruct(a.shape, a.dtype) for a in smalls),
        in_specs=[SMEM] + [HBM] * (3 + len(smalls)),
        out_specs=(VMEM,) * (2 + len(smalls)),
        scratch_shapes=[pltpu.SemaphoreType.DMA((6 * STEPS + len(smalls),))],
        compiler_params=params(4),
        name="pack_rims",
    )(slab, head, perm, wells, *smalls)


def kernel_rows(total_rows, slab, at_ref, layer_ref, high_ref, low_ref, dy2_ref):
    cells, pixels = dy2_ref.shape
    rows = layer_ref.shape[0]
    position = lax.broadcasted_iota(jnp.int32, (cells, 128), 0).astype(F32)
    cell_y = (position + 0.5) * (pixel_span / cells)
    for lane in range(0, pixels, 128):
        delta = cell_y - at_ref[1:2, lane : lane + 128]
        dy2_ref[:, lane : lane + 128] = delta * delta

    def one_row(row, carry):
        cell_x = ((slab * rows + row).astype(F32) + 0.5) * (pixel_span / total_rows)
        layer = layer_ref[pl.ds(row, 1), :].astype(F32) + top_depth
        depth = jnp.swapaxes(jnp.broadcast_to(layer, (cells, cells)), 0, 1)
        depth2 = depth * depth
        scaled = depth * (pixel_span * pixel_span / (total_rows * cells))
        for lane in range(0, pixels, 128):
            delta = cell_x - at_ref[0:1, lane : lane + 128]
            dx2 = jnp.broadcast_to(delta * delta, (32, 128))
            for sub in range(0, cells, 32):
                r2 = dy2_ref[sub : sub + 32, lane : lane + 128] + dx2 + depth2[sub : sub + 32, :128]
                inverse = lax.rsqrt(r2)
                value = scaled[sub : sub + 32, :128] * inverse * (inverse * inverse)
                high, low = split(value)
                at = pl.ds(pl.multiple_of(row * cells + sub, 32), 32)
                high_ref[at, lane : lane + 128] = high
                low_ref[at, lane : lane + 128] = low
        return carry

    lax.fori_loop(0, rows, one_row, 0)


def observed_kernel(total_rows, slab_ref, coords_ref, index_ref, layer_ref, head_ref, perm_ref, high_ref, low_ref, p_ref, k_ref, dy2_ref, at_ref, table_ref, sems):
    rows = layer_ref.shape[0]
    pixels = dy2_ref.shape[1]
    tall = table_ref.shape[0] // 2
    moves = []
    for row in range(rows):
        for source, target in ((head_ref, p_ref), (perm_ref, k_ref)):
            moves.append(pltpu.make_async_copy(source.at[:, row, :], target.at[row], sems.at[len(moves)]))
            moves[-1].start()
    for row in range(tall):
        for which in range(2):
            table_ref[which * tall + row : which * tall + row + 1, :] = coords_ref[
                which : which + 1, row * 128 : row * 128 + 128
            ].astype(F32)
    table = table_ref[...].astype(BF16)
    blocks = pixels // 128
    core = lax.rem(slab_ref[0], 2)
    for block in range(blocks):
        lane = block * 128
        index = index_ref[pl.ds(lax.rem(core * (blocks // 2) + block, blocks), 1), :]
        pick = (lax.broadcasted_iota(jnp.int32, (128, 128), 0) == (index & 127)).astype(BF16)
        found = dot(table, pick)
        own = lax.broadcasted_iota(jnp.int32, (tall, 128), 0) == (index >> 7)
        at_ref[0:1, lane : lane + 128] = jnp.sum(jnp.where(own, found[:tall], 0.0), 0, keepdims=True)
        at_ref[1:2, lane : lane + 128] = jnp.sum(jnp.where(own, found[tall:], 0.0), 0, keepdims=True)
    kernel_rows(total_rows, slab_ref[0], at_ref, layer_ref, high_ref, low_ref, dy2_ref)
    for one in moves:
        one.wait()


def kernel_of_observed(total_rows, slab, coords, index, layer, head, perm):
    members = head.shape[0]
    rows, cells = layer.shape
    pixels = index.size
    out = jax.ShapeDtypeStruct((rows * cells, pixels), BF16)
    state = jax.ShapeDtypeStruct((rows, members, cells), F32)
    return pl.pallas_call(
        functools.partial(observed_kernel, total_rows),
        out_shape=(out, out, state, state),
        in_specs=[SMEM, VMEM, VMEM, VMEM, HBM, HBM],
        out_specs=(VMEM,) * 4,
        scratch_shapes=[
            pltpu.VMEM((cells, pixels), F32),
            pltpu.VMEM((8, pixels), F32),
            pltpu.VMEM((coords.size // 128, 128), F32),
            pltpu.SemaphoreType.DMA((2 * rows,)),
        ],
        compiler_params=params(20),
        cost_estimate=cost(rows * cells * pixels * 16, rows * cells * pixels * 4),
        name="kernel_of_observed",
    )(slab, coords, index, layer, head, perm)


def pixel_kernel(total_rows, chips, own_rows, slab_ref, member_ref, coords_ref, layer_ref, high_ref, low_ref, dy2_ref, at_ref):
    if own_rows % 128:
        at_ref[0:2, :] = coords_ref[...]
    else:
        core = lax.rem(slab_ref[0], 2)
        lane = 0
        for own in (core, 1 - core):
            for chip in range(chips):
                first = ((member_ref[0] * chips + chip) * 2 + own) * own_rows
                for part in range(0, own_rows, 128):
                    at = pl.ds(pl.multiple_of(first + part, 128), 128)
                    at_ref[0:2, lane : lane + 128] = coords_ref[:, at].astype(F32)
                    lane += 128
    kernel_rows(total_rows, slab_ref[0], at_ref, layer_ref, high_ref, low_ref, dy2_ref)


def kernel_of_pixels(total_rows, groups, slab, member, coords, layer):
    rows, cells = layer.shape
    slabs = total_rows // rows
    chips = slabs // 2
    own_rows = coords.shape[1] // (groups * slabs)
    pixels = slabs * own_rows
    if own_rows % 128:
        coords = coords.astype(F32).reshape(2, groups, chips, 2, own_rows)
        coords = lax.dynamic_index_in_dim(coords, member[0], 1, keepdims=False)
        coords = jnp.swapaxes(coords, 1, 2)
        coords = jnp.where(slab[0] % 2 == 0, coords, coords[:, ::-1]).reshape(2, pixels)
    out = jax.ShapeDtypeStruct((rows * cells, pixels), BF16)
    return pl.pallas_call(
        functools.partial(pixel_kernel, total_rows, chips, own_rows),
        out_shape=(out, out),
        in_specs=[SMEM, SMEM, VMEM, VMEM],
        out_specs=(VMEM,) * 2,
        scratch_shapes=[pltpu.VMEM((cells, pixels), F32), pltpu.VMEM((8, pixels), F32)],
        compiler_params=params(20),
        cost_estimate=cost(rows * cells * pixels * 16, rows * cells * pixels * 4),
        name="kernel_of_pixels",
    )(slab, member, coords, layer)


def forecast_steps(slab, slabs, start_ref, perm_ref, wells_ref, near_ref, far_ref, p_ref, rim_ref):
    rows, members, cells = start_ref.shape
    even = lax.rem(slab, 2) == 0
    reach = rows + 2 * STEPS
    for k in range(STEPS):
        near = near_ref[k, 0 : 2 * members, :]
        far = far_ref[k, 0 : 2 * members, :]
        before = jnp.where(even, far, near)
        after = jnp.where(even, near, far)
        p_ref[k] = before[:members]
        rim_ref[k] = before[members:]
        p_ref[STEPS + rows + k] = after[:members]
        rim_ref[STEPS + k] = after[members:]
    last_lane = lax.broadcasted_iota(jnp.int32, (members, cells), 1) == cells - 1
    no_before = slab == 0
    no_after = slab == slabs - 1
    well_row = slice(2 * members, 2 * members + 1)

    def wells_of(i):
        if i < STEPS:
            return jnp.where(even, far_ref[i, well_row, :], near_ref[i, well_row, :])
        if i >= STEPS + rows:
            j = i - STEPS - rows
            return jnp.where(even, near_ref[j, well_row, :], far_ref[j, well_row, :])
        return wells_ref[i - STEPS : i - STEPS + 1, :]

    def head_of(step, i):
        if step == 0 and STEPS <= i < STEPS + rows:
            return start_ref[i - STEPS]
        return p_ref[i]

    def mobility_of(i, head):
        if i < STEPS:
            perm = rim_ref[i]
        elif i >= STEPS + rows:
            perm = rim_ref[i - rows]
        else:
            perm = perm_ref[i - STEPS]
        return perm * (1.0 + 0.5 * jnp.tanh(head))

    def row_flux(mobility, head, mobility_next, head_next, i):
        flux = 0.5 * (mobility_next + mobility) * (head_next - head)
        if i == STEPS - 1:
            flux = jnp.where(no_before, 0.0, flux)
        if i == STEPS + rows - 1:
            flux = jnp.where(no_after, 0.0, flux)
        return flux

    for step in range(STEPS):
        first = step + 1
        head_before = head_of(step, first - 1)
        head = head_of(step, first)
        mobility_before = mobility_of(first - 1, head_before)
        mobility = mobility_of(first, head)
        flux_before = row_flux(mobility_before, head_before, mobility, head, first - 1)
        for i in range(first, reach - first):
            head_next = head_of(step, i + 1)
            mobility_next = mobility_of(i + 1, head_next)
            flux_after = row_flux(mobility, head, mobility_next, head_next, i)
            along = 0.5 * (pltpu.roll(mobility, cells - 1, 1) + mobility) * (pltpu.roll(head, cells - 1, 1) - head)
            along = jnp.where(last_lane, 0.0, along)
            inflow = (flux_after - flux_before) + (along - pltpu.roll(along, 1, 1))
            p_ref[i] = head + time_step * (inflow + wells_of(i))
            head, mobility, flux_before = head_next, mobility_next, flux_after


def spread_product(left, padded, high_ref, low_ref, own_ref, other_ref):
    half = own_ref.shape[1]
    wide = 256 if half % 256 == 0 else 128
    for first in range(0, 2 * half, wide):
        both = dot(left, high_ref[:, first : first + wide])
        value = both[:padded] + both[padded:] + dot(left[:padded], low_ref[:, first : first + wide])
        if first < half:
            own_ref[:, first : first + wide] = value
        else:
            other_ref[:, first - half : first - half + wide] = value


def forecast_kernel(slabs, slab_ref, start_ref, perm_ref, wells_ref, near_ref, far_ref, high_ref, low_ref, cast_ref, own_ref, other_ref, p_ref, rim_ref, left_ref):
    rows, members, cells = start_ref.shape
    padded = cast_ref.shape[0]
    forecast_steps(slab_ref[0], slabs, start_ref, perm_ref, wells_ref, near_ref, far_ref, p_ref, rim_ref)
    if padded != members:
        cast_ref[...] = jnp.zeros_like(cast_ref)
        left_ref[...] = jnp.zeros_like(left_ref)
    for i in range(rows):
        value = p_ref[STEPS + i]
        high, low = split(value)
        lane = slice(i * cells, (i + 1) * cells)
        cast_ref[0:members, lane] = value
        left_ref[0:members, lane] = high
        left_ref[padded : padded + members, lane] = low
    spread_product(left_ref[...], padded, high_ref, low_ref, own_ref, other_ref)


def forecast(slabs, padded, slab, start, perm, wells, near, far, high, low):
    rows, members, cells = start.shape
    total, observed = high.shape
    half = jax.ShapeDtypeStruct((padded, observed // 2), F32)
    return pl.pallas_call(
        functools.partial(forecast_kernel, slabs),
        out_shape=(jax.ShapeDtypeStruct((padded, total), F32), half, half),
        in_specs=[SMEM] + [VMEM] * 7,
        out_specs=(VMEM,) * 3,
        scratch_shapes=[
            pltpu.VMEM((rows + 2 * STEPS, members, cells), F32),
            pltpu.VMEM((2 * STEPS, members, cells), F32),
            pltpu.VMEM((2 * padded, total), BF16),
        ],
        compiler_params=params(20),
        cost_estimate=cost(6 * padded * total * observed, 4 * total * observed),
        name="forecast",
    )(slab, start, perm, wells, near, far, high, low)


def subsidence_kernel(groups, member_ref, *refs):
    pieces = refs[:groups]
    high_ref, low_ref, own_ref, other_ref, cast_ref = refs[groups:]
    padded, total = pieces[0].shape
    every = groups * padded
    for offset in range(groups):
        at = member_ref[0] ^ offset
        high, low = split(pieces[offset][...])
        cast_ref[at] = high
        cast_ref[groups + at] = low
    left = cast_ref[...].reshape(2 * every, total)
    spread_product(left, every, high_ref, low_ref, own_ref, other_ref)


def subsidence_partial(member, pieces, high, low):
    groups = len(pieces)
    padded, total = pieces[0].shape
    pixels = high.shape[1]
    every = groups * padded
    out = jax.ShapeDtypeStruct((every, pixels // 2), F32)
    return pl.pallas_call(
        functools.partial(subsidence_kernel, groups),
        out_shape=(out, out),
        in_specs=[SMEM] + [VMEM] * (groups + 2),
        out_specs=(VMEM,) * 2,
        scratch_shapes=[pltpu.VMEM((2 * groups, padded, total), BF16)],
        compiler_params=params(24),
        cost_estimate=cost(6 * every * total * pixels, 4 * total * pixels + 4 * every * total),
        name="subsidence",
    )(member, *pieces, high, low)


def gram_kernel(groups, members, slab_ref, member_ref, *refs):
    pieces = refs[:groups]
    value_ref, sigma_ref, out_ref, seen_ref = refs[groups:]
    padded, half = pieces[0].shape
    every = groups * padded
    for offset in range(groups):
        seen_ref[member_ref[0] ^ offset] = pieces[offset][...]
    seen = seen_ref[...].reshape(every, half)
    centre = jnp.sum(seen, 0, keepdims=True) * (1.0 / (groups * members))
    anomaly = seen - centre
    if padded != members:
        here = lax.rem(lax.broadcasted_iota(jnp.int32, (every, half), 0), padded) < members
        anomaly = jnp.where(here, anomaly, 0.0)
    blocks = half // 128
    first = lax.rem(slab_ref[0], 2) * blocks
    rows_of = lambda ref: jnp.concatenate([ref[pl.ds(first + k, 1), :] for k in range(blocks)], 1)
    sigma = rows_of(sigma_ref)
    weighted = anomaly * (1.0 / (sigma * sigma))
    innovation = jnp.broadcast_to(rows_of(value_ref) - centre, (8, half))
    extra = jnp.where(lax.broadcasted_iota(jnp.int32, (8, half), 0) == 0, innovation, 0.0)
    contract = (((1,), (1,)), ((), ()))
    out_ref[...] = jnp.zeros_like(out_ref)
    out_ref[:, 0:every] = lax.dot_general(
        weighted, anomaly, contract, precision=lax.Precision.HIGHEST, preferred_element_type=F32
    )
    out_ref[:, every : every + 8] = lax.dot_general(
        weighted, extra, contract, precision=lax.Precision.HIGHEST, preferred_element_type=F32
    )


def gram_partial(members, slab, member, pieces, value, sigma):
    groups = len(pieces)
    padded, half = pieces[0].shape
    every = groups * padded
    width = -(-(every + 8) // 128) * 128
    return pl.pallas_call(
        functools.partial(gram_kernel, groups, members),
        out_shape=jax.ShapeDtypeStruct((every, width), F32),
        in_specs=[SMEM, SMEM] + [VMEM] * (groups + 2),
        out_specs=VMEM,
        scratch_shapes=[pltpu.VMEM((groups, padded, half), F32)],
        compiler_params=params(),
        cost_estimate=cost(12 * every * every * half, 4 * every * half),
        name="gram",
    )(slab, member, *pieces, value, sigma)


def eliminate_panel(rows, scaled, first, count):
    groups = count // 8
    tiles = rows.shape[1] // 128
    sub_row = lax.broadcasted_iota(jnp.int32, (8, 128), 0)
    lane = lax.broadcasted_iota(jnp.int32, (8, 128), 1)
    x = [[rows[8 * g : 8 * g + 8, 128 * t : 128 * t + 128] for t in range(tiles)] for g in range(groups)]
    full = lambda v: jnp.broadcast_to(v, (8, 128))
    scale = [None] * groups
    for s in range(groups):
        column = first + 8 * s
        tile, at = column // 128, column % 128
        c = [[full(x[g][tile][:, at + j : at + j + 1]) for g in range(s, groups)] for j in range(8)]
        scale[s] = jnp.zeros((8, 128), F32)
        for j in range(8):
            pivot = full(c[j][0][j : j + 1, :])
            inverse = pltpu.reciprocal(pivot, approx=False)
            below = sub_row > j
            m = [v * inverse for v in c[j]]
            m[0] = jnp.where(below, m[0], 0.0)
            root = lax.rsqrt(pivot)
            root = root * (1.5 - 0.5 * pivot * root * root)
            scale[s] = jnp.where(sub_row == j, root, scale[s])
            for l in range(j + 1, 8):
                entry = full(c[l][0][j : j + 1, :])
                c[l] = [v - k * entry for v, k in zip(c[l], m)]
            here = lane == at + j
            for t in range(tiles):
                row = full(x[s][t][j : j + 1, :])
                if t == tile:
                    row = jnp.where(here, 1.0, row)
                for g in range(s, groups):
                    old = x[g][t]
                    if t == tile:
                        old = jnp.where(here & below if g == s else here, 0.0, old)
                    x[g][t] = old - m[g - s] * row
    for g in range(groups):
        for t in range(tiles):
            value = x[g][t]
            column = lane + 128 * t
            row = first + 8 * g + sub_row
            inside = column < first + count
            value = jnp.where(inside & (column == row), 1.0, jnp.where(inside & (column > row), 0.0, value))
            scaled[first + 8 * g : first + 8 * g + 8, 128 * t : 128 * t + 128] = value * scale[g]


def invert(work_ref):
    every, width = work_ref.shape
    panel = 32
    for first in range(0, every, panel):
        eliminate_panel(work_ref[first : first + panel, :], work_ref, first, panel)
        below = first + panel
        if below < every:
            done = work_ref[first:below, :]
            product = lax.dot_general(
                done[:, below:every] if below % 128 == 0 else done[:, below // 128 * 128 : every],
                done,
                (((0,), (0,)), ((), ())),
                precision=lax.Precision.HIGHEST,
                preferred_element_type=F32,
            )
            column = lax.broadcasted_iota(jnp.int32, (every - below, width), 1)
            own = (column >= first) & (column < below)
            old = jnp.where(own, 0.0, work_ref[below:every, :])
            work_ref[below:every, :] = old - product[below - below // 128 * 128 :]


def finish_kernel(groups, members, member_ref, gram_ref, more_ref, *refs):
    pieces = refs[:groups]
    out_ref, cast_ref, work_ref = refs[groups:]
    padded, total = pieces[0].shape
    rows, cells = out_ref.shape[1:]
    every, width = work_ref.shape
    count = groups * members
    member = member_ref[0]
    for offset in range(groups):
        at = member ^ offset
        high, low = split(pieces[offset][...])
        cast_ref[at] = high
        cast_ref[groups + at] = low
    row = lax.broadcasted_iota(jnp.int32, (every, width), 0)
    column = lax.broadcasted_iota(jnp.int32, (every, width), 1)
    work_ref[...] = gram_ref[...] + more_ref[...] + jnp.where(row == column, count - 1.0, 0.0)
    invert(work_ref)

    solved = jnp.broadcast_to(work_ref[:, every : every + 1], (every, width))
    inverse = jnp.where(column <= row, work_ref[...], 0.0)
    weights = jnp.sum(inverse * solved, 0, keepdims=True)
    first = pl.multiple_of(member * padded, padded)
    column = lax.broadcasted_iota(jnp.int32, (padded, width), 1)
    row = lax.broadcasted_iota(jnp.int32, (padded, width), 0) + first
    own = jnp.where(column <= row, work_ref[pl.ds(first, padded), :], 0.0)
    here = column < every
    if padded != members:
        here = here & (lax.rem(column, padded) < members)
    mix = jnp.where(here, weights + math.sqrt(count - 1.0) * own, 0.0)
    mix = mix + (1.0 - jnp.sum(mix, 1, keepdims=True)) * (1.0 / count)
    mix = jnp.where(here, mix, 0.0)[:, :every]

    mix_high, mix_low = split(mix)
    mix_both = jnp.concatenate([mix_high, mix_low], 0)
    depth = 4 * cells if rows % 4 == 0 else cells
    for lane in range(0, total, depth):
        high = cast_ref[0:groups, :, lane : lane + depth].reshape(every, depth)
        low = cast_ref[groups:, :, lane : lane + depth].reshape(every, depth)
        both = dot(mix_both, high)
        value = both[:padded] + both[padded:] + dot(mix_high, low)
        for part in range(depth // cells):
            out_ref[:, lane // cells + part, :] = value[:members, part * cells : (part + 1) * cells]


def finish(members, rows, cells, member, gram, more, pieces):
    groups = len(pieces)
    padded, total = pieces[0].shape
    return pl.pallas_call(
        functools.partial(finish_kernel, groups, members),
        out_shape=jax.ShapeDtypeStruct((members, rows, cells), F32),
        in_specs=[SMEM] + [VMEM] * (groups + 2),
        out_specs=VMEM,
        scratch_shapes=[pltpu.VMEM((2 * groups, padded, total), BF16), pltpu.VMEM(gram.shape, F32)],
        compiler_params=params(),
        cost_estimate=cost(6 * padded * groups * padded * total, 4 * groups * padded * total),
        name="finish",
    )(member, gram, more, *pieces)


def cycle(head, perm, wells, layer, coords, obs_index, obs_value, obs_sigma):
    members, rows, cells = head.shape
    groups = lax.axis_size("member")
    slabs = lax.axis_size("slab")
    slab = lax.axis_index("slab")
    member = lax.axis_index("member")
    total_rows = rows * slabs
    padded = -(-members // 16) * 16
    slab_s = slab.astype(jnp.int32).reshape(1)
    member_s = member.astype(jnp.int32).reshape(1)
    pair = [(i, i ^ 1) for i in range(slabs)]
    across = [(i, i + 1) for i in range(1, slabs - 1, 2)] + [(i + 1, i) for i in range(1, slabs - 1, 2)]

    def swap(value, axis, offset):
        size = lax.axis_size(axis)
        return lax.ppermute(value, axis, [(i, i ^ offset) for i in range(size)])

    smalls = (wells, layer, coords, *(a.reshape(-1, 128) for a in (obs_index, obs_value, obs_sigma)))
    head, perm, wells, *smalls = (
        pltpu.with_memory_space_constraint(a, pltpu.HBM) for a in (head, perm, wells, *smalls)
    )
    near, far, wells, layer, coords, index, value, sigma = pack(slab_s, head, perm, wells, smalls)
    far = lax.ppermute(far, "slab", across)
    near = lax.ppermute(near, "slab", pair)

    high, low, start, perm_rows = kernel_of_observed(total_rows, slab_s, coords, index, layer, head, perm)
    cast, own, other = forecast(slabs, padded, slab_s, start, perm_rows, wells, near, far, high, low)
    seen = own + swap(other, "slab", 1)
    pieces = [cast] + [swap(cast, "member", offset) for offset in range(1, groups)]
    offset = 2
    while offset < slabs:
        seen = seen + swap(seen, "slab", offset)
        offset *= 2
    views = [seen] + [swap(seen, "member", offset) for offset in range(1, groups)]
    gram = gram_partial(members, slab_s, member_s, views, value, sigma)
    gram_more = swap(gram, "slab", 1)

    chips = slabs // 2
    own_rows = coords.shape[1] // (groups * slabs)
    pixel_high, pixel_low = kernel_of_pixels(total_rows, groups, slab_s, member_s, coords, layer)
    sunk, sunk_other = subsidence_partial(member_s, pieces, pixel_high, pixel_low)
    sunk_recv = swap(sunk_other, "slab", 1)
    chip = slab // 2

    def block(which):
        first = which * own_rows
        return lax.dynamic_slice_in_dim(sunk, first, own_rows, 1) + lax.dynamic_slice_in_dim(
            sunk_recv, first, own_rows, 1
        )

    sunk_own = block(chip)
    for offset in range(1, chips):
        sunk_own = sunk_own + swap(block(chip ^ offset), "slab", 2 * offset)
    if padded != members:
        sunk_own = sunk_own.reshape(groups, padded, own_rows)[:, :members].reshape(groups * members, own_rows)
    subsidence = sunk_own.T

    analysed = finish(members, rows, cells, member_s, gram, gram_more, pieces)
    return (analysed, subsidence)


def solution(mesh):
    return jax.shard_map(
        cycle,
        mesh=mesh,
        in_specs=(
            P("member", "slab", None),
            P("member", "slab", None),
            P("slab", None),
            P("slab", None),
            P(),
            P(),
            P(),
            P(),
        ),
        out_specs=(P("member", "slab", None), P(("member", "slab"), None)),
        check_vma=False,
    )
```

time: 76.6 us -> 76.2 us (level)
  waiting for transfers between devices: 11.2 us -> 21.7 us
  local copies, waits for them, and re-layouts: 6.95 us -> 0 us
  Pallas kernels: 32.3 us -> 27.8 us
  starting transfers between devices: 22.4 us -> 24.8 us
  other arithmetic: 2.3 us -> 0.82 us
    ppermute x14, waiting for transfers between devices: 11.2 us -> 21.7 us  [swap(): return lax.ppermute(value, axis, [(i, i ^ offset) for i in range(size)])]
    unnamed x20 -> x0, local copies, waits for them, and re-layouts: 6.07 us -> none
    pallas_call x5, Pallas kernels: 23.2 us -> 18.7 us  [the longest x1 5.91 us: kernel_of_observed(): pl.pallas_call(functools.partial(observed_kernel, total_rows), out_shape=...]
    ppermute x14, starting transfers between devices: 21.2 us -> 23.6 us  [swap(): return lax.ppermute(value, axis, [(i, i ^ offset) for i in range(size)])]
    slice x5 -> x0, local copies, waits for them, and re-layouts: 0.78 us -> none  [the longest x3 0.77 us: own_first(): return jnp.where(core == 0, row, jnp.roll(row, half)).reshape(1, observed)]
    convert_element_type x1 -> x0, other arithmetic: 0.77 us -> none  [shards(): table = coords.astype(F32).reshape(2 * pixel_total // 128, 128)]
  transfers between devices with their start and end apart: 16 -> 16, of which waited for: 6 -> 7; matrix products, arithmetic and copies ran while one was open for 3% -> 0% of each run, Pallas kernels for 31% -> 31%
where the time goes in v3:
time: 76.2 us; the launch traced here: 75.9 us
  Pallas kernels  27.8 us (36%)
  starting transfers between devices  24.8 us (33%)
  waiting for transfers between devices  21.7 us (28%)
  other arithmetic  0.82 us (1%)
    ppermute x14, starting transfers between devices, swap(): return lax.ppermute(value, axis, [(i, i ^ offset) for i in range(size)])  23.6 us
    ppermute x14, waiting for transfers between devices, swap(): return lax.ppermute(value, axis, [(i, i ^ offset) for i in range(size)])  21.7 us
    pallas_call x1, Pallas kernels, finish(): pl.pallas_call(functools.partial(finish_kernel, groups, members), out_sha...  8.26 us
    pallas_call x1, Pallas kernels, kernel_of_observed(): pl.pallas_call(functools.partial(observed_kernel, total_rows), out_shape=...  5.91 us
    pallas_call x1, Pallas kernels, kernel_of_pixels(): pl.pallas_call(functools.partial(pixel_kernel, total_rows, chips, own_row...  5.32 us
    pallas_call x1, Pallas kernels, forecast(): pl.pallas_call(functools.partial(forecast_kernel, slabs), out_shape=(jax....  3.12 us
    pallas_call x1, Pallas kernels, subsidence_partial(): pl.pallas_call(functools.partial(subsidence_kernel, groups), out_shape=(o...  3.01 us
  transfers between devices with their start and end apart: 16, of which 7 were waited for; matrix products, arithmetic and copies ran while one was open for 0% of the time, Pallas kernels for 31%

profile of v3, /device:TPU:0, one launch (start us, length us, event | category | flops | bytes accessed | tf_op | source)
XLA Modules:
  0.0 75.9 jit_solution(3158045702553005916)
XLA Ops:
  0.6 1.3 %pack_rims.1 = (f32[4,104,128]{2,1,0:T(8,128)S(1)}, f32[4,104,128]{2,1,0:T(8,128)S(1)}, f32[16,128]{1,0:T(8,128)S(1)}, s32[16,128]{1,0:T(8,128)S(1)}, s32[2,4096...) custom-call(s32[1]{0:T(128)} %bitcast.1.slab_ref, f32[48,16,128]{2,1,0:T(8,128)} %head_ref.3, ...), custom_call_target="tpu_custom_call" | custom-call | tf_op jit(solution)/shard_map/pack_rims/pallas_call | solution.py:75
  2.0 0.6 collective-permute-start
  2.5 0.7 collective-permute-start.1
  3.2 5.9 %kernel_of_observed.1 = (bf16[2048,1024]{1,0:T(8,128)(2,1)S(1)}, bf16[2048,1024]{1,0:T(8,128)(2,1)S(1)}, f32[16,48,128]{2,1,0:T(8,128)S(1)}, f32[16,48,128]{2,1,0:T(8,128)S(1)}) custom-call(s32[1]{0:T(128)} %bitcast.1.slab_ref, s32[2,4096]{1,0:T(2,128)S(1)} %get-tuple-element.21.coords_ref, s32[8,128]{1,0:T(8,128)S(1)} %get-tuple-element.22.index_ref, ...), custom_call_target="tpu_custom_call" | custom-call | flops 33554432 | bytes 8388608 | tf_op jit(solution)/shard_map/kernel_of_observed/pallas_call | solution.py:153
  9.1 0.0 collective-permute-done.near_ref
  9.1 0.0 collective-permute-done.1.far_ref
  9.1 3.1 %forecast.1 = (f32[48,2048]{1,0:T(8,128)S(1)}, f32[48,512]{1,0:T(8,128)S(1)}, f32[48,512]{1,0:T(8,128)S(1)}) custom-call(s32[1]{0:T(128)} %bitcast.1.slab_ref, f32[16,48,128]{2,1,0:T(8,128)S(1)} %get-tuple-element.24.start_ref, f32[16,48,128]{2,1,0:T(8,128)S(1)} %get-tuple-element.25.perm_ref, f32[16,128]{1,0:T(8,128)S(1)} %get-tuple-element.26.wells_ref, ...), custom_call_target="tpu_custom_call" | custom-call | flops 603979776 | bytes 8388608 | tf_op jit(solution)/shard_map/forecast/pallas_call | solution.py:309
  12.2 2.6 %collective-permute-start.10 = (f32[48,2048]{1,0:T(8,128)S(1)}, f32[48,2048]{1,0:T(8,128)S(1)}, u32[]{:S(2)}, u32[]{:S(2)}) collective-permute-start(f32[48,2048]{1,0:T(8,128)S(1)} %get-tuple-element.35.refs_0_), channel_id=1, source_target_pairs={{0,16},{8,24},{16,0},{24,8},{1,17},{9,25},{17,1},{25,9},{2,18},{10... | collective-permute-start | bytes 1179656 | tf_op jit(solution)/shard_map/ppermute | solution.py:544
  14.8 1.4 %collective-permute-start.11 = (f32[48,2048]{1,0:T(8,128)S(1)}, f32[48,2048]{1,0:T(8,128)S(1)}, u32[]{:S(2)}, u32[]{:S(2)}) collective-permute-start(f32[48,2048]{1,0:T(8,128)S(1)} %get-tuple-element.35.refs_0_), channel_id=1, source_target_pairs={{0,24},{8,16},{16,8},{24,0},{1,25},{9,17},{17,9},{25,1},{2,26},{10... | collective-permute-start | bytes 1179656 | tf_op jit(solution)/shard_map/ppermute | solution.py:544
  16.3 0.1 collective-permute-start.9
  16.4 5.3 %kernel_of_pixels.1 = (bf16[2048,1024]{1,0:T(8,128)(2,1)S(1)}, bf16[2048,1024]{1,0:T(8,128)(2,1)S(1)}) custom-call(s32[1]{0:T(128)} %bitcast.1.slab_ref, s32[1]{0:T(128)} %bitcast.member_ref, s32[2,4096]{1,0:T(2,128)S(1)} %get-tuple-element.21.coords_ref, s32[16,128]{1,0:T(8,128)S(1)} %get-tuple-element.23.layer_ref), custom_call_target="tpu_custom_call" | custom-call | flops 33554432 | bytes 8388608 | tf_op jit(solution)/shard_map/kernel_of_pixels/pallas_call | solution.py:198
  21.7 2.6 %collective-permute-start.2 = (f32[48,512]{1,0:T(8,128)S(1)}, f32[48,512]{1,0:T(8,128)S(1)}, u32[]{:S(2)}, u32[]{:S(2)}) collective-permute-start(f32[48,512]{1,0:T(8,128)S(1)} %get-tuple-element.32), channel_id=1, source_target_pairs={{0,1},{1,0},{2,3},{3,2},{4,5},{5,4},{6,7},{7,6},{8,9},{9,8},{10,11... | collective-permute-start | bytes 294920 | tf_op jit(solution)/shard_map/ppermute | solution.py:544
  24.3 7.4 %collective-permute-done.10.refs_2_ = f32[48,2048]{1,0:T(8,128)S(1)} collective-permute-done((f32[48,2048]{1,0:T(8,128)S(1)}, f32[48,2048]{1,0:T(8,128)S(1)}, u32[]{:S(2)}, u32[]{:S(2)}) %collective-permute-start.10) | collective-permute-done | bytes 393248 | tf_op jit(solution)/shard_map/ppermute | solution.py:544
  31.7 0.0 collective-permute-done.11.refs_3_
  31.7 1.1 %collective-permute-done.9.refs_1_ = f32[48,2048]{1,0:T(8,128)S(1)} collective-permute-done((f32[48,2048]{1,0:T(8,128)S(1)}, f32[48,2048]{1,0:T(8,128)S(1)}, u32[]{:S(2)}, u32[]{:S(2)}) %collective-permute-start.9) | collective-permute-done | bytes 393248 | tf_op jit(solution)/shard_map/ppermute | solution.py:544
  32.8 3.0 %subsidence.1 = (f32[192,512]{1,0:T(8,128)S(1)}, f32[192,512]{1,0:T(8,128)S(1)}) custom-call(s32[1]{0:T(128)} %bitcast.member_ref, f32[48,2048]{1,0:T(8,128)S(1)} %get-tuple-element.35.refs_0_, f32[48,2048]{1,0:T(8,128)S(1)} %collective-permute-done.9.refs_1_, f32[48,2048]{1,0:T(8,128)S(1)} %collective-permute-done.10.refs_2_, ...), custom_call_target="tpu_custom_call" | custom-call | flops 2415919104 | bytes 9961472 | tf_op jit(solution)/shard_map/subsidence/pallas_call | solution.py:345
  35.8 1.9 %collective-permute-start.12 = (f32[192,512]{1,0:T(8,128)S(1)}, f32[192,512]{1,0:T(8,128)S(1)}, u32[]{:S(2)}, u32[]{:S(2)}) collective-permute-start(f32[192,512]{1,0:T(8,128)S(1)} %get-tuple-element.39), channel_id=1, source_target_pairs={{0,1},{1,0},{2,3},{3,2},{4,5},{5,4},{6,7},{7,6},{8,9},{9,8},{10,11... | collective-permute-start | bytes 1179656 | tf_op jit(solution)/shard_map/ppermute | solution.py:544
  37.7 0.0 collective-permute-done.2
  37.8 3.4 %collective-permute-start.3 = (f32[48,512]{1,0:T(8,128)S(1)}, f32[48,512]{1,0:T(8,128)S(1)}, u32[]{:S(2)}, u32[]{:S(2)}) collective-permute-start(f32[48,512]{1,0:T(8,128)S(1)} %add.47), channel_id=1, source_target_pairs={{0,2},{1,3},{2,0},{3,1},{4,6},{5,7},{6,4},{7,5},{8,10},{9,11},{10,... | collective-permute-start | bytes 294920 | tf_op jit(solution)/shard_map/ppermute | solution.py:544
  41.2 3.3 %collective-permute-done.3 = f32[48,512]{1,0:T(8,128)S(1)} collective-permute-done((f32[48,512]{1,0:T(8,128)S(1)}, f32[48,512]{1,0:T(8,128)S(1)}, u32[]{:S(2)}, u32[]{:S(2)}) %collective-permute-start.3) | collective-permute-done | bytes 98336 | tf_op jit(solution)/shard_map/ppermute | solution.py:544
  44.5 3.5 %collective-permute-start.4 = (f32[48,512]{1,0:T(8,128)S(1)}, f32[48,512]{1,0:T(8,128)S(1)}, u32[]{:S(2)}, u32[]{:S(2)}) collective-permute-start(f32[48,512]{1,0:T(8,128)S(1)} %add.48), channel_id=1, source_target_pairs={{0,4},{1,5},{2,6},{3,7},{4,0},{5,1},{6,2},{7,3},{8,12},{9,13},{10,... | collective-permute-start | bytes 294920 | tf_op jit(solution)/shard_map/ppermute | solution.py:544
  48.0 4.7 %collective-permute-done.4 = f32[48,512]{1,0:T(8,128)S(1)} collective-permute-done((f32[48,512]{1,0:T(8,128)S(1)}, f32[48,512]{1,0:T(8,128)S(1)}, u32[]{:S(2)}, u32[]{:S(2)}) %collective-permute-start.4) | collective-permute-done | bytes 98336 | tf_op jit(solution)/shard_map/ppermute | solution.py:544
  52.7 1.7 %collective-permute-start.5 = (f32[48,512]{1,0:T(8,128)S(1)}, f32[48,512]{1,0:T(8,128)S(1)}, u32[]{:S(2)}, u32[]{:S(2)}) collective-permute-start(f32[48,512]{1,0:T(8,128)S(1)} %add.49.refs_0_), channel_id=1, source_target_pairs={{0,8},{8,0},{16,24},{24,16},{1,9},{9,1},{17,25},{25,17},{2,10},{10... | collective-permute-start | bytes 294920 | tf_op jit(solution)/shard_map/ppermute | solution.py:544
  54.4 1.5 %collective-permute-start.6 = (f32[48,512]{1,0:T(8,128)S(1)}, f32[48,512]{1,0:T(8,128)S(1)}, u32[]{:S(2)}, u32[]{:S(2)}) collective-permute-start(f32[48,512]{1,0:T(8,128)S(1)} %add.49.refs_0_), channel_id=1, source_target_pairs={{0,16},{8,24},{16,0},{24,8},{1,17},{9,25},{17,1},{25,9},{2,18},{10... | collective-permute-start | bytes 294920 | tf_op jit(solution)/shard_map/ppermute | solution.py:544
  55.9 0.3 collective-permute-start.7
  56.2 2.2 %collective-permute-done.5.refs_1_ = f32[48,512]{1,0:T(8,128)S(1)} collective-permute-done((f32[48,512]{1,0:T(8,128)S(1)}, f32[48,512]{1,0:T(8,128)S(1)}, u32[]{:S(2)}, u32[]{:S(2)}) %collective-permute-start.5) | collective-permute-done | bytes 98336 | tf_op jit(solution)/shard_map/ppermute | solution.py:544
  58.4 0.9 %collective-permute-done.6.refs_2_ = f32[48,512]{1,0:T(8,128)S(1)} collective-permute-done((f32[48,512]{1,0:T(8,128)S(1)}, f32[48,512]{1,0:T(8,128)S(1)}, u32[]{:S(2)}, u32[]{:S(2)}) %collective-permute-start.6) | collective-permute-done | bytes 98336 | tf_op jit(solution)/shard_map/ppermute | solution.py:544
  59.3 2.1 %collective-permute-done.7.refs_3_ = f32[48,512]{1,0:T(8,128)S(1)} collective-permute-done((f32[48,512]{1,0:T(8,128)S(1)}, f32[48,512]{1,0:T(8,128)S(1)}, u32[]{:S(2)}, u32[]{:S(2)}) %collective-permute-start.7) | collective-permute-done | bytes 98336 | tf_op jit(solution)/shard_map/ppermute | solution.py:544
  61.5 0.9 %gram.1.gram_ref = f32[192,256]{1,0:T(8,128)S(1)} custom-call(s32[1]{0:T(128)} %bitcast.1.slab_ref, s32[1]{0:T(128)} %bitcast.member_ref, f32[48,512]{1,0:T(8,128)S(1)} %add.49.refs_0_, f32[48,512]{1,0:T(8,128)S(1)} %collective-permute-done.5.refs_1_, f32[48,512]{1,0:T(8,128)S(1)} %collective-permute-done.6.refs_2_, ...), custom_call_target="tpu_custom_call" | custom-call | flops 226492416 | bytes 393216 | tf_op jit(solution)/shard_map/gram/pallas_call | solution.py:392
  62.3 0.1 collective-permute-start.8
  62.4 0.0 collective-permute-done.12
  62.4 0.1 dynamic-slice_add_fusion.2
  62.5 0.1 collective-permute-start.13
  62.6 3.0 %collective-permute-start.14 = (f32[192,128]{1,0:T(8,128)S(1)}, f32[192,128]{1,0:T(8,128)S(1)}, u32[]{:S(2)}, u32[]{:S(2)}) collective-permute-start(f32[192,128]{1,0:T(8,128)S(1)} %get-tuple-element.42), channel_id=1, source_target_pairs={{0,4},{1,5},{2,6},{3,7},{4,0},{5,1},{6,2},{7,3},{8,12},{9,13},{10,... | collective-permute-start | bytes 294920 | tf_op jit(solution)/shard_map/ppermute | solution.py:544
  65.6 1.3 %collective-permute-start.15 = (f32[192,128]{1,0:T(8,128)S(1)}, f32[192,128]{1,0:T(8,128)S(1)}, u32[]{:S(2)}, u32[]{:S(2)}) collective-permute-start(f32[192,128]{1,0:T(8,128)S(1)} %get-tuple-element.41), channel_id=1, source_target_pairs={{0,6},{1,7},{2,4},{3,5},{4,2},{5,3},{6,0},{7,1},{8,14},{9,15},{10,... | collective-permute-start | bytes 294920 | tf_op jit(solution)/shard_map/ppermute | solution.py:544
  67.0 0.0 collective-permute-done.8.more_ref
  67.0 8.3 %finish.1 = f32[48,16,128]{2,1,0:T(8,128)} custom-call(s32[1]{0:T(128)} %bitcast.member_ref, f32[192,256]{1,0:T(8,128)S(1)} %gram.1.gram_ref, f32[192,256]{1,0:T(8,128)S(1)} %collective-permute-done.8.more_ref, f32[48,2048]{1,0:T(8,128)S(1)} %get-tuple-element.35.refs_0_, f32[48,2048]{1,0:T(8,128)S(1)} %collective-permute-done.9.refs_1_, ...), custom_call_target="tpu_custom_call" | custom-call | flops 113246208 | bytes 1572864 | tf_op jit(solution)/shard_map/finish/pallas_call | solution.py:517
  75.2 0.0 collective-permute-done.13
  75.2 0.0 collective-permute-done.14
  75.2 0.0 collective-permute-done.15
  75.3 0.7 add_bitcast_fusion
  (3 shorter events, 0.0 us)
Async XLA Ops:
  2.0 7.1 %collective-permute-start = (f32[4,104,128]{2,1,0:T(8,128)S(1)}, f32[4,104,128]{2,1,0:T(8,128)S(1)}, u32[]{:S(2)}, u32[]{:S(2)}) collective-permute-start(f32[4,104,128]{2,1,0:T(8,128)S(1)} %get-tuple-element.27), channel_id=1, source_target_pairs={{0,1},{1,0},{2,3},{3,2},{4,5},{5,4},{6,7},{7,6},{8,9},{9,8},{10,11... | collective-permute-start | bytes 638984 | tf_op jit(solution)/shard_map/ppermute | solution.py:552
  2.5 6.6 %collective-permute-start.1 = (f32[4,104,128]{2,1,0:T(8,128)S(1)}, f32[4,104,128]{2,1,0:T(8,128)S(1)}, u32[]{:S(2)}, u32[]{:S(2)}) collective-permute-start(f32[4,104,128]{2,1,0:T(8,128)S(1)} %get-tuple-element.28), channel_id=1, source_target_pairs={{1,2},{3,4},{5,6},{2,1},{4,3},{6,5},{9,10},{11,12},{13,14},{10,9},... | collective-permute-start | bytes 638984 | tf_op jit(solution)/shard_map/ppermute | solution.py:551
  12.2 19.5 %collective-permute-start.10 = (f32[48,2048]{1,0:T(8,128)S(1)}, f32[48,2048]{1,0:T(8,128)S(1)}, u32[]{:S(2)}, u32[]{:S(2)}) collective-permute-start(f32[48,2048]{1,0:T(8,128)S(1)} %get-tuple-element.35.refs_0_), channel_id=1, source_target_pairs={{0,16},{8,24},{16,0},{24,8},{1,17},{9,25},{17,1},{25,9},{2,18},{10... | collective-permute-start | bytes 1179656 | tf_op jit(solution)/shard_map/ppermute | solution.py:544
  14.8 16.9 %collective-permute-start.11 = (f32[48,2048]{1,0:T(8,128)S(1)}, f32[48,2048]{1,0:T(8,128)S(1)}, u32[]{:S(2)}, u32[]{:S(2)}) collective-permute-start(f32[48,2048]{1,0:T(8,128)S(1)} %get-tuple-element.35.refs_0_), channel_id=1, source_target_pairs={{0,24},{8,16},{16,8},{24,0},{1,25},{9,17},{17,9},{25,1},{2,26},{10... | collective-permute-start | bytes 1179656 | tf_op jit(solution)/shard_map/ppermute | solution.py:544
  16.3 16.5 %collective-permute-start.9 = (f32[48,2048]{1,0:T(8,128)S(1)}, f32[48,2048]{1,0:T(8,128)S(1)}, u32[]{:S(2)}, u32[]{:S(2)}) collective-permute-start(f32[48,2048]{1,0:T(8,128)S(1)} %get-tuple-element.35.refs_0_), channel_id=1, source_target_pairs={{0,8},{8,0},{16,24},{24,16},{1,9},{9,1},{17,25},{25,17},{2,10},{10... | collective-permute-start | bytes 1179656 | tf_op jit(solution)/shard_map/ppermute | solution.py:544
  21.7 16.0 %collective-permute-start.2 = (f32[48,512]{1,0:T(8,128)S(1)}, f32[48,512]{1,0:T(8,128)S(1)}, u32[]{:S(2)}, u32[]{:S(2)}) collective-permute-start(f32[48,512]{1,0:T(8,128)S(1)} %get-tuple-element.32), channel_id=1, source_target_pairs={{0,1},{1,0},{2,3},{3,2},{4,5},{5,4},{6,7},{7,6},{8,9},{9,8},{10,11... | collective-permute-start | bytes 294920 | tf_op jit(solution)/shard_map/ppermute | solution.py:544
  35.8 26.6 %collective-permute-start.12 = (f32[192,512]{1,0:T(8,128)S(1)}, f32[192,512]{1,0:T(8,128)S(1)}, u32[]{:S(2)}, u32[]{:S(2)}) collective-permute-start(f32[192,512]{1,0:T(8,128)S(1)} %get-tuple-element.39), channel_id=1, source_target_pairs={{0,1},{1,0},{2,3},{3,2},{4,5},{5,4},{6,7},{7,6},{8,9},{9,8},{10,11... | collective-permute-start | bytes 1179656 | tf_op jit(solution)/shard_map/ppermute | solution.py:544
  37.8 6.7 %collective-permute-start.3 = (f32[48,512]{1,0:T(8,128)S(1)}, f32[48,512]{1,0:T(8,128)S(1)}, u32[]{:S(2)}, u32[]{:S(2)}) collective-permute-start(f32[48,512]{1,0:T(8,128)S(1)} %add.47), channel_id=1, source_target_pairs={{0,2},{1,3},{2,0},{3,1},{4,6},{5,7},{6,4},{7,5},{8,10},{9,11},{10,... | collective-permute-start | bytes 294920 | tf_op jit(solution)/shard_map/ppermute | solution.py:544
  44.5 8.2 %collective-permute-start.4 = (f32[48,512]{1,0:T(8,128)S(1)}, f32[48,512]{1,0:T(8,128)S(1)}, u32[]{:S(2)}, u32[]{:S(2)}) collective-permute-start(f32[48,512]{1,0:T(8,128)S(1)} %add.48), channel_id=1, source_target_pairs={{0,4},{1,5},{2,6},{3,7},{4,0},{5,1},{6,2},{7,3},{8,12},{9,13},{10,... | collective-permute-start | bytes 294920 | tf_op jit(solution)/shard_map/ppermute | solution.py:544
  52.7 5.7 %collective-permute-start.5 = (f32[48,512]{1,0:T(8,128)S(1)}, f32[48,512]{1,0:T(8,128)S(1)}, u32[]{:S(2)}, u32[]{:S(2)}) collective-permute-start(f32[48,512]{1,0:T(8,128)S(1)} %add.49.refs_0_), channel_id=1, source_target_pairs={{0,8},{8,0},{16,24},{24,16},{1,9},{9,1},{17,25},{25,17},{2,10},{10... | collective-permute-start | bytes 294920 | tf_op jit(solution)/shard_map/ppermute | solution.py:544
  54.4 4.9 %collective-permute-start.6 = (f32[48,512]{1,0:T(8,128)S(1)}, f32[48,512]{1,0:T(8,128)S(1)}, u32[]{:S(2)}, u32[]{:S(2)}) collective-permute-start(f32[48,512]{1,0:T(8,128)S(1)} %add.49.refs_0_), channel_id=1, source_target_pairs={{0,16},{8,24},{16,0},{24,8},{1,17},{9,25},{17,1},{25,9},{2,18},{10... | collective-permute-start | bytes 294920 | tf_op jit(solution)/shard_map/ppermute | solution.py:544
  55.9 5.5 %collective-permute-start.7 = (f32[48,512]{1,0:T(8,128)S(1)}, f32[48,512]{1,0:T(8,128)S(1)}, u32[]{:S(2)}, u32[]{:S(2)}) collective-permute-start(f32[48,512]{1,0:T(8,128)S(1)} %add.49.refs_0_), channel_id=1, source_target_pairs={{0,24},{8,16},{16,8},{24,0},{1,25},{9,17},{17,9},{25,1},{2,26},{10... | collective-permute-start | bytes 294920 | tf_op jit(solution)/shard_map/ppermute | solution.py:544
  62.3 4.6 %collective-permute-start.8 = (f32[192,256]{1,0:T(8,128)S(1)}, f32[192,256]{1,0:T(8,128)S(1)}, u32[]{:S(2)}, u32[]{:S(2)}) collective-permute-start(f32[192,256]{1,0:T(8,128)S(1)} %gram.1.gram_ref), channel_id=1, source_target_pairs={{0,1},{1,0},{2,3},{3,2},{4,5},{5,4},{6,7},{7,6},{8,9},{9,8},{10,11... | collective-permute-start | bytes 589832 | tf_op jit(solution)/shard_map/ppermute | solution.py:544
  62.5 12.7 %collective-permute-start.13 = (f32[192,128]{1,0:T(8,128)S(1)}, f32[192,128]{1,0:T(8,128)S(1)}, u32[]{:S(2)}, u32[]{:S(2)}) collective-permute-start(f32[192,128]{1,0:T(8,128)S(1)} %get-tuple-element.40), channel_id=1, source_target_pairs={{0,2},{1,3},{2,0},{3,1},{4,6},{5,7},{6,4},{7,5},{8,10},{9,11},{10,... | collective-permute-start | bytes 294920 | tf_op jit(solution)/shard_map/ppermute | solution.py:544
  62.6 12.6 %collective-permute-start.14 = (f32[192,128]{1,0:T(8,128)S(1)}, f32[192,128]{1,0:T(8,128)S(1)}, u32[]{:S(2)}, u32[]{:S(2)}) collective-permute-start(f32[192,128]{1,0:T(8,128)S(1)} %get-tuple-element.42), channel_id=1, source_target_pairs={{0,4},{1,5},{2,6},{3,7},{4,0},{5,1},{6,2},{7,3},{8,12},{9,13},{10,... | collective-permute-start | bytes 294920 | tf_op jit(solution)/shard_map/ppermute | solution.py:544
  65.6 9.6 %collective-permute-start.15 = (f32[192,128]{1,0:T(8,128)S(1)}, f32[192,128]{1,0:T(8,128)S(1)}, u32[]{:S(2)}, u32[]{:S(2)}) collective-permute-start(f32[192,128]{1,0:T(8,128)S(1)} %get-tuple-element.41), channel_id=1, source_target_pairs={{0,6},{1,7},{2,4},{3,5},{4,2},{5,3},{6,0},{7,1},{8,14},{9,15},{10,... | collective-permute-start | bytes 294920 | tf_op jit(solution)/shard_map/ppermute | solution.py:544

commit v4 on v3

--- a/solution.py
+++ b/solution.py
@@ -17,6 +17,7 @@
 
 F32 = jnp.float32
 BF16 = jnp.bfloat16
+
 MIB = 1024 * 1024
 
 
@@ -83,7 +84,7 @@
     )(slab, head, perm, wells, *smalls)
 
 
-def kernel_rows(total_rows, slab, at_ref, layer_ref, high_ref, low_ref, dy2_ref):
+def kernel_rows(total_rows, slab, at_ref, layer_ref, out_ref, dy2_ref):
     cells, pixels = dy2_ref.shape
     rows = layer_ref.shape[0]
     position = lax.broadcasted_iota(jnp.int32, (cells, 128), 0).astype(F32)
@@ -104,17 +105,14 @@
             for sub in range(0, cells, 32):
                 r2 = dy2_ref[sub : sub + 32, lane : lane + 128] + dx2 + depth2[sub : sub + 32, :128]
                 inverse = lax.rsqrt(r2)
-                value = scaled[sub : sub + 32, :128] * inverse * (inverse * inverse)
-                high, low = split(value)
                 at = pl.ds(pl.multiple_of(row * cells + sub, 32), 32)
-                high_ref[at, lane : lane + 128] = high
-                low_ref[at, lane : lane + 128] = low
+                out_ref[at, lane : lane + 128] = scaled[sub : sub + 32, :128] * inverse * (inverse * inverse)
         return carry
 
-    lax.fori_loop(0, rows, one_row, 0)
-
-
-def observed_kernel(total_rows, slab_ref, coords_ref, index_ref, layer_ref, head_ref, perm_ref, high_ref, low_ref, p_ref, k_ref, dy2_ref, at_ref, table_ref, sems):
+    lax.fori_loop(0, rows, one_row, 0, unroll=4)
+
+
+def observed_kernel(total_rows, slab_ref, coords_ref, index_ref, layer_ref, head_ref, perm_ref, out_ref, p_ref, k_ref, dy2_ref, at_ref, table_ref, sems):
     rows = layer_ref.shape[0]
     pixels = dy2_ref.shape[1]
     tall = table_ref.shape[0] // 2
@@ -139,7 +137,7 @@
         own = lax.broadcasted_iota(jnp.int32, (tall, 128), 0) == (index >> 7)
         at_ref[0:1, lane : lane + 128] = jnp.sum(jnp.where(own, found[:tall], 0.0), 0, keepdims=True)
         at_ref[1:2, lane : lane + 128] = jnp.sum(jnp.where(own, found[tall:], 0.0), 0, keepdims=True)
-    kernel_rows(total_rows, slab_ref[0], at_ref, layer_ref, high_ref, low_ref, dy2_ref)
+    kernel_rows(total_rows, slab_ref[0], at_ref, layer_ref, out_ref, dy2_ref)
     for one in moves:
         one.wait()
 
@@ -148,13 +146,13 @@
     members = head.shape[0]
     rows, cells = layer.shape
     pixels = index.size
-    out = jax.ShapeDtypeStruct((rows * cells, pixels), BF16)
+    out = jax.ShapeDtypeStruct((rows * cells, pixels), F32)
     state = jax.ShapeDtypeStruct((rows, members, cells), F32)
     return pl.pallas_call(
         functools.partial(observed_kernel, total_rows),
-        out_shape=(out, out, state, state),
+        out_shape=(out, state, state),
         in_specs=[SMEM, VMEM, VMEM, VMEM, HBM, HBM],
-        out_specs=(VMEM,) * 4,
+        out_specs=(VMEM,) * 3,
         scratch_shapes=[
             pltpu.VMEM((cells, pixels), F32),
             pltpu.VMEM((8, pixels), F32),
@@ -167,7 +165,7 @@
     )(slab, coords, index, layer, head, perm)
 
 
-def pixel_kernel(total_rows, chips, own_rows, slab_ref, member_ref, coords_ref, layer_ref, high_ref, low_ref, dy2_ref, at_ref):
+def pixel_kernel(total_rows, chips, own_rows, slab_ref, member_ref, coords_ref, layer_ref, out_ref, dy2_ref, at_ref):
     if own_rows % 128:
         at_ref[0:2, :] = coords_ref[...]
     else:
@@ -180,7 +178,7 @@
                     at = pl.ds(pl.multiple_of(first + part, 128), 128)
                     at_ref[0:2, lane : lane + 128] = coords_ref[:, at].astype(F32)
                     lane += 128
-    kernel_rows(total_rows, slab_ref[0], at_ref, layer_ref, high_ref, low_ref, dy2_ref)
+    kernel_rows(total_rows, slab_ref[0], at_ref, layer_ref, out_ref, dy2_ref)
 
 
 def kernel_of_pixels(total_rows, groups, slab, member, coords, layer):
@@ -194,12 +192,12 @@
         coords = lax.dynamic_index_in_dim(coords, member[0], 1, keepdims=False)
         coords = jnp.swapaxes(coords, 1, 2)
         coords = jnp.where(slab[0] % 2 == 0, coords, coords[:, ::-1]).reshape(2, pixels)
-    out = jax.ShapeDtypeStruct((rows * cells, pixels), BF16)
+    out = jax.ShapeDtypeStruct((rows * cells, pixels), F32)
     return pl.pallas_call(
         functools.partial(pixel_kernel, total_rows, chips, own_rows),
-        out_shape=(out, out),
+        out_shape=out,
         in_specs=[SMEM, SMEM, VMEM, VMEM],
-        out_specs=(VMEM,) * 2,
+        out_specs=VMEM,
         scratch_shapes=[pltpu.VMEM((cells, pixels), F32), pltpu.VMEM((8, pixels), F32)],
         compiler_params=params(20),
         cost_estimate=cost(rows * cells * pixels * 16, rows * cells * pixels * 4),
@@ -273,19 +271,26 @@
             head, mobility, flux_before = head_next, mobility_next, flux_after
 
 
-def spread_product(left, padded, high_ref, low_ref, own_ref, other_ref):
+def spread_product(left_ref, padded, kernel_ref, own_ref, other_ref):
     half = own_ref.shape[1]
+    total = kernel_ref.shape[0]
     wide = 256 if half % 256 == 0 else 128
+    deep = min(total, 512)
     for first in range(0, 2 * half, wide):
-        both = dot(left, high_ref[:, first : first + wide])
-        value = both[:padded] + both[padded:] + dot(left[:padded], low_ref[:, first : first + wide])
+        value = None
+        for cell in range(0, total, deep):
+            high, low = split(kernel_ref[cell : cell + deep, first : first + wide])
+            both = dot(left_ref[:, cell : cell + deep], high)
+            thin = dot(left_ref[:padded, cell : cell + deep], low)
+            part = both[:padded] + both[padded:] + thin
+            value = part if value is None else value + part
         if first < half:
             own_ref[:, first : first + wide] = value
         else:
             other_ref[:, first - half : first - half + wide] = value
 
 
-def forecast_kernel(slabs, slab_ref, start_ref, perm_ref, wells_ref, near_ref, far_ref, high_ref, low_ref, cast_ref, own_ref, other_ref, p_ref, rim_ref, left_ref):
+def forecast_kernel(slabs, slab_ref, start_ref, perm_ref, wells_ref, near_ref, far_ref, kernel_ref, cast_ref, own_ref, other_ref, p_ref, rim_ref, left_ref):
     rows, members, cells = start_ref.shape
     padded = cast_ref.shape[0]
     forecast_steps(slab_ref[0], slabs, start_ref, perm_ref, wells_ref, near_ref, far_ref, p_ref, rim_ref)
@@ -299,17 +304,17 @@
         cast_ref[0:members, lane] = value
         left_ref[0:members, lane] = high
         left_ref[padded : padded + members, lane] = low
-    spread_product(left_ref[...], padded, high_ref, low_ref, own_ref, other_ref)
-
-
-def forecast(slabs, padded, slab, start, perm, wells, near, far, high, low):
+    spread_product(left_ref, padded, kernel_ref, own_ref, other_ref)
+
+
+def forecast(slabs, padded, slab, start, perm, wells, near, far, kernel):
     rows, members, cells = start.shape
-    total, observed = high.shape
+    total, observed = kernel.shape
     half = jax.ShapeDtypeStruct((padded, observed // 2), F32)
     return pl.pallas_call(
         functools.partial(forecast_kernel, slabs),
         out_shape=(jax.ShapeDtypeStruct((padded, total), F32), half, half),
-        in_specs=[SMEM] + [VMEM] * 7,
+        in_specs=[SMEM] + [VMEM] * 6,
         out_specs=(VMEM,) * 3,
         scratch_shapes=[
             pltpu.VMEM((rows + 2 * STEPS, members, cells), F32),
@@ -319,39 +324,38 @@
         compiler_params=params(20),
         cost_estimate=cost(6 * padded * total * observed, 4 * total * observed),
         name="forecast",
-    )(slab, start, perm, wells, near, far, high, low)
+    )(slab, start, perm, wells, near, far, kernel)
 
 
 def subsidence_kernel(groups, member_ref, *refs):
     pieces = refs[:groups]
-    high_ref, low_ref, own_ref, other_ref, cast_ref = refs[groups:]
-    padded, total = pieces[0].shape
+    kernel_ref, own_ref, other_ref, left_ref = refs[groups:]
+    padded, _ = pieces[0].shape
     every = groups * padded
     for offset in range(groups):
         at = member_ref[0] ^ offset
         high, low = split(pieces[offset][...])
-        cast_ref[at] = high
-        cast_ref[groups + at] = low
-    left = cast_ref[...].reshape(2 * every, total)
-    spread_product(left, every, high_ref, low_ref, own_ref, other_ref)
-
-
-def subsidence_partial(member, pieces, high, low):
+        left_ref[pl.ds(pl.multiple_of(at * padded, padded), padded), :] = high
+        left_ref[pl.ds(pl.multiple_of(every + at * padded, padded), padded), :] = low
+    spread_product(left_ref, every, kernel_ref, own_ref, other_ref)
+
+
+def subsidence_partial(member, pieces, kernel):
     groups = len(pieces)
     padded, total = pieces[0].shape
-    pixels = high.shape[1]
+    pixels = kernel.shape[1]
     every = groups * padded
     out = jax.ShapeDtypeStruct((every, pixels // 2), F32)
     return pl.pallas_call(
         functools.partial(subsidence_kernel, groups),
         out_shape=(out, out),
-        in_specs=[SMEM] + [VMEM] * (groups + 2),
+        in_specs=[SMEM] + [VMEM] * (groups + 1),
         out_specs=(VMEM,) * 2,
-        scratch_shapes=[pltpu.VMEM((2 * groups, padded, total), BF16)],
+        scratch_shapes=[pltpu.VMEM((2 * every, total), BF16)],
         compiler_params=params(24),
         cost_estimate=cost(6 * every * total * pixels, 4 * total * pixels + 4 * every * total),
         name="subsidence",
-    )(member, *pieces, high, low)
+    )(member, *pieces, kernel)
 
 
 def gram_kernel(groups, members, slab_ref, member_ref, *refs):
@@ -551,8 +555,8 @@
     far = lax.ppermute(far, "slab", across)
     near = lax.ppermute(near, "slab", pair)
 
-    high, low, start, perm_rows = kernel_of_observed(total_rows, slab_s, coords, index, layer, head, perm)
-    cast, own, other = forecast(slabs, padded, slab_s, start, perm_rows, wells, near, far, high, low)
+    kernel, start, perm_rows = kernel_of_observed(total_rows, slab_s, coords, index, layer, head, perm)
+    cast, own, other = forecast(slabs, padded, slab_s, start, perm_rows, wells, near, far, kernel)
     seen = own + swap(other, "slab", 1)
     pieces = [cast] + [swap(cast, "member", offset) for offset in range(1, groups)]
     offset = 2
@@ -565,8 +569,8 @@
 
     chips = slabs // 2
     own_rows = coords.shape[1] // (groups * slabs)
-    pixel_high, pixel_low = kernel_of_pixels(total_rows, groups, slab_s, member_s, coords, layer)
-    sunk, sunk_other = subsidence_partial(member_s, pieces, pixel_high, pixel_low)
+    kernel_all = kernel_of_pixels(total_rows, groups, slab_s, member_s, coords, layer)
+    sunk, sunk_other = subsidence_partial(member_s, pieces, kernel_all)
     sunk_recv = swap(sunk_other, "slab", 1)
     chip = slab // 2
 

time: 76.2 us -> 74.9 us (0.983)
  Pallas kernels: 27.8 us -> 23.4 us
  starting transfers between devices: 24.8 us -> 26.6 us
  waiting for transfers between devices: 21.7 us -> 23 us
    pallas_call x1, Pallas kernels: 5.91 us -> 3.25 us  [kernel_of_observed(): pl.pallas_call(functools.partial(observed_kernel, total_rows), out_shape=...]
    pallas_call x1, Pallas kernels: 5.32 us -> 2.89 us  [kernel_of_pixels(): pl.pallas_call(functools.partial(pixel_kernel, total_rows, chips, own_row...]
    ppermute x14, starting transfers between devices: 23.6 us -> 25.4 us  [swap(): return lax.ppermute(value, axis, [(i, i ^ offset) for i in range(size)])]
    ppermute x14, waiting for transfers between devices: 21.7 us -> 23 us  [swap(): return lax.ppermute(value, axis, [(i, i ^ offset) for i in range(size)])]
  transfers between devices with their start and end apart: 16 -> 16, of which waited for: 7 -> 7; matrix products, arithmetic and copies ran while one was open for 0% -> 0% of each run, Pallas kernels for 31% -> 25%
where the time goes in v4:
time: 74.9 us; the launch traced here: 74.6 us
  starting transfers between devices  26.6 us (36%)
  Pallas kernels  23.4 us (31%)
  waiting for transfers between devices  23 us (31%)
  other arithmetic  0.82 us (1%)
  between operations  0.75 us (1%)
    ppermute x14, starting transfers between devices, swap(): return lax.ppermute(value, axis, [(i, i ^ offset) for i in range(size)])  25.4 us
    ppermute x14, waiting for transfers between devices, swap(): return lax.ppermute(value, axis, [(i, i ^ offset) for i in range(size)])  23 us
    pallas_call x1, Pallas kernels, finish(): pl.pallas_call(functools.partial(finish_kernel, groups, members), out_sha...  8.26 us
    pallas_call x1, Pallas kernels, forecast(): pl.pallas_call(functools.partial(forecast_kernel, slabs), out_shape=(jax....  3.53 us
    pallas_call x1, Pallas kernels, subsidence_partial(): pl.pallas_call(functools.partial(subsidence_kernel, groups), out_shape=(o...  3.26 us
    pallas_call x1, Pallas kernels, kernel_of_observed(): pl.pallas_call(functools.partial(observed_kernel, total_rows), out_shape=...  3.25 us
    pallas_call x1, Pallas kernels, kernel_of_pixels(): pl.pallas_call(functools.partial(pixel_kernel, total_rows, chips, own_row...  2.89 us
  transfers between devices with their start and end apart: 16, of which 7 were waited for; matrix products, arithmetic and copies ran while one was open for 0% of the time, Pallas kernels for 25%

profile of v4, /device:TPU:0, one launch (start us, length us, event | category | flops | bytes accessed | tf_op | source)
XLA Modules:
  0.0 74.6 jit_solution(5583850918747435907)
XLA Ops:
  0.6 1.3 %pack_rims.1 = (f32[4,104,128]{2,1,0:T(8,128)S(1)}, f32[4,104,128]{2,1,0:T(8,128)S(1)}, f32[16,128]{1,0:T(8,128)S(1)}, s32[16,128]{1,0:T(8,128)S(1)}, s32[2,4096...) custom-call(s32[1]{0:T(128)} %bitcast.1.slab_ref, f32[48,16,128]{2,1,0:T(8,128)} %head_ref.3, ...), custom_call_target="tpu_custom_call" | custom-call | tf_op jit(solution)/shard_map/pack_rims/pallas_call | solution.py:76
  2.0 0.6 collective-permute-start
  2.5 0.7 collective-permute-start.1
  3.2 3.3 %kernel_of_observed.1 = (f32[2048,1024]{1,0:T(8,128)S(1)}, f32[16,48,128]{2,1,0:T(8,128)S(1)}, f32[16,48,128]{2,1,0:T(8,128)S(1)}) custom-call(s32[1]{0:T(128)} %bitcast.1.slab_ref, s32[2,4096]{1,0:T(2,128)S(1)} %get-tuple-element.18.coords_ref, s32[8,128]{1,0:T(8,128)S(1)} %get-tuple-element.19.index_ref, s32[16,128]{1,0:T(8,128)S(1)} %get-tuple-element.20.layer_ref, ...), custom_call_target="tpu_custom_call" | custom-call | flops 33554432 | bytes 8388608 | tf_op jit(solution)/shard_map/kernel_of_observed/pallas_call | solution.py:151
  6.4 0.0 collective-permute-done.near_ref
  6.5 0.0 collective-permute-done.1.far_ref
  6.5 3.5 %forecast.1 = (f32[48,2048]{1,0:T(8,128)S(1)}, f32[48,512]{1,0:T(8,128)S(1)}, f32[48,512]{1,0:T(8,128)S(1)}) custom-call(s32[1]{0:T(128)} %bitcast.1.slab_ref, f32[16,48,128]{2,1,0:T(8,128)S(1)} %get-tuple-element.21.start_ref, f32[16,48,128]{2,1,0:T(8,128)S(1)} %get-tuple-element.22.perm_ref, f32[16,128]{1,0:T(8,128)S(1)} %get-tuple-element.23.wells_ref, ...), custom_call_target="tpu_custom_call" | custom-call | flops 603979776 | bytes 8388608 | tf_op jit(solution)/shard_map/forecast/pallas_call | solution.py:314
  10.0 2.5 %collective-permute-start.10 = (f32[48,2048]{1,0:T(8,128)S(1)}, f32[48,2048]{1,0:T(8,128)S(1)}, u32[]{:S(2)}, u32[]{:S(2)}) collective-permute-start(f32[48,2048]{1,0:T(8,128)S(1)} %get-tuple-element.31.refs_0_), channel_id=1, source_target_pairs={{0,16},{8,24},{16,0},{24,8},{1,17},{9,25},{17,1},{25,9},{2,18},{10... | collective-permute-start | bytes 1179656 | tf_op jit(solution)/shard_map/ppermute | solution.py:548
  12.5 1.4 %collective-permute-start.11 = (f32[48,2048]{1,0:T(8,128)S(1)}, f32[48,2048]{1,0:T(8,128)S(1)}, u32[]{:S(2)}, u32[]{:S(2)}) collective-permute-start(f32[48,2048]{1,0:T(8,128)S(1)} %get-tuple-element.31.refs_0_), channel_id=1, source_target_pairs={{0,24},{8,16},{16,8},{24,0},{1,25},{9,17},{17,9},{25,1},{2,26},{10... | collective-permute-start | bytes 1179656 | tf_op jit(solution)/shard_map/ppermute | solution.py:548
  14.0 0.1 collective-permute-start.9
  14.1 2.9 %kernel_of_pixels.1.refs_4_ = f32[2048,1024]{1,0:T(8,128)S(1)} custom-call(s32[1]{0:T(128)} %bitcast.1.slab_ref, s32[1]{0:T(128)} %bitcast.member_ref, s32[2,4096]{1,0:T(2,128)S(1)} %get-tuple-element.18.coords_ref, s32[16,128]{1,0:T(8,128)S(1)} %get-tuple-element.20.layer_ref), custom_call_target="tpu_custom_call" | custom-call | flops 33554432 | bytes 8388608 | tf_op jit(solution)/shard_map/kernel_of_pixels/pallas_call | solution.py:196
  17.0 3.2 %collective-permute-start.2 = (f32[48,512]{1,0:T(8,128)S(1)}, f32[48,512]{1,0:T(8,128)S(1)}, u32[]{:S(2)}, u32[]{:S(2)}) collective-permute-start(f32[48,512]{1,0:T(8,128)S(1)} %get-tuple-element.28), channel_id=1, source_target_pairs={{0,1},{1,0},{2,3},{3,2},{4,5},{5,4},{6,7},{7,6},{8,9},{9,8},{10,11... | collective-permute-start | bytes 294920 | tf_op jit(solution)/shard_map/ppermute | solution.py:548
  20.2 9.2 %collective-permute-done.10.refs_2_ = f32[48,2048]{1,0:T(8,128)S(1)} collective-permute-done((f32[48,2048]{1,0:T(8,128)S(1)}, f32[48,2048]{1,0:T(8,128)S(1)}, u32[]{:S(2)}, u32[]{:S(2)}) %collective-permute-start.10) | collective-permute-done | bytes 393248 | tf_op jit(solution)/shard_map/ppermute | solution.py:548
  29.4 0.0 collective-permute-done.11.refs_3_
  29.4 0.4 collective-permute-done.9.refs_1_
  29.8 3.3 %subsidence.1 = (f32[192,512]{1,0:T(8,128)S(1)}, f32[192,512]{1,0:T(8,128)S(1)}) custom-call(s32[1]{0:T(128)} %bitcast.member_ref, f32[48,2048]{1,0:T(8,128)S(1)} %get-tuple-element.31.refs_0_, f32[48,2048]{1,0:T(8,128)S(1)} %collective-permute-done.9.refs_1_, f32[48,2048]{1,0:T(8,128)S(1)} %collective-permute-done.10.refs_2_, ...), custom_call_target="tpu_custom_call" | custom-call | flops 2415919104 | bytes 9961472 | tf_op jit(solution)/shard_map/subsidence/pallas_call | solution.py:349
  33.1 2.6 %collective-permute-start.12 = (f32[192,512]{1,0:T(8,128)S(1)}, f32[192,512]{1,0:T(8,128)S(1)}, u32[]{:S(2)}, u32[]{:S(2)}) collective-permute-start(f32[192,512]{1,0:T(8,128)S(1)} %get-tuple-element.33), channel_id=1, source_target_pairs={{0,1},{1,0},{2,3},{3,2},{4,5},{5,4},{6,7},{7,6},{8,9},{9,8},{10,11... | collective-permute-start | bytes 1179656 | tf_op jit(solution)/shard_map/ppermute | solution.py:548
  35.7 0.0 collective-permute-done.2
  35.7 4.7 %collective-permute-start.3 = (f32[48,512]{1,0:T(8,128)S(1)}, f32[48,512]{1,0:T(8,128)S(1)}, u32[]{:S(2)}, u32[]{:S(2)}) collective-permute-start(f32[48,512]{1,0:T(8,128)S(1)} %add.47), channel_id=1, source_target_pairs={{0,2},{1,3},{2,0},{3,1},{4,6},{5,7},{6,4},{7,5},{8,10},{9,11},{10,... | collective-permute-start | bytes 294920 | tf_op jit(solution)/shard_map/ppermute | solution.py:548
  40.4 3.4 %collective-permute-done.3 = f32[48,512]{1,0:T(8,128)S(1)} collective-permute-done((f32[48,512]{1,0:T(8,128)S(1)}, f32[48,512]{1,0:T(8,128)S(1)}, u32[]{:S(2)}, u32[]{:S(2)}) %collective-permute-start.3) | collective-permute-done | bytes 98336 | tf_op jit(solution)/shard_map/ppermute | solution.py:548
  43.9 2.8 %collective-permute-start.4 = (f32[48,512]{1,0:T(8,128)S(1)}, f32[48,512]{1,0:T(8,128)S(1)}, u32[]{:S(2)}, u32[]{:S(2)}) collective-permute-start(f32[48,512]{1,0:T(8,128)S(1)} %add.48), channel_id=1, source_target_pairs={{0,4},{1,5},{2,6},{3,7},{4,0},{5,1},{6,2},{7,3},{8,12},{9,13},{10,... | collective-permute-start | bytes 294920 | tf_op jit(solution)/shard_map/ppermute | solution.py:548
  46.7 4.9 %collective-permute-done.4 = f32[48,512]{1,0:T(8,128)S(1)} collective-permute-done((f32[48,512]{1,0:T(8,128)S(1)}, f32[48,512]{1,0:T(8,128)S(1)}, u32[]{:S(2)}, u32[]{:S(2)}) %collective-permute-start.4) | collective-permute-done | bytes 98336 | tf_op jit(solution)/shard_map/ppermute | solution.py:548
  51.6 1.6 %collective-permute-start.5 = (f32[48,512]{1,0:T(8,128)S(1)}, f32[48,512]{1,0:T(8,128)S(1)}, u32[]{:S(2)}, u32[]{:S(2)}) collective-permute-start(f32[48,512]{1,0:T(8,128)S(1)} %add.49.refs_0_), channel_id=1, source_target_pairs={{0,8},{8,0},{16,24},{24,16},{1,9},{9,1},{17,25},{25,17},{2,10},{10... | collective-permute-start | bytes 294920 | tf_op jit(solution)/shard_map/ppermute | solution.py:548
  53.1 1.5 %collective-permute-start.6 = (f32[48,512]{1,0:T(8,128)S(1)}, f32[48,512]{1,0:T(8,128)S(1)}, u32[]{:S(2)}, u32[]{:S(2)}) collective-permute-start(f32[48,512]{1,0:T(8,128)S(1)} %add.49.refs_0_), channel_id=1, source_target_pairs={{0,16},{8,24},{16,0},{24,8},{1,17},{9,25},{17,1},{25,9},{2,18},{10... | collective-permute-start | bytes 294920 | tf_op jit(solution)/shard_map/ppermute | solution.py:548
  54.6 0.5 collective-permute-start.7
  55.1 1.7 %collective-permute-done.5.refs_1_ = f32[48,512]{1,0:T(8,128)S(1)} collective-permute-done((f32[48,512]{1,0:T(8,128)S(1)}, f32[48,512]{1,0:T(8,128)S(1)}, u32[]{:S(2)}, u32[]{:S(2)}) %collective-permute-start.5) | collective-permute-done | bytes 98336 | tf_op jit(solution)/shard_map/ppermute | solution.py:548
  56.8 1.2 %collective-permute-done.6.refs_2_ = f32[48,512]{1,0:T(8,128)S(1)} collective-permute-done((f32[48,512]{1,0:T(8,128)S(1)}, f32[48,512]{1,0:T(8,128)S(1)}, u32[]{:S(2)}, u32[]{:S(2)}) %collective-permute-start.6) | collective-permute-done | bytes 98336 | tf_op jit(solution)/shard_map/ppermute | solution.py:548
  58.0 2.1 %collective-permute-done.7.refs_3_ = f32[48,512]{1,0:T(8,128)S(1)} collective-permute-done((f32[48,512]{1,0:T(8,128)S(1)}, f32[48,512]{1,0:T(8,128)S(1)}, u32[]{:S(2)}, u32[]{:S(2)}) %collective-permute-start.7) | collective-permute-done | bytes 98336 | tf_op jit(solution)/shard_map/ppermute | solution.py:548
  60.1 0.9 %gram.1.gram_ref = f32[192,256]{1,0:T(8,128)S(1)} custom-call(s32[1]{0:T(128)} %bitcast.1.slab_ref, s32[1]{0:T(128)} %bitcast.member_ref, f32[48,512]{1,0:T(8,128)S(1)} %add.49.refs_0_, f32[48,512]{1,0:T(8,128)S(1)} %collective-permute-done.5.refs_1_, f32[48,512]{1,0:T(8,128)S(1)} %collective-permute-done.6.refs_2_, ...), custom_call_target="tpu_custom_call" | custom-call | flops 226492416 | bytes 393216 | tf_op jit(solution)/shard_map/gram/pallas_call | solution.py:396
  61.0 0.1 collective-permute-start.8
  61.1 0.0 collective-permute-done.12
  61.1 0.1 dynamic-slice_add_fusion.2
  61.2 0.1 collective-permute-start.13
  61.3 3.0 %collective-permute-start.14 = (f32[192,128]{1,0:T(8,128)S(1)}, f32[192,128]{1,0:T(8,128)S(1)}, u32[]{:S(2)}, u32[]{:S(2)}) collective-permute-start(f32[192,128]{1,0:T(8,128)S(1)} %get-tuple-element.36), channel_id=1, source_target_pairs={{0,4},{1,5},{2,6},{3,7},{4,0},{5,1},{6,2},{7,3},{8,12},{9,13},{10,... | collective-permute-start | bytes 294920 | tf_op jit(solution)/shard_map/ppermute | solution.py:548
  64.3 1.3 %collective-permute-start.15 = (f32[192,128]{1,0:T(8,128)S(1)}, f32[192,128]{1,0:T(8,128)S(1)}, u32[]{:S(2)}, u32[]{:S(2)}) collective-permute-start(f32[192,128]{1,0:T(8,128)S(1)} %get-tuple-element.35), channel_id=1, source_target_pairs={{0,6},{1,7},{2,4},{3,5},{4,2},{5,3},{6,0},{7,1},{8,14},{9,15},{10,... | collective-permute-start | bytes 294920 | tf_op jit(solution)/shard_map/ppermute | solution.py:548
  65.7 0.0 collective-permute-done.8.more_ref
  65.7 8.3 %finish.1 = f32[48,16,128]{2,1,0:T(8,128)} custom-call(s32[1]{0:T(128)} %bitcast.member_ref, f32[192,256]{1,0:T(8,128)S(1)} %gram.1.gram_ref, f32[192,256]{1,0:T(8,128)S(1)} %collective-permute-done.8.more_ref, f32[48,2048]{1,0:T(8,128)S(1)} %get-tuple-element.31.refs_0_, f32[48,2048]{1,0:T(8,128)S(1)} %collective-permute-done.9.refs_1_, ...), custom_call_target="tpu_custom_call" | custom-call | flops 113246208 | bytes 1572864 | tf_op jit(solution)/shard_map/finish/pallas_call | solution.py:521
  73.9 0.0 collective-permute-done.13
  73.9 0.0 collective-permute-done.14
  73.9 0.0 collective-permute-done.15
  73.9 0.7 add_bitcast_fusion
  (3 shorter events, 0.0 us)
Async XLA Ops:
  2.0 4.5 %collective-permute-start = (f32[4,104,128]{2,1,0:T(8,128)S(1)}, f32[4,104,128]{2,1,0:T(8,128)S(1)}, u32[]{:S(2)}, u32[]{:S(2)}) collective-permute-start(f32[4,104,128]{2,1,0:T(8,128)S(1)} %get-tuple-element.24), channel_id=1, source_target_pairs={{0,1},{1,0},{2,3},{3,2},{4,5},{5,4},{6,7},{7,6},{8,9},{9,8},{10,11... | collective-permute-start | bytes 638984 | tf_op jit(solution)/shard_map/ppermute | solution.py:556
  2.5 3.9 %collective-permute-start.1 = (f32[4,104,128]{2,1,0:T(8,128)S(1)}, f32[4,104,128]{2,1,0:T(8,128)S(1)}, u32[]{:S(2)}, u32[]{:S(2)}) collective-permute-start(f32[4,104,128]{2,1,0:T(8,128)S(1)} %get-tuple-element.25), channel_id=1, source_target_pairs={{1,2},{3,4},{5,6},{2,1},{4,3},{6,5},{9,10},{11,12},{13,14},{10,9},... | collective-permute-start | bytes 638984 | tf_op jit(solution)/shard_map/ppermute | solution.py:555
  10.0 19.4 %collective-permute-start.10 = (f32[48,2048]{1,0:T(8,128)S(1)}, f32[48,2048]{1,0:T(8,128)S(1)}, u32[]{:S(2)}, u32[]{:S(2)}) collective-permute-start(f32[48,2048]{1,0:T(8,128)S(1)} %get-tuple-element.31.refs_0_), channel_id=1, source_target_pairs={{0,16},{8,24},{16,0},{24,8},{1,17},{9,25},{17,1},{25,9},{2,18},{10... | collective-permute-start | bytes 1179656 | tf_op jit(solution)/shard_map/ppermute | solution.py:548
  12.5 16.9 %collective-permute-start.11 = (f32[48,2048]{1,0:T(8,128)S(1)}, f32[48,2048]{1,0:T(8,128)S(1)}, u32[]{:S(2)}, u32[]{:S(2)}) collective-permute-start(f32[48,2048]{1,0:T(8,128)S(1)} %get-tuple-element.31.refs_0_), channel_id=1, source_target_pairs={{0,24},{8,16},{16,8},{24,0},{1,25},{9,17},{17,9},{25,1},{2,26},{10... | collective-permute-start | bytes 1179656 | tf_op jit(solution)/shard_map/ppermute | solution.py:548
  14.0 15.9 %collective-permute-start.9 = (f32[48,2048]{1,0:T(8,128)S(1)}, f32[48,2048]{1,0:T(8,128)S(1)}, u32[]{:S(2)}, u32[]{:S(2)}) collective-permute-start(f32[48,2048]{1,0:T(8,128)S(1)} %get-tuple-element.31.refs_0_), channel_id=1, source_target_pairs={{0,8},{8,0},{16,24},{24,16},{1,9},{9,1},{17,25},{25,17},{2,10},{10... | collective-permute-start | bytes 1179656 | tf_op jit(solution)/shard_map/ppermute | solution.py:548
  17.0 18.7 %collective-permute-start.2 = (f32[48,512]{1,0:T(8,128)S(1)}, f32[48,512]{1,0:T(8,128)S(1)}, u32[]{:S(2)}, u32[]{:S(2)}) collective-permute-start(f32[48,512]{1,0:T(8,128)S(1)} %get-tuple-element.28), channel_id=1, source_target_pairs={{0,1},{1,0},{2,3},{3,2},{4,5},{5,4},{6,7},{7,6},{8,9},{9,8},{10,11... | collective-permute-start | bytes 294920 | tf_op jit(solution)/shard_map/ppermute | solution.py:548
  33.1 28.0 %collective-permute-start.12 = (f32[192,512]{1,0:T(8,128)S(1)}, f32[192,512]{1,0:T(8,128)S(1)}, u32[]{:S(2)}, u32[]{:S(2)}) collective-permute-start(f32[192,512]{1,0:T(8,128)S(1)} %get-tuple-element.33), channel_id=1, source_target_pairs={{0,1},{1,0},{2,3},{3,2},{4,5},{5,4},{6,7},{7,6},{8,9},{9,8},{10,11... | collective-permute-start | bytes 1179656 | tf_op jit(solution)/shard_map/ppermute | solution.py:548
  35.7 8.2 %collective-permute-start.3 = (f32[48,512]{1,0:T(8,128)S(1)}, f32[48,512]{1,0:T(8,128)S(1)}, u32[]{:S(2)}, u32[]{:S(2)}) collective-permute-start(f32[48,512]{1,0:T(8,128)S(1)} %add.47), channel_id=1, source_target_pairs={{0,2},{1,3},{2,0},{3,1},{4,6},{5,7},{6,4},{7,5},{8,10},{9,11},{10,... | collective-permute-start | bytes 294920 | tf_op jit(solution)/shard_map/ppermute | solution.py:548
  43.9 7.7 %collective-permute-start.4 = (f32[48,512]{1,0:T(8,128)S(1)}, f32[48,512]{1,0:T(8,128)S(1)}, u32[]{:S(2)}, u32[]{:S(2)}) collective-permute-start(f32[48,512]{1,0:T(8,128)S(1)} %add.48), channel_id=1, source_target_pairs={{0,4},{1,5},{2,6},{3,7},{4,0},{5,1},{6,2},{7,3},{8,12},{9,13},{10,... | collective-permute-start | bytes 294920 | tf_op jit(solution)/shard_map/ppermute | solution.py:548
  51.6 5.2 %collective-permute-start.5 = (f32[48,512]{1,0:T(8,128)S(1)}, f32[48,512]{1,0:T(8,128)S(1)}, u32[]{:S(2)}, u32[]{:S(2)}) collective-permute-start(f32[48,512]{1,0:T(8,128)S(1)} %add.49.refs_0_), channel_id=1, source_target_pairs={{0,8},{8,0},{16,24},{24,16},{1,9},{9,1},{17,25},{25,17},{2,10},{10... | collective-permute-start | bytes 294920 | tf_op jit(solution)/shard_map/ppermute | solution.py:548
  53.1 4.9 %collective-permute-start.6 = (f32[48,512]{1,0:T(8,128)S(1)}, f32[48,512]{1,0:T(8,128)S(1)}, u32[]{:S(2)}, u32[]{:S(2)}) collective-permute-start(f32[48,512]{1,0:T(8,128)S(1)} %add.49.refs_0_), channel_id=1, source_target_pairs={{0,16},{8,24},{16,0},{24,8},{1,17},{9,25},{17,1},{25,9},{2,18},{10... | collective-permute-start | bytes 294920 | tf_op jit(solution)/shard_map/ppermute | solution.py:548
  54.6 5.5 %collective-permute-start.7 = (f32[48,512]{1,0:T(8,128)S(1)}, f32[48,512]{1,0:T(8,128)S(1)}, u32[]{:S(2)}, u32[]{:S(2)}) collective-permute-start(f32[48,512]{1,0:T(8,128)S(1)} %add.49.refs_0_), channel_id=1, source_target_pairs={{0,24},{8,16},{16,8},{24,0},{1,25},{9,17},{17,9},{25,1},{2,26},{10... | collective-permute-start | bytes 294920 | tf_op jit(solution)/shard_map/ppermute | solution.py:548
  61.0 4.6 %collective-permute-start.8 = (f32[192,256]{1,0:T(8,128)S(1)}, f32[192,256]{1,0:T(8,128)S(1)}, u32[]{:S(2)}, u32[]{:S(2)}) collective-permute-start(f32[192,256]{1,0:T(8,128)S(1)} %gram.1.gram_ref), channel_id=1, source_target_pairs={{0,1},{1,0},{2,3},{3,2},{4,5},{5,4},{6,7},{7,6},{8,9},{9,8},{10,11... | collective-permute-start | bytes 589832 | tf_op jit(solution)/shard_map/ppermute | solution.py:548
  61.2 12.7 %collective-permute-start.13 = (f32[192,128]{1,0:T(8,128)S(1)}, f32[192,128]{1,0:T(8,128)S(1)}, u32[]{:S(2)}, u32[]{:S(2)}) collective-permute-start(f32[192,128]{1,0:T(8,128)S(1)} %get-tuple-element.34), channel_id=1, source_target_pairs={{0,2},{1,3},{2,0},{3,1},{4,6},{5,7},{6,4},{7,5},{8,10},{9,11},{10,... | collective-permute-start | bytes 294920 | tf_op jit(solution)/shard_map/ppermute | solution.py:548
  61.3 12.6 %collective-permute-start.14 = (f32[192,128]{1,0:T(8,128)S(1)}, f32[192,128]{1,0:T(8,128)S(1)}, u32[]{:S(2)}, u32[]{:S(2)}) collective-permute-start(f32[192,128]{1,0:T(8,128)S(1)} %get-tuple-element.36), channel_id=1, source_target_pairs={{0,4},{1,5},{2,6},{3,7},{4,0},{5,1},{6,2},{7,3},{8,12},{9,13},{10,... | collective-permute-start | bytes 294920 | tf_op jit(solution)/shard_map/ppermute | solution.py:548
  64.3 9.6 %collective-permute-start.15 = (f32[192,128]{1,0:T(8,128)S(1)}, f32[192,128]{1,0:T(8,128)S(1)}, u32[]{:S(2)}, u32[]{:S(2)}) collective-permute-start(f32[192,128]{1,0:T(8,128)S(1)} %get-tuple-element.35), channel_id=1, source_target_pairs={{0,6},{1,7},{2,4},{3,5},{4,2},{5,3},{6,0},{7,1},{8,14},{9,15},{10,... | collective-permute-start | bytes 294920 | tf_op jit(solution)/shard_map/ppermute | solution.py:548

commit v5 on v4

--- a/solution.py
+++ b/solution.py
@@ -405,41 +405,53 @@
     )(slab, member, *pieces, value, sigma)
 
 
+COLUMNS = 8
+
+
 def eliminate_panel(rows, scaled, first, count):
     groups = count // 8
     tiles = rows.shape[1] // 128
     sub_row = lax.broadcasted_iota(jnp.int32, (8, 128), 0)
     lane = lax.broadcasted_iota(jnp.int32, (8, 128), 1)
     x = [[rows[8 * g : 8 * g + 8, 128 * t : 128 * t + 128] for t in range(tiles)] for g in range(groups)]
-    full = lambda v: jnp.broadcast_to(v, (8, 128))
-    scale = [None] * groups
-    for s in range(groups):
-        column = first + 8 * s
-        tile, at = column // 128, column % 128
-        c = [[full(x[g][tile][:, at + j : at + j + 1]) for g in range(s, groups)] for j in range(8)]
-        scale[s] = jnp.zeros((8, 128), F32)
-        for j in range(8):
-            pivot = full(c[j][0][j : j + 1, :])
+    pick = lambda v, j: jnp.take_along_axis(v, jnp.full((8, 128), j, jnp.int32), 0, mode="promise_in_bounds")
+    scale = [jnp.zeros((8, 128), F32) for _ in range(groups)]
+    batch = min(COLUMNS, count)
+    for start in range(0, count, batch):
+        low = start // 8
+        c = []
+        for j in range(batch):
+            tile, at = (first + start + j) // 128, (first + start + j) % 128
+            c.append({g: jnp.broadcast_to(x[g][tile][:, at : at + 1], (8, 128)) for g in range(low, groups)})
+        pivot = pick(c[0][low], 0)
+        for j in range(batch):
+            own, sub = low + j // 8, j % 8
+            tile, at = (first + start + j) // 128, (first + start + j) % 128
             inverse = pltpu.reciprocal(pivot, approx=False)
-            below = sub_row > j
-            m = [v * inverse for v in c[j]]
-            m[0] = jnp.where(below, m[0], 0.0)
             root = lax.rsqrt(pivot)
             root = root * (1.5 - 0.5 * pivot * root * root)
-            scale[s] = jnp.where(sub_row == j, root, scale[s])
-            for l in range(j + 1, 8):
-                entry = full(c[l][0][j : j + 1, :])
-                c[l] = [v - k * entry for v, k in zip(c[l], m)]
-            here = lane == at + j
+            scale[own] = jnp.where(sub_row == sub, root, scale[own])
+            if j + 1 < batch:
+                after, after_sub = low + (j + 1) // 8, (j + 1) % 8
+                cross = pick(c[j][after], after_sub) * pick(c[j + 1][own], sub)
+                pivot = pick(c[j + 1][after], after_sub) - cross * inverse
+            for l in range(j + 1, batch):
+                entry = pick(c[l][own], sub)
+                for g in range(own, groups):
+                    c[l][g] = c[l][g] - (c[j][g] * entry) * inverse
+            below = sub_row > sub
+            m = {g: c[j][g] * inverse for g in range(own, groups)}
+            m[own] = jnp.where(below, m[own], 0.0)
+            here = lane == at
             for t in range(tiles):
-                row = full(x[s][t][j : j + 1, :])
+                row = pick(x[own][t], sub)
                 if t == tile:
                     row = jnp.where(here, 1.0, row)
-                for g in range(s, groups):
+                for g in range(own, groups):
                     old = x[g][t]
                     if t == tile:
-                        old = jnp.where(here & below if g == s else here, 0.0, old)
-                    x[g][t] = old - m[g - s] * row
+                        old = jnp.where(here & below if g == own else here, 0.0, old)
+                    x[g][t] = old - m[g] * row
     for g in range(groups):
         for t in range(tiles):
             value = x[g][t]
@@ -452,23 +464,26 @@
 
 def invert(work_ref):
     every, width = work_ref.shape
-    panel = 32
+    panel = math.gcd(every, 64)
     for first in range(0, every, panel):
         eliminate_panel(work_ref[first : first + panel, :], work_ref, first, panel)
         below = first + panel
         if below < every:
             done = work_ref[first:below, :]
+            base = below // 128 * 128
+            one = done.astype(BF16)
+            rest = done - one.astype(F32)
+            two = rest.astype(BF16)
+            three = (rest - two.astype(F32)).astype(BF16)
+            left = jnp.concatenate([one, one, two, two, one, three], 0)[:, base:every]
+            right = jnp.concatenate([one, two, one, two, three, one], 0)
             product = lax.dot_general(
-                done[:, below:every] if below % 128 == 0 else done[:, below // 128 * 128 : every],
-                done,
-                (((0,), (0,)), ((), ())),
-                precision=lax.Precision.HIGHEST,
-                preferred_element_type=F32,
+                left, right, (((0,), (0,)), ((), ())), preferred_element_type=F32
             )
             column = lax.broadcasted_iota(jnp.int32, (every - below, width), 1)
             own = (column >= first) & (column < below)
             old = jnp.where(own, 0.0, work_ref[below:every, :])
-            work_ref[below:every, :] = old - product[below - below // 128 * 128 :]
+            work_ref[below:every, :] = old - product[below - base :]
 
 
 def finish_kernel(groups, members, member_ref, gram_ref, more_ref, *refs):

time: 74.9 us -> 73.1 us (0.976)
  Pallas kernels: 23.4 us -> 21.1 us
    pallas_call x1, Pallas kernels: 8.26 us -> 5.95 us  [finish(): pl.pallas_call(functools.partial(finish_kernel, groups, members), out_sha...]
  transfers between devices with their start and end apart: 16 -> 16, of which waited for: 7 -> 8; matrix products, arithmetic and copies ran while one was open for 0% -> 0% of each run, Pallas kernels for 25% -> 22%
where the time goes in v5:
time: 73.1 us; the launch traced here: 72.9 us
  starting transfers between devices  26.6 us (36%)
  waiting for transfers between devices  23.6 us (32%)
  Pallas kernels  21.1 us (29%)
  other arithmetic  0.82 us (1%)
  between operations  0.75 us (1%)
    ppermute x14, starting transfers between devices, swap(): return lax.ppermute(value, axis, [(i, i ^ offset) for i in range(size)])  25.4 us
    ppermute x14, waiting for transfers between devices, swap(): return lax.ppermute(value, axis, [(i, i ^ offset) for i in range(size)])  23.6 us
    pallas_call x1, Pallas kernels, finish(): pl.pallas_call(functools.partial(finish_kernel, groups, members), out_sha...  5.95 us
    pallas_call x1, Pallas kernels, forecast(): pl.pallas_call(functools.partial(forecast_kernel, slabs), out_shape=(jax....  3.53 us
    pallas_call x1, Pallas kernels, subsidence_partial(): pl.pallas_call(functools.partial(subsidence_kernel, groups), out_shape=(o...  3.26 us
    pallas_call x1, Pallas kernels, kernel_of_observed(): pl.pallas_call(functools.partial(observed_kernel, total_rows), out_shape=...  3.25 us
    pallas_call x1, Pallas kernels, kernel_of_pixels(): pl.pallas_call(functools.partial(pixel_kernel, total_rows, chips, own_row...  2.89 us
  transfers between devices with their start and end apart: 16, of which 8 were waited for; matrix products, arithmetic and copies ran while one was open for 0% of the time, Pallas kernels for 22%

profile of v5, /device:TPU:0, one launch (start us, length us, event | category | flops | bytes accessed | tf_op | source)
XLA Modules:
  0.0 72.9 jit_solution(6146782384347941486)
XLA Ops:
  0.6 1.3 %pack_rims.1 = (f32[4,104,128]{2,1,0:T(8,128)S(1)}, f32[4,104,128]{2,1,0:T(8,128)S(1)}, f32[16,128]{1,0:T(8,128)S(1)}, s32[16,128]{1,0:T(8,128)S(1)}, s32[2,4096...) custom-call(s32[1]{0:T(128)} %bitcast.1.slab_ref, f32[48,16,128]{2,1,0:T(8,128)} %head_ref.3, ...), custom_call_target="tpu_custom_call" | custom-call | tf_op jit(solution)/shard_map/pack_rims/pallas_call | solution.py:76
  2.0 0.6 collective-permute-start
  2.5 0.7 collective-permute-start.1
  3.2 3.3 %kernel_of_observed.1 = (f32[2048,1024]{1,0:T(8,128)S(1)}, f32[16,48,128]{2,1,0:T(8,128)S(1)}, f32[16,48,128]{2,1,0:T(8,128)S(1)}) custom-call(s32[1]{0:T(128)} %bitcast.1.slab_ref, s32[2,4096]{1,0:T(2,128)S(1)} %get-tuple-element.18.coords_ref, s32[8,128]{1,0:T(8,128)S(1)} %get-tuple-element.19.index_ref, s32[16,128]{1,0:T(8,128)S(1)} %get-tuple-element.20.layer_ref, ...), custom_call_target="tpu_custom_call" | custom-call | flops 33554432 | bytes 8388608 | tf_op jit(solution)/shard_map/kernel_of_observed/pallas_call | solution.py:151
  6.4 0.0 collective-permute-done.near_ref
  6.5 0.0 collective-permute-done.1.far_ref
  6.5 3.5 %forecast.1 = (f32[48,2048]{1,0:T(8,128)S(1)}, f32[48,512]{1,0:T(8,128)S(1)}, f32[48,512]{1,0:T(8,128)S(1)}) custom-call(s32[1]{0:T(128)} %bitcast.1.slab_ref, f32[16,48,128]{2,1,0:T(8,128)S(1)} %get-tuple-element.21.start_ref, f32[16,48,128]{2,1,0:T(8,128)S(1)} %get-tuple-element.22.perm_ref, f32[16,128]{1,0:T(8,128)S(1)} %get-tuple-element.23.wells_ref, ...), custom_call_target="tpu_custom_call" | custom-call | flops 603979776 | bytes 8388608 | tf_op jit(solution)/shard_map/forecast/pallas_call | solution.py:314
  10.0 2.5 %collective-permute-start.10 = (f32[48,2048]{1,0:T(8,128)S(1)}, f32[48,2048]{1,0:T(8,128)S(1)}, u32[]{:S(2)}, u32[]{:S(2)}) collective-permute-start(f32[48,2048]{1,0:T(8,128)S(1)} %get-tuple-element.31.refs_0_), channel_id=1, source_target_pairs={{0,16},{8,24},{16,0},{24,8},{1,17},{9,25},{17,1},{25,9},{2,18},{10... | collective-permute-start | bytes 1179656 | tf_op jit(solution)/shard_map/ppermute | solution.py:563
  12.5 1.4 %collective-permute-start.11 = (f32[48,2048]{1,0:T(8,128)S(1)}, f32[48,2048]{1,0:T(8,128)S(1)}, u32[]{:S(2)}, u32[]{:S(2)}) collective-permute-start(f32[48,2048]{1,0:T(8,128)S(1)} %get-tuple-element.31.refs_0_), channel_id=1, source_target_pairs={{0,24},{8,16},{16,8},{24,0},{1,25},{9,17},{17,9},{25,1},{2,26},{10... | collective-permute-start | bytes 1179656 | tf_op jit(solution)/shard_map/ppermute | solution.py:563
  14.0 0.1 collective-permute-start.9
  14.1 2.9 %kernel_of_pixels.1.refs_4_ = f32[2048,1024]{1,0:T(8,128)S(1)} custom-call(s32[1]{0:T(128)} %bitcast.1.slab_ref, s32[1]{0:T(128)} %bitcast.member_ref, s32[2,4096]{1,0:T(2,128)S(1)} %get-tuple-element.18.coords_ref, s32[16,128]{1,0:T(8,128)S(1)} %get-tuple-element.20.layer_ref), custom_call_target="tpu_custom_call" | custom-call | flops 33554432 | bytes 8388608 | tf_op jit(solution)/shard_map/kernel_of_pixels/pallas_call | solution.py:196
  17.0 3.2 %collective-permute-start.2 = (f32[48,512]{1,0:T(8,128)S(1)}, f32[48,512]{1,0:T(8,128)S(1)}, u32[]{:S(2)}, u32[]{:S(2)}) collective-permute-start(f32[48,512]{1,0:T(8,128)S(1)} %get-tuple-element.28), channel_id=1, source_target_pairs={{0,1},{1,0},{2,3},{3,2},{4,5},{5,4},{6,7},{7,6},{8,9},{9,8},{10,11... | collective-permute-start | bytes 294920 | tf_op jit(solution)/shard_map/ppermute | solution.py:563
  20.2 9.2 %collective-permute-done.10.refs_2_ = f32[48,2048]{1,0:T(8,128)S(1)} collective-permute-done((f32[48,2048]{1,0:T(8,128)S(1)}, f32[48,2048]{1,0:T(8,128)S(1)}, u32[]{:S(2)}, u32[]{:S(2)}) %collective-permute-start.10) | collective-permute-done | bytes 393248 | tf_op jit(solution)/shard_map/ppermute | solution.py:563
  29.4 0.0 collective-permute-done.11.refs_3_
  29.4 0.4 collective-permute-done.9.refs_1_
  29.8 3.3 %subsidence.1 = (f32[192,512]{1,0:T(8,128)S(1)}, f32[192,512]{1,0:T(8,128)S(1)}) custom-call(s32[1]{0:T(128)} %bitcast.member_ref, f32[48,2048]{1,0:T(8,128)S(1)} %get-tuple-element.31.refs_0_, f32[48,2048]{1,0:T(8,128)S(1)} %collective-permute-done.9.refs_1_, f32[48,2048]{1,0:T(8,128)S(1)} %collective-permute-done.10.refs_2_, ...), custom_call_target="tpu_custom_call" | custom-call | flops 2415919104 | bytes 9961472 | tf_op jit(solution)/shard_map/subsidence/pallas_call | solution.py:349
  33.1 2.6 %collective-permute-start.12 = (f32[192,512]{1,0:T(8,128)S(1)}, f32[192,512]{1,0:T(8,128)S(1)}, u32[]{:S(2)}, u32[]{:S(2)}) collective-permute-start(f32[192,512]{1,0:T(8,128)S(1)} %get-tuple-element.33), channel_id=1, source_target_pairs={{0,1},{1,0},{2,3},{3,2},{4,5},{5,4},{6,7},{7,6},{8,9},{9,8},{10,11... | collective-permute-start | bytes 1179656 | tf_op jit(solution)/shard_map/ppermute | solution.py:563
  35.7 0.0 collective-permute-done.2
  35.7 4.7 %collective-permute-start.3 = (f32[48,512]{1,0:T(8,128)S(1)}, f32[48,512]{1,0:T(8,128)S(1)}, u32[]{:S(2)}, u32[]{:S(2)}) collective-permute-start(f32[48,512]{1,0:T(8,128)S(1)} %add.47), channel_id=1, source_target_pairs={{0,2},{1,3},{2,0},{3,1},{4,6},{5,7},{6,4},{7,5},{8,10},{9,11},{10,... | collective-permute-start | bytes 294920 | tf_op jit(solution)/shard_map/ppermute | solution.py:563
  40.4 3.4 %collective-permute-done.3 = f32[48,512]{1,0:T(8,128)S(1)} collective-permute-done((f32[48,512]{1,0:T(8,128)S(1)}, f32[48,512]{1,0:T(8,128)S(1)}, u32[]{:S(2)}, u32[]{:S(2)}) %collective-permute-start.3) | collective-permute-done | bytes 98336 | tf_op jit(solution)/shard_map/ppermute | solution.py:563
  43.9 2.8 %collective-permute-start.4 = (f32[48,512]{1,0:T(8,128)S(1)}, f32[48,512]{1,0:T(8,128)S(1)}, u32[]{:S(2)}, u32[]{:S(2)}) collective-permute-start(f32[48,512]{1,0:T(8,128)S(1)} %add.48), channel_id=1, source_target_pairs={{0,4},{1,5},{2,6},{3,7},{4,0},{5,1},{6,2},{7,3},{8,12},{9,13},{10,... | collective-permute-start | bytes 294920 | tf_op jit(solution)/shard_map/ppermute | solution.py:563
  46.7 4.9 %collective-permute-done.4 = f32[48,512]{1,0:T(8,128)S(1)} collective-permute-done((f32[48,512]{1,0:T(8,128)S(1)}, f32[48,512]{1,0:T(8,128)S(1)}, u32[]{:S(2)}, u32[]{:S(2)}) %collective-permute-start.4) | collective-permute-done | bytes 98336 | tf_op jit(solution)/shard_map/ppermute | solution.py:563
  51.6 1.6 %collective-permute-start.5 = (f32[48,512]{1,0:T(8,128)S(1)}, f32[48,512]{1,0:T(8,128)S(1)}, u32[]{:S(2)}, u32[]{:S(2)}) collective-permute-start(f32[48,512]{1,0:T(8,128)S(1)} %add.49.refs_0_), channel_id=1, source_target_pairs={{0,8},{8,0},{16,24},{24,16},{1,9},{9,1},{17,25},{25,17},{2,10},{10... | collective-permute-start | bytes 294920 | tf_op jit(solution)/shard_map/ppermute | solution.py:563
  53.1 1.5 %collective-permute-start.6 = (f32[48,512]{1,0:T(8,128)S(1)}, f32[48,512]{1,0:T(8,128)S(1)}, u32[]{:S(2)}, u32[]{:S(2)}) collective-permute-start(f32[48,512]{1,0:T(8,128)S(1)} %add.49.refs_0_), channel_id=1, source_target_pairs={{0,16},{8,24},{16,0},{24,8},{1,17},{9,25},{17,1},{25,9},{2,18},{10... | collective-permute-start | bytes 294920 | tf_op jit(solution)/shard_map/ppermute | solution.py:563
  54.6 0.5 collective-permute-start.7
  55.1 1.7 %collective-permute-done.5.refs_1_ = f32[48,512]{1,0:T(8,128)S(1)} collective-permute-done((f32[48,512]{1,0:T(8,128)S(1)}, f32[48,512]{1,0:T(8,128)S(1)}, u32[]{:S(2)}, u32[]{:S(2)}) %collective-permute-start.5) | collective-permute-done | bytes 98336 | tf_op jit(solution)/shard_map/ppermute | solution.py:563
  56.8 1.2 %collective-permute-done.6.refs_2_ = f32[48,512]{1,0:T(8,128)S(1)} collective-permute-done((f32[48,512]{1,0:T(8,128)S(1)}, f32[48,512]{1,0:T(8,128)S(1)}, u32[]{:S(2)}, u32[]{:S(2)}) %collective-permute-start.6) | collective-permute-done | bytes 98336 | tf_op jit(solution)/shard_map/ppermute | solution.py:563
  58.0 2.1 %collective-permute-done.7.refs_3_ = f32[48,512]{1,0:T(8,128)S(1)} collective-permute-done((f32[48,512]{1,0:T(8,128)S(1)}, f32[48,512]{1,0:T(8,128)S(1)}, u32[]{:S(2)}, u32[]{:S(2)}) %collective-permute-start.7) | collective-permute-done | bytes 98336 | tf_op jit(solution)/shard_map/ppermute | solution.py:563
  60.1 0.9 %gram.1.gram_ref = f32[192,256]{1,0:T(8,128)S(1)} custom-call(s32[1]{0:T(128)} %bitcast.1.slab_ref, s32[1]{0:T(128)} %bitcast.member_ref, f32[48,512]{1,0:T(8,128)S(1)} %add.49.refs_0_, f32[48,512]{1,0:T(8,128)S(1)} %collective-permute-done.5.refs_1_, f32[48,512]{1,0:T(8,128)S(1)} %collective-permute-done.6.refs_2_, ...), custom_call_target="tpu_custom_call" | custom-call | flops 226492416 | bytes 393216 | tf_op jit(solution)/shard_map/gram/pallas_call | solution.py:396
  61.0 0.1 collective-permute-start.8
  61.1 0.0 collective-permute-done.12
  61.1 0.1 dynamic-slice_add_fusion.2
  61.2 0.1 collective-permute-start.13
  61.3 3.0 %collective-permute-start.14 = (f32[192,128]{1,0:T(8,128)S(1)}, f32[192,128]{1,0:T(8,128)S(1)}, u32[]{:S(2)}, u32[]{:S(2)}) collective-permute-start(f32[192,128]{1,0:T(8,128)S(1)} %get-tuple-element.36), channel_id=1, source_target_pairs={{0,4},{1,5},{2,6},{3,7},{4,0},{5,1},{6,2},{7,3},{8,12},{9,13},{10,... | collective-permute-start | bytes 294920 | tf_op jit(solution)/shard_map/ppermute | solution.py:563
  64.3 1.3 %collective-permute-start.15 = (f32[192,128]{1,0:T(8,128)S(1)}, f32[192,128]{1,0:T(8,128)S(1)}, u32[]{:S(2)}, u32[]{:S(2)}) collective-permute-start(f32[192,128]{1,0:T(8,128)S(1)} %get-tuple-element.35), channel_id=1, source_target_pairs={{0,6},{1,7},{2,4},{3,5},{4,2},{5,3},{6,0},{7,1},{8,14},{9,15},{10,... | collective-permute-start | bytes 294920 | tf_op jit(solution)/shard_map/ppermute | solution.py:563
  65.7 0.0 collective-permute-done.8.more_ref
  65.7 5.9 %finish.1 = f32[48,16,128]{2,1,0:T(8,128)} custom-call(s32[1]{0:T(128)} %bitcast.member_ref, f32[192,256]{1,0:T(8,128)S(1)} %gram.1.gram_ref, f32[192,256]{1,0:T(8,128)S(1)} %collective-permute-done.8.more_ref, f32[48,2048]{1,0:T(8,128)S(1)} %get-tuple-element.31.refs_0_, f32[48,2048]{1,0:T(8,128)S(1)} %collective-permute-done.9.refs_1_, ...), custom_call_target="tpu_custom_call" | custom-call | flops 113246208 | bytes 1572864 | tf_op jit(solution)/shard_map/finish/pallas_call | solution.py:536
  71.6 0.0 collective-permute-done.13
  71.6 0.6 collective-permute-done.14
  72.2 0.0 collective-permute-done.15
  72.2 0.7 add_bitcast_fusion
  (3 shorter events, 0.0 us)
Async XLA Ops:
  2.0 4.5 %collective-permute-start = (f32[4,104,128]{2,1,0:T(8,128)S(1)}, f32[4,104,128]{2,1,0:T(8,128)S(1)}, u32[]{:S(2)}, u32[]{:S(2)}) collective-permute-start(f32[4,104,128]{2,1,0:T(8,128)S(1)} %get-tuple-element.24), channel_id=1, source_target_pairs={{0,1},{1,0},{2,3},{3,2},{4,5},{5,4},{6,7},{7,6},{8,9},{9,8},{10,11... | collective-permute-start | bytes 638984 | tf_op jit(solution)/shard_map/ppermute | solution.py:571
  2.5 3.9 %collective-permute-start.1 = (f32[4,104,128]{2,1,0:T(8,128)S(1)}, f32[4,104,128]{2,1,0:T(8,128)S(1)}, u32[]{:S(2)}, u32[]{:S(2)}) collective-permute-start(f32[4,104,128]{2,1,0:T(8,128)S(1)} %get-tuple-element.25), channel_id=1, source_target_pairs={{1,2},{3,4},{5,6},{2,1},{4,3},{6,5},{9,10},{11,12},{13,14},{10,9},... | collective-permute-start | bytes 638984 | tf_op jit(solution)/shard_map/ppermute | solution.py:570
  10.0 19.4 %collective-permute-start.10 = (f32[48,2048]{1,0:T(8,128)S(1)}, f32[48,2048]{1,0:T(8,128)S(1)}, u32[]{:S(2)}, u32[]{:S(2)}) collective-permute-start(f32[48,2048]{1,0:T(8,128)S(1)} %get-tuple-element.31.refs_0_), channel_id=1, source_target_pairs={{0,16},{8,24},{16,0},{24,8},{1,17},{9,25},{17,1},{25,9},{2,18},{10... | collective-permute-start | bytes 1179656 | tf_op jit(solution)/shard_map/ppermute | solution.py:563
  12.5 16.9 %collective-permute-start.11 = (f32[48,2048]{1,0:T(8,128)S(1)}, f32[48,2048]{1,0:T(8,128)S(1)}, u32[]{:S(2)}, u32[]{:S(2)}) collective-permute-start(f32[48,2048]{1,0:T(8,128)S(1)} %get-tuple-element.31.refs_0_), channel_id=1, source_target_pairs={{0,24},{8,16},{16,8},{24,0},{1,25},{9,17},{17,9},{25,1},{2,26},{10... | collective-permute-start | bytes 1179656 | tf_op jit(solution)/shard_map/ppermute | solution.py:563
  14.0 15.9 %collective-permute-start.9 = (f32[48,2048]{1,0:T(8,128)S(1)}, f32[48,2048]{1,0:T(8,128)S(1)}, u32[]{:S(2)}, u32[]{:S(2)}) collective-permute-start(f32[48,2048]{1,0:T(8,128)S(1)} %get-tuple-element.31.refs_0_), channel_id=1, source_target_pairs={{0,8},{8,0},{16,24},{24,16},{1,9},{9,1},{17,25},{25,17},{2,10},{10... | collective-permute-start | bytes 1179656 | tf_op jit(solution)/shard_map/ppermute | solution.py:563
  17.0 18.7 %collective-permute-start.2 = (f32[48,512]{1,0:T(8,128)S(1)}, f32[48,512]{1,0:T(8,128)S(1)}, u32[]{:S(2)}, u32[]{:S(2)}) collective-permute-start(f32[48,512]{1,0:T(8,128)S(1)} %get-tuple-element.28), channel_id=1, source_target_pairs={{0,1},{1,0},{2,3},{3,2},{4,5},{5,4},{6,7},{7,6},{8,9},{9,8},{10,11... | collective-permute-start | bytes 294920 | tf_op jit(solution)/shard_map/ppermute | solution.py:563
  33.1 28.0 %collective-permute-start.12 = (f32[192,512]{1,0:T(8,128)S(1)}, f32[192,512]{1,0:T(8,128)S(1)}, u32[]{:S(2)}, u32[]{:S(2)}) collective-permute-start(f32[192,512]{1,0:T(8,128)S(1)} %get-tuple-element.33), channel_id=1, source_target_pairs={{0,1},{1,0},{2,3},{3,2},{4,5},{5,4},{6,7},{7,6},{8,9},{9,8},{10,11... | collective-permute-start | bytes 1179656 | tf_op jit(solution)/shard_map/ppermute | solution.py:563
  35.7 8.2 %collective-permute-start.3 = (f32[48,512]{1,0:T(8,128)S(1)}, f32[48,512]{1,0:T(8,128)S(1)}, u32[]{:S(2)}, u32[]{:S(2)}) collective-permute-start(f32[48,512]{1,0:T(8,128)S(1)} %add.47), channel_id=1, source_target_pairs={{0,2},{1,3},{2,0},{3,1},{4,6},{5,7},{6,4},{7,5},{8,10},{9,11},{10,... | collective-permute-start | bytes 294920 | tf_op jit(solution)/shard_map/ppermute | solution.py:563
  43.9 7.7 %collective-permute-start.4 = (f32[48,512]{1,0:T(8,128)S(1)}, f32[48,512]{1,0:T(8,128)S(1)}, u32[]{:S(2)}, u32[]{:S(2)}) collective-permute-start(f32[48,512]{1,0:T(8,128)S(1)} %add.48), channel_id=1, source_target_pairs={{0,4},{1,5},{2,6},{3,7},{4,0},{5,1},{6,2},{7,3},{8,12},{9,13},{10,... | collective-permute-start | bytes 294920 | tf_op jit(solution)/shard_map/ppermute | solution.py:563
  51.6 5.2 %collective-permute-start.5 = (f32[48,512]{1,0:T(8,128)S(1)}, f32[48,512]{1,0:T(8,128)S(1)}, u32[]{:S(2)}, u32[]{:S(2)}) collective-permute-start(f32[48,512]{1,0:T(8,128)S(1)} %add.49.refs_0_), channel_id=1, source_target_pairs={{0,8},{8,0},{16,24},{24,16},{1,9},{9,1},{17,25},{25,17},{2,10},{10... | collective-permute-start | bytes 294920 | tf_op jit(solution)/shard_map/ppermute | solution.py:563
  53.1 4.9 %collective-permute-start.6 = (f32[48,512]{1,0:T(8,128)S(1)}, f32[48,512]{1,0:T(8,128)S(1)}, u32[]{:S(2)}, u32[]{:S(2)}) collective-permute-start(f32[48,512]{1,0:T(8,128)S(1)} %add.49.refs_0_), channel_id=1, source_target_pairs={{0,16},{8,24},{16,0},{24,8},{1,17},{9,25},{17,1},{25,9},{2,18},{10... | collective-permute-start | bytes 294920 | tf_op jit(solution)/shard_map/ppermute | solution.py:563
  54.6 5.5 %collective-permute-start.7 = (f32[48,512]{1,0:T(8,128)S(1)}, f32[48,512]{1,0:T(8,128)S(1)}, u32[]{:S(2)}, u32[]{:S(2)}) collective-permute-start(f32[48,512]{1,0:T(8,128)S(1)} %add.49.refs_0_), channel_id=1, source_target_pairs={{0,24},{8,16},{16,8},{24,0},{1,25},{9,17},{17,9},{25,1},{2,26},{10... | collective-permute-start | bytes 294920 | tf_op jit(solution)/shard_map/ppermute | solution.py:563
  61.0 4.6 %collective-permute-start.8 = (f32[192,256]{1,0:T(8,128)S(1)}, f32[192,256]{1,0:T(8,128)S(1)}, u32[]{:S(2)}, u32[]{:S(2)}) collective-permute-start(f32[192,256]{1,0:T(8,128)S(1)} %gram.1.gram_ref), channel_id=1, source_target_pairs={{0,1},{1,0},{2,3},{3,2},{4,5},{5,4},{6,7},{7,6},{8,9},{9,8},{10,11... | collective-permute-start | bytes 589832 | tf_op jit(solution)/shard_map/ppermute | solution.py:563
  61.2 10.4 %collective-permute-start.13 = (f32[192,128]{1,0:T(8,128)S(1)}, f32[192,128]{1,0:T(8,128)S(1)}, u32[]{:S(2)}, u32[]{:S(2)}) collective-permute-start(f32[192,128]{1,0:T(8,128)S(1)} %get-tuple-element.34), channel_id=1, source_target_pairs={{0,2},{1,3},{2,0},{3,1},{4,6},{5,7},{6,4},{7,5},{8,10},{9,11},{10,... | collective-permute-start | bytes 294920 | tf_op jit(solution)/shard_map/ppermute | solution.py:563
  61.3 10.9 %collective-permute-start.14 = (f32[192,128]{1,0:T(8,128)S(1)}, f32[192,128]{1,0:T(8,128)S(1)}, u32[]{:S(2)}, u32[]{:S(2)}) collective-permute-start(f32[192,128]{1,0:T(8,128)S(1)} %get-tuple-element.36), channel_id=1, source_target_pairs={{0,4},{1,5},{2,6},{3,7},{4,0},{5,1},{6,2},{7,3},{8,12},{9,13},{10,... | collective-permute-start | bytes 294920 | tf_op jit(solution)/shard_map/ppermute | solution.py:563
  64.3 7.9 %collective-permute-start.15 = (f32[192,128]{1,0:T(8,128)S(1)}, f32[192,128]{1,0:T(8,128)S(1)}, u32[]{:S(2)}, u32[]{:S(2)}) collective-permute-start(f32[192,128]{1,0:T(8,128)S(1)} %get-tuple-element.35), channel_id=1, source_target_pairs={{0,6},{1,7},{2,4},{3,5},{4,2},{5,3},{6,0},{7,1},{8,14},{9,15},{10,... | collective-permute-start | bytes 294920 | tf_op jit(solution)/shard_map/ppermute | solution.py:563

commit v6 on v5

--- a/solution.py
+++ b/solution.py
@@ -290,18 +290,20 @@
             other_ref[:, first - half : first - half + wide] = value
 
 
-def forecast_kernel(slabs, slab_ref, start_ref, perm_ref, wells_ref, near_ref, far_ref, kernel_ref, cast_ref, own_ref, other_ref, p_ref, rim_ref, left_ref):
+def forecast_kernel(slabs, slab_ref, start_ref, perm_ref, wells_ref, near_ref, far_ref, kernel_ref, first_ref, second_ref, own_ref, other_ref, p_ref, rim_ref, left_ref):
     rows, members, cells = start_ref.shape
-    padded = cast_ref.shape[0]
+    padded = first_ref.shape[0]
     forecast_steps(slab_ref[0], slabs, start_ref, perm_ref, wells_ref, near_ref, far_ref, p_ref, rim_ref)
     if padded != members:
-        cast_ref[...] = jnp.zeros_like(cast_ref)
+        first_ref[...] = jnp.zeros_like(first_ref)
+        second_ref[...] = jnp.zeros_like(second_ref)
         left_ref[...] = jnp.zeros_like(left_ref)
     for i in range(rows):
         value = p_ref[STEPS + i]
         high, low = split(value)
         lane = slice(i * cells, (i + 1) * cells)
-        cast_ref[0:members, lane] = value
+        part_ref, row = (first_ref, i) if i < rows // 2 else (second_ref, i - rows // 2)
+        part_ref[0:members, row * cells : (row + 1) * cells] = value
         left_ref[0:members, lane] = high
         left_ref[padded : padded + members, lane] = low
     spread_product(left_ref, padded, kernel_ref, own_ref, other_ref)
@@ -313,9 +315,9 @@
     half = jax.ShapeDtypeStruct((padded, observed // 2), F32)
     return pl.pallas_call(
         functools.partial(forecast_kernel, slabs),
-        out_shape=(jax.ShapeDtypeStruct((padded, total), F32), half, half),
+        out_shape=(jax.ShapeDtypeStruct((padded, total // 2), F32),) * 2 + (half, half),
         in_specs=[SMEM] + [VMEM] * 6,
-        out_specs=(VMEM,) * 3,
+        out_specs=(VMEM,) * 4,
         scratch_shapes=[
             pltpu.VMEM((rows + 2 * STEPS, members, cells), F32),
             pltpu.VMEM((2 * STEPS, members, cells), F32),
@@ -327,35 +329,40 @@
     )(slab, start, perm, wells, near, far, kernel)
 
 
-def subsidence_kernel(groups, member_ref, *refs):
-    pieces = refs[:groups]
-    kernel_ref, own_ref, other_ref, left_ref = refs[groups:]
-    padded, _ = pieces[0].shape
-    every = groups * padded
-    for offset in range(groups):
+def pieces_of(plan, arrays, padded):
+    for offset, halves in enumerate(plan):
+        for which, (index, first) in enumerate(halves):
+            yield offset, which, arrays[index][first : first + padded, :]
+
+
+def subsidence_kernel(plan, padded, member_ref, *refs):
+    arrays = refs[:-4]
+    kernel_ref, own_ref, other_ref, left_ref = refs[-4:]
+    every = len(plan) * padded
+    width = arrays[0].shape[1]
+    for offset, which, piece in pieces_of(plan, arrays, padded):
         at = member_ref[0] ^ offset
-        high, low = split(pieces[offset][...])
-        left_ref[pl.ds(pl.multiple_of(at * padded, padded), padded), :] = high
-        left_ref[pl.ds(pl.multiple_of(every + at * padded, padded), padded), :] = low
+        high, low = split(piece)
+        lane = slice(which * width, (which + 1) * width)
+        left_ref[pl.ds(pl.multiple_of(at * padded, padded), padded), lane] = high
+        left_ref[pl.ds(pl.multiple_of(every + at * padded, padded), padded), lane] = low
     spread_product(left_ref, every, kernel_ref, own_ref, other_ref)
 
 
-def subsidence_partial(member, pieces, kernel):
-    groups = len(pieces)
-    padded, total = pieces[0].shape
-    pixels = kernel.shape[1]
-    every = groups * padded
+def subsidence_partial(plan, padded, member, arrays, kernel):
+    total, pixels = kernel.shape
+    every = len(plan) * padded
     out = jax.ShapeDtypeStruct((every, pixels // 2), F32)
     return pl.pallas_call(
-        functools.partial(subsidence_kernel, groups),
+        functools.partial(subsidence_kernel, plan, padded),
         out_shape=(out, out),
-        in_specs=[SMEM] + [VMEM] * (groups + 1),
+        in_specs=[SMEM] + [VMEM] * (len(arrays) + 1),
         out_specs=(VMEM,) * 2,
         scratch_shapes=[pltpu.VMEM((2 * every, total), BF16)],
         compiler_params=params(24),
         cost_estimate=cost(6 * every * total * pixels, 4 * total * pixels + 4 * every * total),
         name="subsidence",
-    )(member, *pieces, kernel)
+    )(member, *arrays, kernel)
 
 
 def gram_kernel(groups, members, slab_ref, member_ref, *refs):
@@ -486,19 +493,21 @@
             work_ref[below:every, :] = old - product[below - base :]
 
 
-def finish_kernel(groups, members, member_ref, gram_ref, more_ref, *refs):
-    pieces = refs[:groups]
-    out_ref, cast_ref, work_ref = refs[groups:]
-    padded, total = pieces[0].shape
+def finish_kernel(plan, padded, members, member_ref, gram_ref, more_ref, *refs):
+    groups = len(plan)
+    arrays = refs[:-3]
+    out_ref, cast_ref, work_ref = refs[-3:]
+    total = cast_ref.shape[2]
     rows, cells = out_ref.shape[1:]
     every, width = work_ref.shape
     count = groups * members
     member = member_ref[0]
-    for offset in range(groups):
+    for offset, which, piece in pieces_of(plan, arrays, padded):
         at = member ^ offset
-        high, low = split(pieces[offset][...])
-        cast_ref[at] = high
-        cast_ref[groups + at] = low
+        high, low = split(piece)
+        lane = slice(which * (total // 2), (which + 1) * (total // 2))
+        cast_ref[at, :, lane] = high
+        cast_ref[groups + at, :, lane] = low
     row = lax.broadcasted_iota(jnp.int32, (every, width), 0)
     column = lax.broadcasted_iota(jnp.int32, (every, width), 1)
     work_ref[...] = gram_ref[...] + more_ref[...] + jnp.where(row == column, count - 1.0, 0.0)
@@ -530,19 +539,19 @@
             out_ref[:, lane // cells + part, :] = value[:members, part * cells : (part + 1) * cells]
 
 
-def finish(members, rows, cells, member, gram, more, pieces):
-    groups = len(pieces)
-    padded, total = pieces[0].shape
+def finish(plan, padded, members, rows, cells, member, gram, more, arrays):
+    groups = len(plan)
+    total = rows * cells
     return pl.pallas_call(
-        functools.partial(finish_kernel, groups, members),
+        functools.partial(finish_kernel, plan, padded, members),
         out_shape=jax.ShapeDtypeStruct((members, rows, cells), F32),
-        in_specs=[SMEM] + [VMEM] * (groups + 2),
+        in_specs=[SMEM] + [VMEM] * (len(arrays) + 2),
         out_specs=VMEM,
         scratch_shapes=[pltpu.VMEM((2 * groups, padded, total), BF16), pltpu.VMEM(gram.shape, F32)],
         compiler_params=params(),
         cost_estimate=cost(6 * padded * groups * padded * total, 4 * groups * padded * total),
         name="finish",
-    )(member, gram, more, *pieces)
+    )(member, gram, more, *arrays)
 
 
 def cycle(head, perm, wells, layer, coords, obs_index, obs_value, obs_sigma):
@@ -571,9 +580,19 @@
     near = lax.ppermute(near, "slab", pair)
 
     kernel, start, perm_rows = kernel_of_observed(total_rows, slab_s, coords, index, layer, head, perm)
-    cast, own, other = forecast(slabs, padded, slab_s, start, perm_rows, wells, near, far, kernel)
+    first, second, own, other = forecast(slabs, padded, slab_s, start, perm_rows, wells, near, far, kernel)
     seen = own + swap(other, "slab", 1)
-    pieces = [cast] + [swap(cast, "member", offset) for offset in range(1, groups)]
+    if groups == 4:
+        across_first = swap(first, "member", 1)
+        along_second = swap(second, "member", 2)
+        far_first = swap(jnp.concatenate([first, across_first], 0), "member", 2)
+        far_second = swap(jnp.concatenate([second, along_second], 0), "member", 1)
+        arrays = (first, second, across_first, along_second, far_first, far_second)
+        plan = (((0, 0), (1, 0)), ((2, 0), (5, 0)), ((4, 0), (3, 0)), ((4, padded), (5, padded)))
+    else:
+        both = jnp.concatenate([first, second], 0)
+        arrays = (both,) + tuple(swap(both, "member", k) for k in range(1, groups))
+        plan = tuple(((k, 0), (k, padded)) for k in range(groups))
     offset = 2
     while offset < slabs:
         seen = seen + swap(seen, "slab", offset)
@@ -585,7 +604,7 @@
     chips = slabs // 2
     own_rows = coords.shape[1] // (groups * slabs)
     kernel_all = kernel_of_pixels(total_rows, groups, slab_s, member_s, coords, layer)
-    sunk, sunk_other = subsidence_partial(member_s, pieces, kernel_all)
+    sunk, sunk_other = subsidence_partial(plan, padded, member_s, arrays, kernel_all)
     sunk_recv = swap(sunk_other, "slab", 1)
     chip = slab // 2
 
@@ -602,7 +621,7 @@
         sunk_own = sunk_own.reshape(groups, padded, own_rows)[:, :members].reshape(groups * members, own_rows)
     subsidence = sunk_own.T
 
-    analysed = finish(members, rows, cells, member_s, gram, gram_more, pieces)
+    analysed = finish(plan, padded, members, rows, cells, member_s, gram, gram_more, arrays)
     return (analysed, subsidence)
 
 

time: 73.1 us -> 70.3 us (0.962)
  waiting for transfers between devices: 23.6 us -> 18.5 us
  starting transfers between devices: 26.6 us -> 29 us
    ppermute x14 -> x15, waiting for transfers between devices: 23.6 us -> 18.5 us  [swap(): return lax.ppermute(value, axis, [(i, i ^ offset) for i in range(size)])]
    ppermute x14 -> x15, starting transfers between devices: 25.4 us -> 27.8 us  [swap(): return lax.ppermute(value, axis, [(i, i ^ offset) for i in range(size)])]
  transfers between devices with their start and end apart: 16 -> 17, of which waited for: 8 -> 9; matrix products, arithmetic and copies ran while one was open for 0% -> 0% of each run, Pallas kernels for 22% -> 23%
where the time goes in v6:
time: 70.3 us; the launch traced here: 70.1 us
  starting transfers between devices  29 us (41%)
  Pallas kernels  20.9 us (30%)
  waiting for transfers between devices  18.5 us (26%)
  other arithmetic  0.87 us (1%)
  between operations  0.76 us (1%)
    ppermute x15, starting transfers between devices, swap(): return lax.ppermute(value, axis, [(i, i ^ offset) for i in range(size)])  27.8 us
    ppermute x15, waiting for transfers between devices, swap(): return lax.ppermute(value, axis, [(i, i ^ offset) for i in range(size)])  18.5 us
    pallas_call x1, Pallas kernels, finish(): pl.pallas_call(functools.partial(finish_kernel, plan, padded, members), o...  5.88 us
    pallas_call x1, Pallas kernels, forecast(): pl.pallas_call(functools.partial(forecast_kernel, slabs), out_shape=(jax....  3.53 us
    pallas_call x1, Pallas kernels, kernel_of_observed(): pl.pallas_call(functools.partial(observed_kernel, total_rows), out_shape=...  3.25 us
    pallas_call x1, Pallas kernels, subsidence_partial(): pl.pallas_call(functools.partial(subsidence_kernel, plan, padded), out_sh...  3.18 us
    pallas_call x1, Pallas kernels, kernel_of_pixels(): pl.pallas_call(functools.partial(pixel_kernel, total_rows, chips, own_row...  2.89 us
  transfers between devices with their start and end apart: 17, of which 9 were waited for; matrix products, arithmetic and copies ran while one was open for 0% of the time, Pallas kernels for 23%

profile of v6, /device:TPU:0, one launch (start us, length us, event | category | flops | bytes accessed | tf_op | source)
XLA Modules:
  0.0 70.1 jit_solution(12466564341717966412)
XLA Ops:
  0.6 1.3 %pack_rims.1 = (f32[4,104,128]{2,1,0:T(8,128)S(1)}, f32[4,104,128]{2,1,0:T(8,128)S(1)}, f32[16,128]{1,0:T(8,128)S(1)}, s32[16,128]{1,0:T(8,128)S(1)}, s32[2,4096...) custom-call(s32[1]{0:T(128)} %bitcast.1.slab_ref, f32[48,16,128]{2,1,0:T(8,128)} %head_ref.3, ...), custom_call_target="tpu_custom_call" | custom-call | tf_op jit(solution)/shard_map/pack_rims/pallas_call | solution.py:76
  2.0 0.6 collective-permute-start
  2.5 0.7 collective-permute-start.1
  3.2 3.3 %kernel_of_observed.1 = (f32[2048,1024]{1,0:T(8,128)S(1)}, f32[16,48,128]{2,1,0:T(8,128)S(1)}, f32[16,48,128]{2,1,0:T(8,128)S(1)}) custom-call(s32[1]{0:T(128)} %bitcast.1.slab_ref, s32[2,4096]{1,0:T(2,128)S(1)} %get-tuple-element.19.coords_ref, s32[8,128]{1,0:T(8,128)S(1)} %get-tuple-element.20.index_ref, s32[16,128]{1,0:T(8,128)S(1)} %get-tuple-element.21.layer_ref, ...), custom_call_target="tpu_custom_call" | custom-call | flops 33554432 | bytes 8388608 | tf_op jit(solution)/shard_map/kernel_of_observed/pallas_call | solution.py:151
  6.4 0.0 collective-permute-done.near_ref
  6.5 0.0 collective-permute-done.1.far_ref
  6.5 3.5 %forecast.1 = (f32[48,1024]{1,0:T(8,128)S(1)}, f32[48,1024]{1,0:T(8,128)S(1)}, f32[48,512]{1,0:T(8,128)S(1)}, f32[48,512]{1,0:T(8,128)S(1)}) custom-call(s32[1]{0:T(128)} %bitcast.1.slab_ref, f32[16,48,128]{2,1,0:T(8,128)S(1)} %get-tuple-element.22.start_ref, f32[16,48,128]{2,1,0:T(8,128)S(1)} %get-tuple-element.23.perm_ref, ...), custom_call_target="tpu_custom_call" | custom-call | flops 603979776 | bytes 8388608 | tf_op jit(solution)/shard_map/forecast/pallas_call | solution.py:316
  10.0 2.5 %collective-permute-start.10 = (f32[48,1024]{1,0:T(8,128)S(1)}, f32[48,1024]{1,0:T(8,128)S(1)}, u32[]{:S(2)}, u32[]{:S(2)}) collective-permute-start(f32[48,1024]{1,0:T(8,128)S(1)} %get-tuple-element.33.refs_1_), channel_id=1, source_target_pairs={{0,16},{8,24},{16,0},{24,8},{1,17},{9,25},{17,1},{25,9},{2,18},{10... | collective-permute-start | bytes 589832 | tf_op jit(solution)/shard_map/ppermute | solution.py:572
  12.5 1.5 %collective-permute-start.9 = (f32[48,1024]{1,0:T(8,128)S(1)}, f32[48,1024]{1,0:T(8,128)S(1)}, u32[]{:S(2)}, u32[]{:S(2)}) collective-permute-start(f32[48,1024]{1,0:T(8,128)S(1)} %get-tuple-element.32.refs_0_), channel_id=1, source_target_pairs={{0,8},{8,0},{16,24},{24,16},{1,9},{9,1},{17,25},{25,17},{2,10},{10... | collective-permute-start | bytes 589832 | tf_op jit(solution)/shard_map/ppermute | solution.py:572
  14.0 2.2 %collective-permute-done.10.refs_3_ = f32[48,1024]{1,0:T(8,128)S(1)} collective-permute-done((f32[48,1024]{1,0:T(8,128)S(1)}, f32[48,1024]{1,0:T(8,128)S(1)}, u32[]{:S(2)}, u32[]{:S(2)}) %collective-permute-start.10) | collective-permute-done | bytes 196640 | tf_op jit(solution)/shard_map/ppermute | solution.py:572
  16.2 2.1 %collective-permute-start.12 = (f32[96,1024]{1,0:T(8,128)S(1)}, f32[96,1024]{1,0:T(8,128)S(1)}, u32[]{:S(2)}, u32[]{:S(2)}) collective-permute-start(f32[96,1024]{1,0:T(8,128)S(1)} %pad_maximum_fusion.1), channel_id=1, source_target_pairs={{0,8},{8,0},{16,24},{24,16},{1,9},{9,1},{17,25},{25,17},{2,10},{10... | collective-permute-start | bytes 1179656 | tf_op jit(solution)/shard_map/ppermute | solution.py:572
  18.3 0.0 collective-permute-done.9.refs_2_
  18.3 1.6 %collective-permute-start.11 = (f32[96,1024]{1,0:T(8,128)S(1)}, f32[96,1024]{1,0:T(8,128)S(1)}, u32[]{:S(2)}, u32[]{:S(2)}) collective-permute-start(f32[96,1024]{1,0:T(8,128)S(1)} %pad_maximum_fusion), channel_id=1, source_target_pairs={{0,16},{8,24},{16,0},{24,8},{1,17},{9,25},{17,1},{25,9},{2,18},{10... | collective-permute-start | bytes 1179656 | tf_op jit(solution)/shard_map/ppermute | solution.py:572
  19.9 2.9 %kernel_of_pixels.1.refs_6_ = f32[2048,1024]{1,0:T(8,128)S(1)} custom-call(s32[1]{0:T(128)} %bitcast.1.slab_ref, s32[1]{0:T(128)} %bitcast.member_ref, s32[2,4096]{1,0:T(2,128)S(1)} %get-tuple-element.19.coords_ref, s32[16,128]{1,0:T(8,128)S(1)} %get-tuple-element.21.layer_ref), custom_call_target="tpu_custom_call" | custom-call | flops 33554432 | bytes 8388608 | tf_op jit(solution)/shard_map/kernel_of_pixels/pallas_call | solution.py:196
  22.8 2.0 %collective-permute-start.2 = (f32[48,512]{1,0:T(8,128)S(1)}, f32[48,512]{1,0:T(8,128)S(1)}, u32[]{:S(2)}, u32[]{:S(2)}) collective-permute-start(f32[48,512]{1,0:T(8,128)S(1)} %get-tuple-element.29), channel_id=1, source_target_pairs={{0,1},{1,0},{2,3},{3,2},{4,5},{5,4},{6,7},{7,6},{8,9},{9,8},{10,11... | collective-permute-start | bytes 294920 | tf_op jit(solution)/shard_map/ppermute | solution.py:572
  24.8 3.2 %collective-permute-done.12.refs_5_ = f32[96,1024]{1,0:T(8,128)S(1)} collective-permute-done((f32[96,1024]{1,0:T(8,128)S(1)}, f32[96,1024]{1,0:T(8,128)S(1)}, u32[]{:S(2)}, u32[]{:S(2)}) %collective-permute-start.12) | collective-permute-done | bytes 393248 | tf_op jit(solution)/shard_map/ppermute | solution.py:572
  28.0 0.1 collective-permute-done.11.refs_4_
  28.1 3.2 %subsidence.1 = (f32[192,512]{1,0:T(8,128)S(1)}, f32[192,512]{1,0:T(8,128)S(1)}) custom-call(s32[1]{0:T(128)} %bitcast.member_ref, f32[48,1024]{1,0:T(8,128)S(1)} %get-tuple-element.32.refs_0_, f32[48,1024]{1,0:T(8,128)S(1)} %get-tuple-element.33.refs_1_, f32[48,1024]{1,0:T(8,128)S(1)} %collective-permute-done.9.refs_2_, ...), custom_call_target="tpu_custom_call" | custom-call | flops 2415919104 | bytes 9961472 | tf_op jit(solution)/shard_map/subsidence/pallas_call | solution.py:356
  31.3 2.1 %collective-permute-start.13 = (f32[192,512]{1,0:T(8,128)S(1)}, f32[192,512]{1,0:T(8,128)S(1)}, u32[]{:S(2)}, u32[]{:S(2)}) collective-permute-start(f32[192,512]{1,0:T(8,128)S(1)} %get-tuple-element.35), channel_id=1, source_target_pairs={{0,1},{1,0},{2,3},{3,2},{4,5},{5,4},{6,7},{7,6},{8,9},{9,8},{10,11... | collective-permute-start | bytes 1179656 | tf_op jit(solution)/shard_map/ppermute | solution.py:572
  33.4 0.0 collective-permute-done.2
  33.5 5.0 %collective-permute-start.3 = (f32[48,512]{1,0:T(8,128)S(1)}, f32[48,512]{1,0:T(8,128)S(1)}, u32[]{:S(2)}, u32[]{:S(2)}) collective-permute-start(f32[48,512]{1,0:T(8,128)S(1)} %add.47), channel_id=1, source_target_pairs={{0,2},{1,3},{2,0},{3,1},{4,6},{5,7},{6,4},{7,5},{8,10},{9,11},{10,... | collective-permute-start | bytes 294920 | tf_op jit(solution)/shard_map/ppermute | solution.py:572
  38.5 3.4 %collective-permute-done.3 = f32[48,512]{1,0:T(8,128)S(1)} collective-permute-done((f32[48,512]{1,0:T(8,128)S(1)}, f32[48,512]{1,0:T(8,128)S(1)}, u32[]{:S(2)}, u32[]{:S(2)}) %collective-permute-start.3) | collective-permute-done | bytes 98336 | tf_op jit(solution)/shard_map/ppermute | solution.py:572
  42.0 2.8 %collective-permute-start.4 = (f32[48,512]{1,0:T(8,128)S(1)}, f32[48,512]{1,0:T(8,128)S(1)}, u32[]{:S(2)}, u32[]{:S(2)}) collective-permute-start(f32[48,512]{1,0:T(8,128)S(1)} %add.48), channel_id=1, source_target_pairs={{0,4},{1,5},{2,6},{3,7},{4,0},{5,1},{6,2},{7,3},{8,12},{9,13},{10,... | collective-permute-start | bytes 294920 | tf_op jit(solution)/shard_map/ppermute | solution.py:572
  44.8 4.9 %collective-permute-done.4 = f32[48,512]{1,0:T(8,128)S(1)} collective-permute-done((f32[48,512]{1,0:T(8,128)S(1)}, f32[48,512]{1,0:T(8,128)S(1)}, u32[]{:S(2)}, u32[]{:S(2)}) %collective-permute-start.4) | collective-permute-done | bytes 98336 | tf_op jit(solution)/shard_map/ppermute | solution.py:572
  49.7 1.2 %collective-permute-start.5 = (f32[48,512]{1,0:T(8,128)S(1)}, f32[48,512]{1,0:T(8,128)S(1)}, u32[]{:S(2)}, u32[]{:S(2)}) collective-permute-start(f32[48,512]{1,0:T(8,128)S(1)} %add.49.refs_0_), channel_id=1, source_target_pairs={{0,8},{8,0},{16,24},{24,16},{1,9},{9,1},{17,25},{25,17},{2,10},{10... | collective-permute-start | bytes 294920 | tf_op jit(solution)/shard_map/ppermute | solution.py:572
  50.9 0.9 %collective-permute-start.6 = (f32[48,512]{1,0:T(8,128)S(1)}, f32[48,512]{1,0:T(8,128)S(1)}, u32[]{:S(2)}, u32[]{:S(2)}) collective-permute-start(f32[48,512]{1,0:T(8,128)S(1)} %add.49.refs_0_), channel_id=1, source_target_pairs={{0,16},{8,24},{16,0},{24,8},{1,17},{9,25},{17,1},{25,9},{2,18},{10... | collective-permute-start | bytes 294920 | tf_op jit(solution)/shard_map/ppermute | solution.py:572
  51.8 1.4 %collective-permute-start.7 = (f32[48,512]{1,0:T(8,128)S(1)}, f32[48,512]{1,0:T(8,128)S(1)}, u32[]{:S(2)}, u32[]{:S(2)}) collective-permute-start(f32[48,512]{1,0:T(8,128)S(1)} %add.49.refs_0_), channel_id=1, source_target_pairs={{0,24},{8,16},{16,8},{24,0},{1,25},{9,17},{17,9},{25,1},{2,26},{10... | collective-permute-start | bytes 294920 | tf_op jit(solution)/shard_map/ppermute | solution.py:572
  53.2 1.3 %collective-permute-done.5.refs_1_ = f32[48,512]{1,0:T(8,128)S(1)} collective-permute-done((f32[48,512]{1,0:T(8,128)S(1)}, f32[48,512]{1,0:T(8,128)S(1)}, u32[]{:S(2)}, u32[]{:S(2)}) %collective-permute-start.5) | collective-permute-done | bytes 98336 | tf_op jit(solution)/shard_map/ppermute | solution.py:572
  54.5 0.9 %collective-permute-done.6.refs_2_ = f32[48,512]{1,0:T(8,128)S(1)} collective-permute-done((f32[48,512]{1,0:T(8,128)S(1)}, f32[48,512]{1,0:T(8,128)S(1)}, u32[]{:S(2)}, u32[]{:S(2)}) %collective-permute-start.6) | collective-permute-done | bytes 98336 | tf_op jit(solution)/shard_map/ppermute | solution.py:572
  55.5 1.8 %collective-permute-done.7.refs_3_ = f32[48,512]{1,0:T(8,128)S(1)} collective-permute-done((f32[48,512]{1,0:T(8,128)S(1)}, f32[48,512]{1,0:T(8,128)S(1)}, u32[]{:S(2)}, u32[]{:S(2)}) %collective-permute-start.7) | collective-permute-done | bytes 98336 | tf_op jit(solution)/shard_map/ppermute | solution.py:572
  57.3 0.9 %gram.1.gram_ref = f32[192,256]{1,0:T(8,128)S(1)} custom-call(s32[1]{0:T(128)} %bitcast.1.slab_ref, s32[1]{0:T(128)} %bitcast.member_ref, f32[48,512]{1,0:T(8,128)S(1)} %add.49.refs_0_, f32[48,512]{1,0:T(8,128)S(1)} %collective-permute-done.5.refs_1_, f32[48,512]{1,0:T(8,128)S(1)} %collective-permute-done.6.refs_2_, ...), custom_call_target="tpu_custom_call" | custom-call | flops 226492416 | bytes 393216 | tf_op jit(solution)/shard_map/gram/pallas_call | solution.py:403
  58.2 0.1 collective-permute-start.8
  58.3 0.0 collective-permute-done.13
  58.3 0.1 dynamic-slice_add_fusion.2
  58.4 0.1 collective-permute-start.14
  58.5 3.0 %collective-permute-start.15 = (f32[192,128]{1,0:T(8,128)S(1)}, f32[192,128]{1,0:T(8,128)S(1)}, u32[]{:S(2)}, u32[]{:S(2)}) collective-permute-start(f32[192,128]{1,0:T(8,128)S(1)} %get-tuple-element.38), channel_id=1, source_target_pairs={{0,4},{1,5},{2,6},{3,7},{4,0},{5,1},{6,2},{7,3},{8,12},{9,13},{10,... | collective-permute-start | bytes 294920 | tf_op jit(solution)/shard_map/ppermute | solution.py:572
  61.5 1.3 %collective-permute-start.16 = (f32[192,128]{1,0:T(8,128)S(1)}, f32[192,128]{1,0:T(8,128)S(1)}, u32[]{:S(2)}, u32[]{:S(2)}) collective-permute-start(f32[192,128]{1,0:T(8,128)S(1)} %get-tuple-element.37), channel_id=1, source_target_pairs={{0,6},{1,7},{2,4},{3,5},{4,2},{5,3},{6,0},{7,1},{8,14},{9,15},{10,... | collective-permute-start | bytes 294920 | tf_op jit(solution)/shard_map/ppermute | solution.py:572
  62.8 0.0 collective-permute-done.8.more_ref
  62.8 5.9 %finish.1 = f32[48,16,128]{2,1,0:T(8,128)} custom-call(s32[1]{0:T(128)} %bitcast.member_ref, f32[192,256]{1,0:T(8,128)S(1)} %gram.1.gram_ref, f32[192,256]{1,0:T(8,128)S(1)} %collective-permute-done.8.more_ref, f32[48,1024]{1,0:T(8,128)S(1)} %get-tuple-element.32.refs_0_, f32[48,1024]{1,0:T(8,128)S(1)} %get-tuple-element.33.refs_1_, ...), custom_call_target="tpu_custom_call" | custom-call | flops 113246208 | bytes 1572864 | tf_op jit(solution)/shard_map/finish/pallas_call | solution.py:545
  68.7 0.0 collective-permute-done.14
  68.7 0.7 collective-permute-done.15
  69.4 0.0 collective-permute-done.16
  69.4 0.7 add_bitcast_fusion
  (5 shorter events, 0.1 us)
Async XLA Ops:
  2.0 4.5 %collective-permute-start = (f32[4,104,128]{2,1,0:T(8,128)S(1)}, f32[4,104,128]{2,1,0:T(8,128)S(1)}, u32[]{:S(2)}, u32[]{:S(2)}) collective-permute-start(f32[4,104,128]{2,1,0:T(8,128)S(1)} %get-tuple-element.25), channel_id=1, source_target_pairs={{0,1},{1,0},{2,3},{3,2},{4,5},{5,4},{6,7},{7,6},{8,9},{9,8},{10,11... | collective-permute-start | bytes 638984 | tf_op jit(solution)/shard_map/ppermute | solution.py:580
  2.5 3.9 %collective-permute-start.1 = (f32[4,104,128]{2,1,0:T(8,128)S(1)}, f32[4,104,128]{2,1,0:T(8,128)S(1)}, u32[]{:S(2)}, u32[]{:S(2)}) collective-permute-start(f32[4,104,128]{2,1,0:T(8,128)S(1)} %get-tuple-element.26), channel_id=1, source_target_pairs={{1,2},{3,4},{5,6},{2,1},{4,3},{6,5},{9,10},{11,12},{13,14},{10,9},... | collective-permute-start | bytes 638984 | tf_op jit(solution)/shard_map/ppermute | solution.py:579
  10.0 6.2 %collective-permute-start.10 = (f32[48,1024]{1,0:T(8,128)S(1)}, f32[48,1024]{1,0:T(8,128)S(1)}, u32[]{:S(2)}, u32[]{:S(2)}) collective-permute-start(f32[48,1024]{1,0:T(8,128)S(1)} %get-tuple-element.33.refs_1_), channel_id=1, source_target_pairs={{0,16},{8,24},{16,0},{24,8},{1,17},{9,25},{17,1},{25,9},{2,18},{10... | collective-permute-start | bytes 589832 | tf_op jit(solution)/shard_map/ppermute | solution.py:572
  12.5 5.7 %collective-permute-start.9 = (f32[48,1024]{1,0:T(8,128)S(1)}, f32[48,1024]{1,0:T(8,128)S(1)}, u32[]{:S(2)}, u32[]{:S(2)}) collective-permute-start(f32[48,1024]{1,0:T(8,128)S(1)} %get-tuple-element.32.refs_0_), channel_id=1, source_target_pairs={{0,8},{8,0},{16,24},{24,16},{1,9},{9,1},{17,25},{25,17},{2,10},{10... | collective-permute-start | bytes 589832 | tf_op jit(solution)/shard_map/ppermute | solution.py:572
  16.2 11.8 %collective-permute-start.12 = (f32[96,1024]{1,0:T(8,128)S(1)}, f32[96,1024]{1,0:T(8,128)S(1)}, u32[]{:S(2)}, u32[]{:S(2)}) collective-permute-start(f32[96,1024]{1,0:T(8,128)S(1)} %pad_maximum_fusion.1), channel_id=1, source_target_pairs={{0,8},{8,0},{16,24},{24,16},{1,9},{9,1},{17,25},{25,17},{2,10},{10... | collective-permute-start | bytes 1179656 | tf_op jit(solution)/shard_map/ppermute | solution.py:572
  18.3 9.8 %collective-permute-start.11 = (f32[96,1024]{1,0:T(8,128)S(1)}, f32[96,1024]{1,0:T(8,128)S(1)}, u32[]{:S(2)}, u32[]{:S(2)}) collective-permute-start(f32[96,1024]{1,0:T(8,128)S(1)} %pad_maximum_fusion), channel_id=1, source_target_pairs={{0,16},{8,24},{16,0},{24,8},{1,17},{9,25},{17,1},{25,9},{2,18},{10... | collective-permute-start | bytes 1179656 | tf_op jit(solution)/shard_map/ppermute | solution.py:572
  22.8 10.7 %collective-permute-start.2 = (f32[48,512]{1,0:T(8,128)S(1)}, f32[48,512]{1,0:T(8,128)S(1)}, u32[]{:S(2)}, u32[]{:S(2)}) collective-permute-start(f32[48,512]{1,0:T(8,128)S(1)} %get-tuple-element.29), channel_id=1, source_target_pairs={{0,1},{1,0},{2,3},{3,2},{4,5},{5,4},{6,7},{7,6},{8,9},{9,8},{10,11... | collective-permute-start | bytes 294920 | tf_op jit(solution)/shard_map/ppermute | solution.py:572
  31.3 27.0 %collective-permute-start.13 = (f32[192,512]{1,0:T(8,128)S(1)}, f32[192,512]{1,0:T(8,128)S(1)}, u32[]{:S(2)}, u32[]{:S(2)}) collective-permute-start(f32[192,512]{1,0:T(8,128)S(1)} %get-tuple-element.35), channel_id=1, source_target_pairs={{0,1},{1,0},{2,3},{3,2},{4,5},{5,4},{6,7},{7,6},{8,9},{9,8},{10,11... | collective-permute-start | bytes 1179656 | tf_op jit(solution)/shard_map/ppermute | solution.py:572
  33.5 8.5 %collective-permute-start.3 = (f32[48,512]{1,0:T(8,128)S(1)}, f32[48,512]{1,0:T(8,128)S(1)}, u32[]{:S(2)}, u32[]{:S(2)}) collective-permute-start(f32[48,512]{1,0:T(8,128)S(1)} %add.47), channel_id=1, source_target_pairs={{0,2},{1,3},{2,0},{3,1},{4,6},{5,7},{6,4},{7,5},{8,10},{9,11},{10,... | collective-permute-start | bytes 294920 | tf_op jit(solution)/shard_map/ppermute | solution.py:572
  42.0 7.7 %collective-permute-start.4 = (f32[48,512]{1,0:T(8,128)S(1)}, f32[48,512]{1,0:T(8,128)S(1)}, u32[]{:S(2)}, u32[]{:S(2)}) collective-permute-start(f32[48,512]{1,0:T(8,128)S(1)} %add.48), channel_id=1, source_target_pairs={{0,4},{1,5},{2,6},{3,7},{4,0},{5,1},{6,2},{7,3},{8,12},{9,13},{10,... | collective-permute-start | bytes 294920 | tf_op jit(solution)/shard_map/ppermute | solution.py:572
  49.7 4.9 %collective-permute-start.5 = (f32[48,512]{1,0:T(8,128)S(1)}, f32[48,512]{1,0:T(8,128)S(1)}, u32[]{:S(2)}, u32[]{:S(2)}) collective-permute-start(f32[48,512]{1,0:T(8,128)S(1)} %add.49.refs_0_), channel_id=1, source_target_pairs={{0,8},{8,0},{16,24},{24,16},{1,9},{9,1},{17,25},{25,17},{2,10},{10... | collective-permute-start | bytes 294920 | tf_op jit(solution)/shard_map/ppermute | solution.py:572
  50.9 4.6 %collective-permute-start.6 = (f32[48,512]{1,0:T(8,128)S(1)}, f32[48,512]{1,0:T(8,128)S(1)}, u32[]{:S(2)}, u32[]{:S(2)}) collective-permute-start(f32[48,512]{1,0:T(8,128)S(1)} %add.49.refs_0_), channel_id=1, source_target_pairs={{0,16},{8,24},{16,0},{24,8},{1,17},{9,25},{17,1},{25,9},{2,18},{10... | collective-permute-start | bytes 294920 | tf_op jit(solution)/shard_map/ppermute | solution.py:572
  51.8 5.5 %collective-permute-start.7 = (f32[48,512]{1,0:T(8,128)S(1)}, f32[48,512]{1,0:T(8,128)S(1)}, u32[]{:S(2)}, u32[]{:S(2)}) collective-permute-start(f32[48,512]{1,0:T(8,128)S(1)} %add.49.refs_0_), channel_id=1, source_target_pairs={{0,24},{8,16},{16,8},{24,0},{1,25},{9,17},{17,9},{25,1},{2,26},{10... | collective-permute-start | bytes 294920 | tf_op jit(solution)/shard_map/ppermute | solution.py:572
  58.2 4.6 %collective-permute-start.8 = (f32[192,256]{1,0:T(8,128)S(1)}, f32[192,256]{1,0:T(8,128)S(1)}, u32[]{:S(2)}, u32[]{:S(2)}) collective-permute-start(f32[192,256]{1,0:T(8,128)S(1)} %gram.1.gram_ref), channel_id=1, source_target_pairs={{0,1},{1,0},{2,3},{3,2},{4,5},{5,4},{6,7},{7,6},{8,9},{9,8},{10,11... | collective-permute-start | bytes 589832 | tf_op jit(solution)/shard_map/ppermute | solution.py:572
  58.4 10.3 %collective-permute-start.14 = (f32[192,128]{1,0:T(8,128)S(1)}, f32[192,128]{1,0:T(8,128)S(1)}, u32[]{:S(2)}, u32[]{:S(2)}) collective-permute-start(f32[192,128]{1,0:T(8,128)S(1)} %get-tuple-element.36), channel_id=1, source_target_pairs={{0,2},{1,3},{2,0},{3,1},{4,6},{5,7},{6,4},{7,5},{8,10},{9,11},{10,... | collective-permute-start | bytes 294920 | tf_op jit(solution)/shard_map/ppermute | solution.py:572
  58.5 10.9 %collective-permute-start.15 = (f32[192,128]{1,0:T(8,128)S(1)}, f32[192,128]{1,0:T(8,128)S(1)}, u32[]{:S(2)}, u32[]{:S(2)}) collective-permute-start(f32[192,128]{1,0:T(8,128)S(1)} %get-tuple-element.38), channel_id=1, source_target_pairs={{0,4},{1,5},{2,6},{3,7},{4,0},{5,1},{6,2},{7,3},{8,12},{9,13},{10,... | collective-permute-start | bytes 294920 | tf_op jit(solution)/shard_map/ppermute | solution.py:572
  61.5 7.9 %collective-permute-start.16 = (f32[192,128]{1,0:T(8,128)S(1)}, f32[192,128]{1,0:T(8,128)S(1)}, u32[]{:S(2)}, u32[]{:S(2)}) collective-permute-start(f32[192,128]{1,0:T(8,128)S(1)} %get-tuple-element.37), channel_id=1, source_target_pairs={{0,6},{1,7},{2,4},{3,5},{4,2},{5,3},{6,0},{7,1},{8,14},{9,15},{10,... | collective-permute-start | bytes 294920 | tf_op jit(solution)/shard_map/ppermute | solution.py:572

commit v7 on v6

--- a/solution.py
+++ b/solution.py
@@ -243,10 +243,10 @@
             perm = rim_ref[i - rows]
         else:
             perm = perm_ref[i - STEPS]
-        return perm * (1.0 + 0.5 * jnp.tanh(head))
+        return perm * (0.5 + 0.25 * jnp.tanh(head))
 
     def row_flux(mobility, head, mobility_next, head_next, i):
-        flux = 0.5 * (mobility_next + mobility) * (head_next - head)
+        flux = (mobility_next + mobility) * (head_next - head)
         if i == STEPS - 1:
             flux = jnp.where(no_before, 0.0, flux)
         if i == STEPS + rows - 1:
@@ -264,7 +264,7 @@
             head_next = head_of(step, i + 1)
             mobility_next = mobility_of(i + 1, head_next)
             flux_after = row_flux(mobility, head, mobility_next, head_next, i)
-            along = 0.5 * (pltpu.roll(mobility, cells - 1, 1) + mobility) * (pltpu.roll(head, cells - 1, 1) - head)
+            along = (pltpu.roll(mobility, cells - 1, 1) + mobility) * (pltpu.roll(head, cells - 1, 1) - head)
             along = jnp.where(last_lane, 0.0, along)
             inflow = (flux_after - flux_before) + (along - pltpu.roll(along, 1, 1))
             p_ref[i] = head + time_step * (inflow + wells_of(i))

time: 70.3 us -> 70.3 us (level)
  no operation moved by 1% of the time
where the time goes in v7:
time: 70.3 us; the launch traced here: 70.1 us
  starting transfers between devices  29 us (41%)
  Pallas kernels  20.9 us (30%)
  waiting for transfers between devices  18.5 us (26%)
  other arithmetic  0.87 us (1%)
  between operations  0.76 us (1%)
    ppermute x15, starting transfers between devices, swap(): return lax.ppermute(value, axis, [(i, i ^ offset) for i in range(size)])  27.8 us
    ppermute x15, waiting for transfers between devices, swap(): return lax.ppermute(value, axis, [(i, i ^ offset) for i in range(size)])  18.5 us
    pallas_call x1, Pallas kernels, finish(): pl.pallas_call(functools.partial(finish_kernel, plan, padded, members), o...  5.88 us
    pallas_call x1, Pallas kernels, forecast(): pl.pallas_call(functools.partial(forecast_kernel, slabs), out_shape=(jax....  3.54 us
    pallas_call x1, Pallas kernels, kernel_of_observed(): pl.pallas_call(functools.partial(observed_kernel, total_rows), out_shape=...  3.25 us
    pallas_call x1, Pallas kernels, subsidence_partial(): pl.pallas_call(functools.partial(subsidence_kernel, plan, padded), out_sh...  3.18 us
    pallas_call x1, Pallas kernels, kernel_of_pixels(): pl.pallas_call(functools.partial(pixel_kernel, total_rows, chips, own_row...  2.89 us
  transfers between devices with their start and end apart: 17, of which 9 were waited for; matrix products, arithmetic and copies ran while one was open for 0% of the time, Pallas kernels for 23%

profile of v7, /device:TPU:0, one launch (start us, length us, event | category | flops | bytes accessed | tf_op | source)
XLA Modules:
  0.0 70.1 jit_solution(3048459772006615803)
XLA Ops:
  0.6 1.3 %pack_rims.1 = (f32[4,104,128]{2,1,0:T(8,128)S(1)}, f32[4,104,128]{2,1,0:T(8,128)S(1)}, f32[16,128]{1,0:T(8,128)S(1)}, s32[16,128]{1,0:T(8,128)S(1)}, s32[2,4096...) custom-call(s32[1]{0:T(128)} %bitcast.1.slab_ref, f32[48,16,128]{2,1,0:T(8,128)} %head_ref.3, ...), custom_call_target="tpu_custom_call" | custom-call | tf_op jit(solution)/shard_map/pack_rims/pallas_call | solution.py:76
  2.0 0.6 collective-permute-start
  2.5 0.7 collective-permute-start.1
  3.2 3.3 %kernel_of_observed.1 = (f32[2048,1024]{1,0:T(8,128)S(1)}, f32[16,48,128]{2,1,0:T(8,128)S(1)}, f32[16,48,128]{2,1,0:T(8,128)S(1)}) custom-call(s32[1]{0:T(128)} %bitcast.1.slab_ref, s32[2,4096]{1,0:T(2,128)S(1)} %get-tuple-element.19.coords_ref, s32[8,128]{1,0:T(8,128)S(1)} %get-tuple-element.20.index_ref, s32[16,128]{1,0:T(8,128)S(1)} %get-tuple-element.21.layer_ref, ...), custom_call_target="tpu_custom_call" | custom-call | flops 33554432 | bytes 8388608 | tf_op jit(solution)/shard_map/kernel_of_observed/pallas_call | solution.py:151
  6.4 0.0 collective-permute-done.near_ref
  6.5 0.0 collective-permute-done.1.far_ref
  6.5 3.5 %forecast.1 = (f32[48,1024]{1,0:T(8,128)S(1)}, f32[48,1024]{1,0:T(8,128)S(1)}, f32[48,512]{1,0:T(8,128)S(1)}, f32[48,512]{1,0:T(8,128)S(1)}) custom-call(s32[1]{0:T(128)} %bitcast.1.slab_ref, f32[16,48,128]{2,1,0:T(8,128)S(1)} %get-tuple-element.22.start_ref, f32[16,48,128]{2,1,0:T(8,128)S(1)} %get-tuple-element.23.perm_ref, ...), custom_call_target="tpu_custom_call" | custom-call | flops 603979776 | bytes 8388608 | tf_op jit(solution)/shard_map/forecast/pallas_call | solution.py:316
  10.0 2.5 %collective-permute-start.10 = (f32[48,1024]{1,0:T(8,128)S(1)}, f32[48,1024]{1,0:T(8,128)S(1)}, u32[]{:S(2)}, u32[]{:S(2)}) collective-permute-start(f32[48,1024]{1,0:T(8,128)S(1)} %get-tuple-element.33.refs_1_), channel_id=1, source_target_pairs={{0,16},{8,24},{16,0},{24,8},{1,17},{9,25},{17,1},{25,9},{2,18},{10... | collective-permute-start | bytes 589832 | tf_op jit(solution)/shard_map/ppermute | solution.py:572
  12.6 1.5 %collective-permute-start.9 = (f32[48,1024]{1,0:T(8,128)S(1)}, f32[48,1024]{1,0:T(8,128)S(1)}, u32[]{:S(2)}, u32[]{:S(2)}) collective-permute-start(f32[48,1024]{1,0:T(8,128)S(1)} %get-tuple-element.32.refs_0_), channel_id=1, source_target_pairs={{0,8},{8,0},{16,24},{24,16},{1,9},{9,1},{17,25},{25,17},{2,10},{10... | collective-permute-start | bytes 589832 | tf_op jit(solution)/shard_map/ppermute | solution.py:572
  14.0 2.2 %collective-permute-done.10.refs_3_ = f32[48,1024]{1,0:T(8,128)S(1)} collective-permute-done((f32[48,1024]{1,0:T(8,128)S(1)}, f32[48,1024]{1,0:T(8,128)S(1)}, u32[]{:S(2)}, u32[]{:S(2)}) %collective-permute-start.10) | collective-permute-done | bytes 196640 | tf_op jit(solution)/shard_map/ppermute | solution.py:572
  16.2 2.1 %collective-permute-start.12 = (f32[96,1024]{1,0:T(8,128)S(1)}, f32[96,1024]{1,0:T(8,128)S(1)}, u32[]{:S(2)}, u32[]{:S(2)}) collective-permute-start(f32[96,1024]{1,0:T(8,128)S(1)} %pad_maximum_fusion.1), channel_id=1, source_target_pairs={{0,8},{8,0},{16,24},{24,16},{1,9},{9,1},{17,25},{25,17},{2,10},{10... | collective-permute-start | bytes 1179656 | tf_op jit(solution)/shard_map/ppermute | solution.py:572
  18.3 0.0 collective-permute-done.9.refs_2_
  18.3 1.6 %collective-permute-start.11 = (f32[96,1024]{1,0:T(8,128)S(1)}, f32[96,1024]{1,0:T(8,128)S(1)}, u32[]{:S(2)}, u32[]{:S(2)}) collective-permute-start(f32[96,1024]{1,0:T(8,128)S(1)} %pad_maximum_fusion), channel_id=1, source_target_pairs={{0,16},{8,24},{16,0},{24,8},{1,17},{9,25},{17,1},{25,9},{2,18},{10... | collective-permute-start | bytes 1179656 | tf_op jit(solution)/shard_map/ppermute | solution.py:572
  19.9 2.9 %kernel_of_pixels.1.refs_6_ = f32[2048,1024]{1,0:T(8,128)S(1)} custom-call(s32[1]{0:T(128)} %bitcast.1.slab_ref, s32[1]{0:T(128)} %bitcast.member_ref, s32[2,4096]{1,0:T(2,128)S(1)} %get-tuple-element.19.coords_ref, s32[16,128]{1,0:T(8,128)S(1)} %get-tuple-element.21.layer_ref), custom_call_target="tpu_custom_call" | custom-call | flops 33554432 | bytes 8388608 | tf_op jit(solution)/shard_map/kernel_of_pixels/pallas_call | solution.py:196
  22.8 2.0 %collective-permute-start.2 = (f32[48,512]{1,0:T(8,128)S(1)}, f32[48,512]{1,0:T(8,128)S(1)}, u32[]{:S(2)}, u32[]{:S(2)}) collective-permute-start(f32[48,512]{1,0:T(8,128)S(1)} %get-tuple-element.29), channel_id=1, source_target_pairs={{0,1},{1,0},{2,3},{3,2},{4,5},{5,4},{6,7},{7,6},{8,9},{9,8},{10,11... | collective-permute-start | bytes 294920 | tf_op jit(solution)/shard_map/ppermute | solution.py:572
  24.8 3.2 %collective-permute-done.12.refs_5_ = f32[96,1024]{1,0:T(8,128)S(1)} collective-permute-done((f32[96,1024]{1,0:T(8,128)S(1)}, f32[96,1024]{1,0:T(8,128)S(1)}, u32[]{:S(2)}, u32[]{:S(2)}) %collective-permute-start.12) | collective-permute-done | bytes 393248 | tf_op jit(solution)/shard_map/ppermute | solution.py:572
  28.0 0.1 collective-permute-done.11.refs_4_
  28.1 3.2 %subsidence.1 = (f32[192,512]{1,0:T(8,128)S(1)}, f32[192,512]{1,0:T(8,128)S(1)}) custom-call(s32[1]{0:T(128)} %bitcast.member_ref, f32[48,1024]{1,0:T(8,128)S(1)} %get-tuple-element.32.refs_0_, f32[48,1024]{1,0:T(8,128)S(1)} %get-tuple-element.33.refs_1_, f32[48,1024]{1,0:T(8,128)S(1)} %collective-permute-done.9.refs_2_, ...), custom_call_target="tpu_custom_call" | custom-call | flops 2415919104 | bytes 9961472 | tf_op jit(solution)/shard_map/subsidence/pallas_call | solution.py:356
  31.3 2.1 %collective-permute-start.13 = (f32[192,512]{1,0:T(8,128)S(1)}, f32[192,512]{1,0:T(8,128)S(1)}, u32[]{:S(2)}, u32[]{:S(2)}) collective-permute-start(f32[192,512]{1,0:T(8,128)S(1)} %get-tuple-element.35), channel_id=1, source_target_pairs={{0,1},{1,0},{2,3},{3,2},{4,5},{5,4},{6,7},{7,6},{8,9},{9,8},{10,11... | collective-permute-start | bytes 1179656 | tf_op jit(solution)/shard_map/ppermute | solution.py:572
  33.5 0.0 collective-permute-done.2
  33.5 5.0 %collective-permute-start.3 = (f32[48,512]{1,0:T(8,128)S(1)}, f32[48,512]{1,0:T(8,128)S(1)}, u32[]{:S(2)}, u32[]{:S(2)}) collective-permute-start(f32[48,512]{1,0:T(8,128)S(1)} %add.47), channel_id=1, source_target_pairs={{0,2},{1,3},{2,0},{3,1},{4,6},{5,7},{6,4},{7,5},{8,10},{9,11},{10,... | collective-permute-start | bytes 294920 | tf_op jit(solution)/shard_map/ppermute | solution.py:572
  38.5 3.4 %collective-permute-done.3 = f32[48,512]{1,0:T(8,128)S(1)} collective-permute-done((f32[48,512]{1,0:T(8,128)S(1)}, f32[48,512]{1,0:T(8,128)S(1)}, u32[]{:S(2)}, u32[]{:S(2)}) %collective-permute-start.3) | collective-permute-done | bytes 98336 | tf_op jit(solution)/shard_map/ppermute | solution.py:572
  42.0 2.8 %collective-permute-start.4 = (f32[48,512]{1,0:T(8,128)S(1)}, f32[48,512]{1,0:T(8,128)S(1)}, u32[]{:S(2)}, u32[]{:S(2)}) collective-permute-start(f32[48,512]{1,0:T(8,128)S(1)} %add.48), channel_id=1, source_target_pairs={{0,4},{1,5},{2,6},{3,7},{4,0},{5,1},{6,2},{7,3},{8,12},{9,13},{10,... | collective-permute-start | bytes 294920 | tf_op jit(solution)/shard_map/ppermute | solution.py:572
  44.8 4.9 %collective-permute-done.4 = f32[48,512]{1,0:T(8,128)S(1)} collective-permute-done((f32[48,512]{1,0:T(8,128)S(1)}, f32[48,512]{1,0:T(8,128)S(1)}, u32[]{:S(2)}, u32[]{:S(2)}) %collective-permute-start.4) | collective-permute-done | bytes 98336 | tf_op jit(solution)/shard_map/ppermute | solution.py:572
  49.7 1.2 %collective-permute-start.5 = (f32[48,512]{1,0:T(8,128)S(1)}, f32[48,512]{1,0:T(8,128)S(1)}, u32[]{:S(2)}, u32[]{:S(2)}) collective-permute-start(f32[48,512]{1,0:T(8,128)S(1)} %add.49.refs_0_), channel_id=1, source_target_pairs={{0,8},{8,0},{16,24},{24,16},{1,9},{9,1},{17,25},{25,17},{2,10},{10... | collective-permute-start | bytes 294920 | tf_op jit(solution)/shard_map/ppermute | solution.py:572
  50.9 0.9 %collective-permute-start.6 = (f32[48,512]{1,0:T(8,128)S(1)}, f32[48,512]{1,0:T(8,128)S(1)}, u32[]{:S(2)}, u32[]{:S(2)}) collective-permute-start(f32[48,512]{1,0:T(8,128)S(1)} %add.49.refs_0_), channel_id=1, source_target_pairs={{0,16},{8,24},{16,0},{24,8},{1,17},{9,25},{17,1},{25,9},{2,18},{10... | collective-permute-start | bytes 294920 | tf_op jit(solution)/shard_map/ppermute | solution.py:572
  51.8 1.4 %collective-permute-start.7 = (f32[48,512]{1,0:T(8,128)S(1)}, f32[48,512]{1,0:T(8,128)S(1)}, u32[]{:S(2)}, u32[]{:S(2)}) collective-permute-start(f32[48,512]{1,0:T(8,128)S(1)} %add.49.refs_0_), channel_id=1, source_target_pairs={{0,24},{8,16},{16,8},{24,0},{1,25},{9,17},{17,9},{25,1},{2,26},{10... | collective-permute-start | bytes 294920 | tf_op jit(solution)/shard_map/ppermute | solution.py:572
  53.2 1.3 %collective-permute-done.5.refs_1_ = f32[48,512]{1,0:T(8,128)S(1)} collective-permute-done((f32[48,512]{1,0:T(8,128)S(1)}, f32[48,512]{1,0:T(8,128)S(1)}, u32[]{:S(2)}, u32[]{:S(2)}) %collective-permute-start.5) | collective-permute-done | bytes 98336 | tf_op jit(solution)/shard_map/ppermute | solution.py:572
  54.6 0.9 %collective-permute-done.6.refs_2_ = f32[48,512]{1,0:T(8,128)S(1)} collective-permute-done((f32[48,512]{1,0:T(8,128)S(1)}, f32[48,512]{1,0:T(8,128)S(1)}, u32[]{:S(2)}, u32[]{:S(2)}) %collective-permute-start.6) | collective-permute-done | bytes 98336 | tf_op jit(solution)/shard_map/ppermute | solution.py:572
  55.5 1.8 %collective-permute-done.7.refs_3_ = f32[48,512]{1,0:T(8,128)S(1)} collective-permute-done((f32[48,512]{1,0:T(8,128)S(1)}, f32[48,512]{1,0:T(8,128)S(1)}, u32[]{:S(2)}, u32[]{:S(2)}) %collective-permute-start.7) | collective-permute-done | bytes 98336 | tf_op jit(solution)/shard_map/ppermute | solution.py:572
  57.3 0.9 %gram.1.gram_ref = f32[192,256]{1,0:T(8,128)S(1)} custom-call(s32[1]{0:T(128)} %bitcast.1.slab_ref, s32[1]{0:T(128)} %bitcast.member_ref, f32[48,512]{1,0:T(8,128)S(1)} %add.49.refs_0_, f32[48,512]{1,0:T(8,128)S(1)} %collective-permute-done.5.refs_1_, f32[48,512]{1,0:T(8,128)S(1)} %collective-permute-done.6.refs_2_, ...), custom_call_target="tpu_custom_call" | custom-call | flops 226492416 | bytes 393216 | tf_op jit(solution)/shard_map/gram/pallas_call | solution.py:403
  58.2 0.1 collective-permute-start.8
  58.3 0.0 collective-permute-done.13
  58.3 0.1 dynamic-slice_add_fusion.2
  58.4 0.1 collective-permute-start.14
  58.5 3.0 %collective-permute-start.15 = (f32[192,128]{1,0:T(8,128)S(1)}, f32[192,128]{1,0:T(8,128)S(1)}, u32[]{:S(2)}, u32[]{:S(2)}) collective-permute-start(f32[192,128]{1,0:T(8,128)S(1)} %get-tuple-element.38), channel_id=1, source_target_pairs={{0,4},{1,5},{2,6},{3,7},{4,0},{5,1},{6,2},{7,3},{8,12},{9,13},{10,... | collective-permute-start | bytes 294920 | tf_op jit(solution)/shard_map/ppermute | solution.py:572
  61.5 1.3 %collective-permute-start.16 = (f32[192,128]{1,0:T(8,128)S(1)}, f32[192,128]{1,0:T(8,128)S(1)}, u32[]{:S(2)}, u32[]{:S(2)}) collective-permute-start(f32[192,128]{1,0:T(8,128)S(1)} %get-tuple-element.37), channel_id=1, source_target_pairs={{0,6},{1,7},{2,4},{3,5},{4,2},{5,3},{6,0},{7,1},{8,14},{9,15},{10,... | collective-permute-start | bytes 294920 | tf_op jit(solution)/shard_map/ppermute | solution.py:572
  62.8 0.0 collective-permute-done.8.more_ref
  62.8 5.9 %finish.1 = f32[48,16,128]{2,1,0:T(8,128)} custom-call(s32[1]{0:T(128)} %bitcast.member_ref, f32[192,256]{1,0:T(8,128)S(1)} %gram.1.gram_ref, f32[192,256]{1,0:T(8,128)S(1)} %collective-permute-done.8.more_ref, f32[48,1024]{1,0:T(8,128)S(1)} %get-tuple-element.32.refs_0_, f32[48,1024]{1,0:T(8,128)S(1)} %get-tuple-element.33.refs_1_, ...), custom_call_target="tpu_custom_call" | custom-call | flops 113246208 | bytes 1572864 | tf_op jit(solution)/shard_map/finish/pallas_call | solution.py:545
  68.7 0.0 collective-permute-done.14
  68.7 0.7 collective-permute-done.15
  69.4 0.0 collective-permute-done.16
  69.4 0.7 add_bitcast_fusion
  (5 shorter events, 0.1 us)
Async XLA Ops:
  2.0 4.5 %collective-permute-start = (f32[4,104,128]{2,1,0:T(8,128)S(1)}, f32[4,104,128]{2,1,0:T(8,128)S(1)}, u32[]{:S(2)}, u32[]{:S(2)}) collective-permute-start(f32[4,104,128]{2,1,0:T(8,128)S(1)} %get-tuple-element.25), channel_id=1, source_target_pairs={{0,1},{1,0},{2,3},{3,2},{4,5},{5,4},{6,7},{7,6},{8,9},{9,8},{10,11... | collective-permute-start | bytes 638984 | tf_op jit(solution)/shard_map/ppermute | solution.py:580
  2.5 3.9 %collective-permute-start.1 = (f32[4,104,128]{2,1,0:T(8,128)S(1)}, f32[4,104,128]{2,1,0:T(8,128)S(1)}, u32[]{:S(2)}, u32[]{:S(2)}) collective-permute-start(f32[4,104,128]{2,1,0:T(8,128)S(1)} %get-tuple-element.26), channel_id=1, source_target_pairs={{1,2},{3,4},{5,6},{2,1},{4,3},{6,5},{9,10},{11,12},{13,14},{10,9},... | collective-permute-start | bytes 638984 | tf_op jit(solution)/shard_map/ppermute | solution.py:579
  10.0 6.2 %collective-permute-start.10 = (f32[48,1024]{1,0:T(8,128)S(1)}, f32[48,1024]{1,0:T(8,128)S(1)}, u32[]{:S(2)}, u32[]{:S(2)}) collective-permute-start(f32[48,1024]{1,0:T(8,128)S(1)} %get-tuple-element.33.refs_1_), channel_id=1, source_target_pairs={{0,16},{8,24},{16,0},{24,8},{1,17},{9,25},{17,1},{25,9},{2,18},{10... | collective-permute-start | bytes 589832 | tf_op jit(solution)/shard_map/ppermute | solution.py:572
  12.6 5.7 %collective-permute-start.9 = (f32[48,1024]{1,0:T(8,128)S(1)}, f32[48,1024]{1,0:T(8,128)S(1)}, u32[]{:S(2)}, u32[]{:S(2)}) collective-permute-start(f32[48,1024]{1,0:T(8,128)S(1)} %get-tuple-element.32.refs_0_), channel_id=1, source_target_pairs={{0,8},{8,0},{16,24},{24,16},{1,9},{9,1},{17,25},{25,17},{2,10},{10... | collective-permute-start | bytes 589832 | tf_op jit(solution)/shard_map/ppermute | solution.py:572
  16.2 11.8 %collective-permute-start.12 = (f32[96,1024]{1,0:T(8,128)S(1)}, f32[96,1024]{1,0:T(8,128)S(1)}, u32[]{:S(2)}, u32[]{:S(2)}) collective-permute-start(f32[96,1024]{1,0:T(8,128)S(1)} %pad_maximum_fusion.1), channel_id=1, source_target_pairs={{0,8},{8,0},{16,24},{24,16},{1,9},{9,1},{17,25},{25,17},{2,10},{10... | collective-permute-start | bytes 1179656 | tf_op jit(solution)/shard_map/ppermute | solution.py:572
  18.3 9.8 %collective-permute-start.11 = (f32[96,1024]{1,0:T(8,128)S(1)}, f32[96,1024]{1,0:T(8,128)S(1)}, u32[]{:S(2)}, u32[]{:S(2)}) collective-permute-start(f32[96,1024]{1,0:T(8,128)S(1)} %pad_maximum_fusion), channel_id=1, source_target_pairs={{0,16},{8,24},{16,0},{24,8},{1,17},{9,25},{17,1},{25,9},{2,18},{10... | collective-permute-start | bytes 1179656 | tf_op jit(solution)/shard_map/ppermute | solution.py:572
  22.8 10.7 %collective-permute-start.2 = (f32[48,512]{1,0:T(8,128)S(1)}, f32[48,512]{1,0:T(8,128)S(1)}, u32[]{:S(2)}, u32[]{:S(2)}) collective-permute-start(f32[48,512]{1,0:T(8,128)S(1)} %get-tuple-element.29), channel_id=1, source_target_pairs={{0,1},{1,0},{2,3},{3,2},{4,5},{5,4},{6,7},{7,6},{8,9},{9,8},{10,11... | collective-permute-start | bytes 294920 | tf_op jit(solution)/shard_map/ppermute | solution.py:572
  31.3 27.0 %collective-permute-start.13 = (f32[192,512]{1,0:T(8,128)S(1)}, f32[192,512]{1,0:T(8,128)S(1)}, u32[]{:S(2)}, u32[]{:S(2)}) collective-permute-start(f32[192,512]{1,0:T(8,128)S(1)} %get-tuple-element.35), channel_id=1, source_target_pairs={{0,1},{1,0},{2,3},{3,2},{4,5},{5,4},{6,7},{7,6},{8,9},{9,8},{10,11... | collective-permute-start | bytes 1179656 | tf_op jit(solution)/shard_map/ppermute | solution.py:572
  33.5 8.5 %collective-permute-start.3 = (f32[48,512]{1,0:T(8,128)S(1)}, f32[48,512]{1,0:T(8,128)S(1)}, u32[]{:S(2)}, u32[]{:S(2)}) collective-permute-start(f32[48,512]{1,0:T(8,128)S(1)} %add.47), channel_id=1, source_target_pairs={{0,2},{1,3},{2,0},{3,1},{4,6},{5,7},{6,4},{7,5},{8,10},{9,11},{10,... | collective-permute-start | bytes 294920 | tf_op jit(solution)/shard_map/ppermute | solution.py:572
  42.0 7.7 %collective-permute-start.4 = (f32[48,512]{1,0:T(8,128)S(1)}, f32[48,512]{1,0:T(8,128)S(1)}, u32[]{:S(2)}, u32[]{:S(2)}) collective-permute-start(f32[48,512]{1,0:T(8,128)S(1)} %add.48), channel_id=1, source_target_pairs={{0,4},{1,5},{2,6},{3,7},{4,0},{5,1},{6,2},{7,3},{8,12},{9,13},{10,... | collective-permute-start | bytes 294920 | tf_op jit(solution)/shard_map/ppermute | solution.py:572
  49.7 4.9 %collective-permute-start.5 = (f32[48,512]{1,0:T(8,128)S(1)}, f32[48,512]{1,0:T(8,128)S(1)}, u32[]{:S(2)}, u32[]{:S(2)}) collective-permute-start(f32[48,512]{1,0:T(8,128)S(1)} %add.49.refs_0_), channel_id=1, source_target_pairs={{0,8},{8,0},{16,24},{24,16},{1,9},{9,1},{17,25},{25,17},{2,10},{10... | collective-permute-start | bytes 294920 | tf_op jit(solution)/shard_map/ppermute | solution.py:572
  50.9 4.6 %collective-permute-start.6 = (f32[48,512]{1,0:T(8,128)S(1)}, f32[48,512]{1,0:T(8,128)S(1)}, u32[]{:S(2)}, u32[]{:S(2)}) collective-permute-start(f32[48,512]{1,0:T(8,128)S(1)} %add.49.refs_0_), channel_id=1, source_target_pairs={{0,16},{8,24},{16,0},{24,8},{1,17},{9,25},{17,1},{25,9},{2,18},{10... | collective-permute-start | bytes 294920 | tf_op jit(solution)/shard_map/ppermute | solution.py:572
  51.8 5.5 %collective-permute-start.7 = (f32[48,512]{1,0:T(8,128)S(1)}, f32[48,512]{1,0:T(8,128)S(1)}, u32[]{:S(2)}, u32[]{:S(2)}) collective-permute-start(f32[48,512]{1,0:T(8,128)S(1)} %add.49.refs_0_), channel_id=1, source_target_pairs={{0,24},{8,16},{16,8},{24,0},{1,25},{9,17},{17,9},{25,1},{2,26},{10... | collective-permute-start | bytes 294920 | tf_op jit(solution)/shard_map/ppermute | solution.py:572
  58.2 4.6 %collective-permute-start.8 = (f32[192,256]{1,0:T(8,128)S(1)}, f32[192,256]{1,0:T(8,128)S(1)}, u32[]{:S(2)}, u32[]{:S(2)}) collective-permute-start(f32[192,256]{1,0:T(8,128)S(1)} %gram.1.gram_ref), channel_id=1, source_target_pairs={{0,1},{1,0},{2,3},{3,2},{4,5},{5,4},{6,7},{7,6},{8,9},{9,8},{10,11... | collective-permute-start | bytes 589832 | tf_op jit(solution)/shard_map/ppermute | solution.py:572
  58.4 10.3 %collective-permute-start.14 = (f32[192,128]{1,0:T(8,128)S(1)}, f32[192,128]{1,0:T(8,128)S(1)}, u32[]{:S(2)}, u32[]{:S(2)}) collective-permute-start(f32[192,128]{1,0:T(8,128)S(1)} %get-tuple-element.36), channel_id=1, source_target_pairs={{0,2},{1,3},{2,0},{3,1},{4,6},{5,7},{6,4},{7,5},{8,10},{9,11},{10,... | collective-permute-start | bytes 294920 | tf_op jit(solution)/shard_map/ppermute | solution.py:572
  58.5 10.9 %collective-permute-start.15 = (f32[192,128]{1,0:T(8,128)S(1)}, f32[192,128]{1,0:T(8,128)S(1)}, u32[]{:S(2)}, u32[]{:S(2)}) collective-permute-start(f32[192,128]{1,0:T(8,128)S(1)} %get-tuple-element.38), channel_id=1, source_target_pairs={{0,4},{1,5},{2,6},{3,7},{4,0},{5,1},{6,2},{7,3},{8,12},{9,13},{10,... | collective-permute-start | bytes 294920 | tf_op jit(solution)/shard_map/ppermute | solution.py:572
  61.5 7.9 %collective-permute-start.16 = (f32[192,128]{1,0:T(8,128)S(1)}, f32[192,128]{1,0:T(8,128)S(1)}, u32[]{:S(2)}, u32[]{:S(2)}) collective-permute-start(f32[192,128]{1,0:T(8,128)S(1)} %get-tuple-element.37), channel_id=1, source_target_pairs={{0,6},{1,7},{2,4},{3,5},{4,2},{5,3},{6,0},{7,1},{8,14},{9,15},{10,... | collective-permute-start | bytes 294920 | tf_op jit(solution)/shard_map/ppermute | solution.py:572
